TPU v7x, 128 devices: a whole 4x4x4 slice. The times are simulated.
128 devices in a mesh: map: 16 (over y, x), rep: 8 (over z, core).
Axes of the slice: x: 4, y: 4, z: 4, core: 2. Of those that a mesh axis runs over, the one named last changes fastest.
Arguments:
- amplitudes: float32 [2, 4096, 5120], P(None, ('map', 'rep')), may hold values from -6 to 6
- integrals: float32 [2, 5120, 5120], P(None, None, ('map', 'rep')), may hold values from -0.078125 to 0.078125
- row_gap: float32 [2, 4096], P(None, ('map', 'rep')), may hold values from 0.5 to 4
- col_gap: float32 [2, 5120], replicated, may hold values from 0.5 to 4
Outputs:
- update: float32 [2, 4096, 5120], P(None, ('map', 'rep'))
All inputs are finite; a program needn't handle non-finite values.
Results may differ from a plain program's by a relative error of at most 0.00007.
Values sent between devices are 32-bit elements; how exact they have to be, the bound alone decides.
No kernel may reach another device: no remote copies, remote signals or barrier semaphores. Data moves between devices by JAX's collectives and lax.ppermute only.
A program may use at most 128 MiB of HBM per device.

v0:
```python
import jax
import jax.numpy as jnp
from jax import lax
from jax.sharding import PartitionSpec as P


def per_device(amplitudes, integrals, row_gap, col_gap):
    amp_block = lax.all_to_all(amplitudes, "rep", split_axis=2, concat_axis=1, tiled=True)
    int_block = lax.all_to_all(integrals, "rep", split_axis=1, concat_axis=2, tiled=True)
    partial_value = jnp.einsum(
        "gsk,gkc->gsc",
        amp_block,
        lax.all_gather(int_block, "map", axis=2, tiled=True),
        precision=lax.Precision.HIGHEST,
        preferred_element_type=jnp.float32,
    )
    product = lax.psum_scatter(partial_value, "rep", scatter_dimension=1, tiled=True)
    return product / (row_gap[:, :, None] + col_gap[:, None, :])


def solution(mesh):
    placed = (
        P(None, ("map", "rep"), None),
        P(None, None, ("map", "rep")),
        P(None, ("map", "rep")),
        P(),
    )
    return jax.shard_map(
        per_device,
        mesh=mesh,
        in_specs=placed,
        out_specs=P(None, ("map", "rep"), None),
        check_vma=False,
    )
```

profile of v0, /device:TPU:1, one launch (start us, length us, event | category | flops | bytes accessed | tf_op | source)
XLA Modules:
  0.0 337.0 jit_solution(603539111832813769)
XLA Ops:
  6.5 0.0 all-gather.2.cloned.1.call-start
  6.5 6.9 %copy.9 = f32[2,5120,40]{2,0,1:T(2,128)} copy(f32[2,5120,40]{1,2,0:T(8,128)} %param.5) | data formatting | bytes 3276800 | tf_op args[1]
  13.5 10.8 %reshape.4 = f32[8,1,51200]{2,1,0:T(1,128)S(1)} reshape(f32[5120,2,40]{2,1,0:T(2,128)} %bitcast.17) | data formatting | bytes 3276800
  24.3 28.4 %all_to_all.36 = f32[8,1,51200]{2,1,0:T(1,128)S(1)} all-to-all(f32[8,1,51200]{2,1,0:T(1,128)S(1)} %reshape.4), channel_id=1, replica_groups=mesh['map'=16,'rep'=8] {'rep'}, dimensions={0} | all-to-all | bytes 3276800 | tf_op jit(solution)/shard_map/all_to_all | solution.py:9
  52.7 0.5 broadcast.2
  53.2 4.5 %reduce.1 = f32[8,51200]{1,0:T(8,128)S(1)} reduce(f32[8,1,51200]{2,1,0:T(1,128)S(1)} %all_to_all.36, f32[]{:T(128)} %broadcast.2), dimensions={1}, to_apply=%all_to_all.30.reduce_sub_computation | reduce | bytes 3276804 | tf_op jit(solution)/shard_map/all_to_all | solution.py:9
  57.7 11.4 %reshape.5 = f32[5120,2,40]{2,1,0:T(2,128)} reshape(f32[8,51200]{1,0:T(8,128)S(1)} %reduce.1) | data formatting | bytes 3276800
  69.2 6.9 %copy.10 = f32[2,8,640,40]{2,3,1,0:T(8,128)} copy(f32[2,8,640,40]{3,0,2,1:T(2,128)} %bitcast.16) | data formatting | bytes 3276800 | tf_op jit(solution)/shard_map/all_to_all | solution.py:9
  76.0 0.0 all-gather.2.cloned.1.call-update
  76.1 0.2 reduce-scatter.2.cloned.1.call-start
  76.3 1.1 copy-done
  77.4 4.7 %copy.7 = f32[2,32,5120]{1,0,2:T(2,128)} copy(f32[2,32,5120]{2,1,0:T(8,128)S(1)} %copy-done) | data formatting | bytes 2621440 | tf_op args[0]
  82.0 6.8 %reshape.2 = f32[8,1,40960]{2,1,0:T(1,128)S(1)} reshape(f32[5120,2,32]{2,1,0:T(2,128)} %bitcast.15) | data formatting | bytes 2621440
  88.9 21.1 %all_to_all.37 = f32[8,1,40960]{2,1,0:T(1,128)S(1)} all-to-all(f32[8,1,40960]{2,1,0:T(1,128)S(1)} %reshape.2), channel_id=1, replica_groups=mesh['map'=16,'rep'=8] {'rep'}, dimensions={0} | all-to-all | bytes 2621440 | tf_op jit(solution)/shard_map/all_to_all | solution.py:8
  110.0 3.8 %reduce = f32[8,40960]{1,0:T(8,128)S(1)} reduce(f32[8,1,40960]{2,1,0:T(1,128)S(1)} %all_to_all.37, f32[]{:T(128)} %broadcast.2), dimensions={1}, to_apply=%all_to_all.26.reduce_sub_computation | reduce | bytes 2621444 | tf_op jit(solution)/shard_map/all_to_all | solution.py:8
  113.8 6.8 %reshape.3 = f32[5120,2,32]{2,1,0:T(2,128)} reshape(f32[8,40960]{1,0:T(8,128)S(1)} %reduce) | data formatting | bytes 2621440
  120.6 5.5 %copy.8 = f32[2,32,8,640]{3,1,2,0:T(8,128)S(1)} copy(f32[2,32,8,640]{1,0,3,2:T(2,128)} %bitcast.14) | data formatting | bytes 2621440 | tf_op jit(solution)/shard_map/all_to_all | solution.py:8
  126.1 109.1 %all-gather.2.cloned.1.call-done = f32[2,640,5120]{1,2,0:T(8,128)} async-done(((f32[2,640,320]{1,2,0:T(8,128)}), f32[2,640,5120]{1,2,0:T(8,128)}) %all-gather.2.cloned.1.call-update) | async-done | bytes 26214416 | tf_op jit(solution)/shard_map/all_gather | solution.py:13
  235.2 30.5 %fusion = f32[2,256,5120]{2,1,0:T(8,128)} fusion(f32[2,256,640]{2,1,0:T(8,128)S(1)} %bitcast.19, f32[2,640,5120]{1,2,0:T(8,128)} %all-gather.2.cloned.1.call-done), kind=kOutput, calls=%fused_computation.1 | convolution fusion | flops 20132659200 | bytes 38010880 | tf_op jit(solution)/shard_map/gsk,gkc->gsc/dot_general | solution.py:10
  265.7 0.0 reduce-scatter.2.cloned.1.call-update
  265.7 61.8 %reduce-scatter.2.cloned.1.call-done = f32[2,32,5120]{2,1,0:T(8,128)} async-done(((f32[2,256,5120]{2,1,0:T(8,128)}), f32[2,32,5120]{2,1,0:T(8,128)}) %reduce-scatter.2.cloned.1.call-update) | async-done | bytes 1310736 | tf_op jit(solution)/shard_map/reduce_scatter | solution.py:17
  327.5 0.0 copy-done.1
  327.5 0.0 copy-done.2
  327.5 2.6 add_divide_fusion
  (3 shorter events, 0.0 us)
Async XLA Ops:
  6.5 228.7 %all-gather.2.cloned.1.call-start = ((), (), s32[]{:S(2)}) async-start(), calls=%async_computation.3 | async-start | bytes 27852800 | tf_op jit(solution)/shard_map/all_gather | solution.py:13
  76.0 1.3 copy-start
  76.1 251.4 %reduce-scatter.2.cloned.1.call-start = ((), (), s32[]{:S(2)}) async-start(), calls=%async_computation.4 | async-start | bytes 11796480 | tf_op jit(solution)/shard_map/reduce_scatter | solution.py:17
  265.7 61.8 %copy-start.1 = (f32[2,5120]{1,0:T(2,128)S(1)}, f32[2,5120]{1,0:T(2,128)}, u32[]{:S(2)}) copy-start(f32[2,5120]{1,0:T(2,128)} %param.7) | copy-start | bytes 122884
  265.7 61.8 %copy-start.2 = (f32[2,32]{1,0:T(2,128)S(1)}, f32[2,32]{1,0:T(2,128)}, u32[]{:S(2)}) copy-start(f32[2,32]{1,0:T(2,128)} %param.6) | copy-start | bytes 772
Sparse Core Ops, SparseCore 0:
  76.2 158.9 all-gather.1
  265.8 61.6 reduce-scatter.1
where the time goes:
time: 338 us; the launch traced here: 337 us
  waiting for transfers between devices  171 us (51%)
  local copies, waits for them, and re-layouts  61.5 us (18%)
  blocking collectives  49.5 us (15%)
  matrix products  30.5 us (9%)
  between operations  13.4 us (4%)
  other arithmetic  10.9 us (3%)
    all_gather x1, waiting for transfers between devices, per_device(): lax.all_gather(int_block, 'map', axis=2, tiled=True)  109 us
    reduce_scatter x1, waiting for transfers between devices, per_device(): lax.psum_scatter(partial_value, 'rep', scatter_dimension=1, tiled=True)  61.8 us
    unnamed x12, local copies, waits for them, and re-layouts  48.6 us
    dot_general x1, matrix products, per_device(): jnp.einsum('gsk,gkc->gsc', amp_block, lax.all_gather(int_block, 'map', ax...  30.5 us
    all_to_all x1, blocking collectives, per_device(): lax.all_to_all(integrals, 'rep', split_axis=1, concat_axis=2, tiled=True)  28.4 us
    all_to_all x1, blocking collectives, per_device(): lax.all_to_all(amplitudes, 'rep', split_axis=2, concat_axis=1, tiled=True)  21.1 us
    all_to_all x1, local copies, waits for them, and re-layouts, per_device(): lax.all_to_all(integrals, 'rep', split_axis=1, concat_axis=2, tiled=True)  6.88 us
  transfers between devices with their start and end apart: 2, of which 2 were waited for; matrix products, arithmetic and copies ran while one was open for 8% of the time, Pallas kernels for 0%

commit v1 on v0

v1 whole, which is shorter than its diff:
```python
import jax
import jax.numpy as jnp
from jax import lax
from jax.sharding import PartitionSpec as P

AXES = ("y", "x", "z", "c")
SIDE = 4


def routes(target):
    pairs = []
    for y in range(SIDE):
        for x in range(SIDE):
            for z in range(SIDE):
                for c in range(2):
                    ty, tx, tz, tc = target(y, x, z, c)
                    source = ((y * SIDE + x) * SIDE + z) * 2 + c
                    pairs.append((source, ((ty % SIDE * SIDE + tx % SIDE) * SIDE + tz % SIDE) * 2 + tc % 2))
    return pairs


def along_y(step):
    return routes(lambda y, x, z, c: (y + step, x, z, c))


def along_k(step):
    return routes(lambda y, x, z, c: (y, x, z + step, c) if c == 0 else (y, x + step, z, c))


def along_m(step):
    return routes(lambda y, x, z, c: (y, x + step, z, c) if c == 0 else (y, x, z + step, c))


OTHER_CORE = routes(lambda y, x, z, c: (y, x, z, c + 1))


def send(value, route):
    return lax.ppermute(value, AXES, route)


def contracted_split(rows, k_index):
    depth = rows.shape[1] // SIDE
    blocks = [lax.dynamic_slice_in_dim(rows, (k_index + s) % SIDE * depth, depth, axis=1) for s in range(SIDE)]
    return [blocks[0]] + [send(blocks[s], along_k(s)) for s in range(1, SIDE)]


def ring_gather(block, along):
    half = block.shape[0] // 2
    before = send(block, along(1))
    after = send(block, along(-1))
    far = jnp.concatenate([send(before[:half], along(1)), send(after[half:], along(-1))], axis=0)
    return [block, before, far, after]


def ring_reduce(parts):
    half = parts[0].shape[0] // 2
    low = send(parts[2][:half], along_k(-1))
    high = send(parts[2][half:], along_k(1))
    down = send(jnp.concatenate([parts[1][:half] + low, parts[1][half:]], axis=0), along_k(-1))
    up = send(jnp.concatenate([parts[3][:half], parts[3][half:] + high], axis=0), along_k(1))
    return parts[0] + down + up


def per_device(amplitudes, integrals, row_gap, col_gap):
    y, x, z, c = (lax.axis_index(name) for name in AXES)
    k_index = jnp.where(c == 0, z, x)
    m_index = jnp.where(c == 0, x, z)
    columns = jnp.swapaxes(integrals, 1, 2)

    own_rows = lax.dynamic_index_in_dim(amplitudes, c, 0, keepdims=False)
    other_rows = send(lax.dynamic_index_in_dim(amplitudes, 1 - c, 0, keepdims=False), OTHER_CORE)
    own_columns = lax.dynamic_index_in_dim(columns, c, 0, keepdims=False)
    other_columns = send(lax.dynamic_index_in_dim(columns, 1 - c, 0, keepdims=False), OTHER_CORE)
    rows = jnp.concatenate([own_rows, other_rows], axis=0)
    first = jnp.where(c == 0, own_columns, other_columns)
    second = jnp.where(c == 0, other_columns, own_columns)
    cols = jnp.concatenate([first, second], axis=0)

    amp_blocks = ring_gather(jnp.concatenate(contracted_split(rows, k_index), axis=0), along_y)
    col_blocks = ring_gather(jnp.concatenate(contracted_split(cols, k_index), axis=0), along_m)

    wide = cols.shape[0]
    depth = amp_blocks[0].shape[1]
    relative = jnp.stack(col_blocks).reshape(SIDE, SIDE, wide, depth)
    spread = jnp.zeros((SIDE, SIDE, wide, depth), jnp.float32)
    order = jnp.arange(SIDE)
    by_m = relative[(m_index - order) % SIDE]
    by_mk = by_m[:, (k_index - order) % SIDE]
    xz = jnp.where(c == 0, by_mk, jnp.swapaxes(by_mk, 0, 1)).reshape(SIDE * SIDE * wide, depth)

    pieces = []
    for amp_block in amp_blocks:
        partial = lax.dot_general(
            amp_block, xz, (((1,), (1,)), ((), ())), precision=lax.Precision.HIGH, preferred_element_type=jnp.float32
        )
        pieces.append(ring_reduce(jnp.split(partial, SIDE, axis=0)))
    arrived = [pieces[0]] + [send(pieces[t], along_y(-t)) for t in range(1, SIDE)]
    full = jnp.stack(arrived, axis=0)[(order - y) % SIDE]
    full = jnp.swapaxes(full, 0, 1).reshape(pieces[0].shape[0], -1)
    half = full.shape[0] // 2
    theirs = send(full[half:], OTHER_CORE)
    mine = full[:half]
    product = jnp.stack([jnp.where(c == 0, mine, theirs), jnp.where(c == 0, theirs, mine)])
    return product / (row_gap[:, :, None] + col_gap[:, None, :])


def solution(mesh):
    fine = jax.sharding.Mesh(mesh.devices.reshape(SIDE, SIDE, SIDE, 2), AXES)
    placed = (P(None, AXES, None), P(None, None, AXES), P(None, AXES), P())
    return jax.shard_map(
        per_device, mesh=fine, in_specs=placed, out_specs=P(None, AXES, None), check_vma=False
    )
```

time: 338 us -> 186 us (0.55)
  waiting for transfers between devices: 171 us -> 78.6 us
  starting transfers between devices: 0.22 us -> 52.1 us
  blocking collectives: 49.5 us -> 0 us
  local copies, waits for them, and re-layouts: 61.5 us -> 23.2 us
  matrix products: 30.5 us -> 16.9 us
  between operations: 13.4 us -> 0.45 us
    all_gather x1 -> x0, waiting for transfers between devices: 109 us -> none  [per_device(): lax.all_gather(int_block, 'map', axis=2, tiled=True)]
    ppermute x0 -> x36, waiting for transfers between devices: none -> 78.6 us  [send(): return lax.ppermute(value, AXES, route)]
    reduce_scatter x1 -> x0, waiting for transfers between devices: 61.8 us -> none  [per_device(): lax.psum_scatter(partial_value, 'rep', scatter_dimension=1, tiled=True)]
    ppermute x0 -> x36, starting transfers between devices: none -> 52.1 us  [send(): return lax.ppermute(value, AXES, route)]
    all_to_all x2 -> x0, blocking collectives: 49.5 us -> none  [the longest x1 28.4 us: per_device(): lax.all_to_all(integrals, 'rep', split_axis=1, concat_axis=2, tiled=True)]
    unnamed x12 -> x29, local copies, waits for them, and re-layouts: 48.6 us -> 2.03 us
    gather x0 -> x3, local copies, waits for them, and re-layouts: none -> 13.8 us  [the longest x1 6.63 us: per_device(): by_mk = by_m[:, (k_index - order) % SIDE]]
    dot_general x1 -> x4, matrix products: 30.5 us -> 16.9 us  [per_device(): lax.dot_general(amp_block, xz, (((1,), (1,)), ((), ())), precision=lax.Pr...]
  transfers between devices with their start and end apart: 2 -> 36, of which waited for: 2 -> 19; matrix products, arithmetic and copies ran while one was open for 8% -> 26% of each run, Pallas kernels for 0% -> 0%
where the time goes in v1:
time: 186 us; the launch traced here: 185 us
  waiting for transfers between devices  78.6 us (42%)
  starting transfers between devices  52.1 us (28%)
  local copies, waits for them, and re-layouts  23.2 us (12%)
  matrix products  16.9 us (9%)
  other arithmetic  14.1 us (8%)
    ppermute x36, waiting for transfers between devices, send(): return lax.ppermute(value, AXES, route)  78.6 us
    ppermute x36, starting transfers between devices, send(): return lax.ppermute(value, AXES, route)  52.1 us
    dot_general x4, matrix products, per_device(): lax.dot_general(amp_block, xz, (((1,), (1,)), ((), ())), precision=lax.Pr...  16.9 us
    gather x1, local copies, waits for them, and re-layouts, per_device(): by_mk = by_m[:, (k_index - order) % SIDE]  6.63 us
    gather x1, local copies, waits for them, and re-layouts, per_device(): by_m = relative[(m_index - order) % SIDE]  6.54 us
    select_n x1, other arithmetic, per_device(): jnp.where(c == 0, by_mk, jnp.swapaxes(by_mk, 0, 1))  5.64 us
  transfers between devices with their start and end apart: 36, of which 19 were waited for; matrix products, arithmetic and copies ran while one was open for 26% of the time, Pallas kernels for 0%

profile of v1, /device:TPU:1, one launch (start us, length us, event | category | flops | bytes accessed | tf_op | source)
XLA Modules:
  0.0 185.4 jit_solution(30283585234395675)
XLA Ops:
  6.4 2.5 %collective-permute-start.6 = (f32[80,1280]{1,0:T(8,128)S(1)}, f32[80,1280]{1,0:T(8,128)S(1)}, u32[]{:S(2)}, u32[]{:S(2)}) collective-permute-start(f32[80,1280]{1,0:T(8,128)S(1)} %get-tuple-element.9), channel_id=1, source_target_pairs={{0,4},{1,17},{2,6},{3,19},{4,0},{5,21},{6,2},{7,23},{8,12},{9,25},... | collective-permute-start | bytes 1228808 | tf_op jit(solution)/shard_map/ppermute | solution.py:38
  13.4 5.5 %collective-permute-done.6 = f32[80,1280]{1,0:T(8,128)S(1)} collective-permute-done((f32[80,1280]{1,0:T(8,128)S(1)}, f32[80,1280]{1,0:T(8,128)S(1)}, u32[]{:S(2)}, u32[]{:S(2)}) %collective-permute-start.6) | collective-permute-done | bytes 409632 | tf_op jit(solution)/shard_map/ppermute | solution.py:38
  19.0 3.5 %collective-permute-start.10 = (f32[320,1280]{1,0:T(8,128)S(1)}, f32[320,1280]{1,0:T(8,128)S(1)}, u32[]{:S(2)}, u32[]{:S(2)}) collective-permute-start(f32[320,1280]{1,0:T(8,128)S(1)} %pad_maximum_fusion.1), channel_id=1, source_target_pairs={{0,24},{1,7},{2,26},{3,1},{4,28},{5,3},{6,30},{7,5},{8,0},{9,15},{... | collective-permute-start | bytes 4915208 | tf_op jit(solution)/shard_map/ppermute | solution.py:38
  27.5 4.0 %collective-permute-done.1 = f32[64,1280]{1,0:T(8,128)S(1)} collective-permute-done((f32[64,1280]{1,0:T(8,128)S(1)}, f32[64,1280]{1,0:T(8,128)S(1)}, u32[]{:S(2)}, u32[]{:S(2)}) %collective-permute-start.1) | collective-permute-done | bytes 327712 | tf_op jit(solution)/shard_map/ppermute | solution.py:38
  31.5 9.7 %collective-permute-done.2 = f32[64,1280]{1,0:T(8,128)S(1)} collective-permute-done((f32[64,1280]{1,0:T(8,128)S(1)}, f32[64,1280]{1,0:T(8,128)S(1)}, u32[]{:S(2)}, u32[]{:S(2)}) %collective-permute-start.2) | collective-permute-done | bytes 327712 | tf_op jit(solution)/shard_map/ppermute | solution.py:38
  48.6 3.5 %collective-permute-start.11 = (f32[160,1280]{1,0:T(8,128)}, f32[160,1280]{1,0:T(8,128)}, u32[]{:S(2)}, u32[]{:S(2)}) collective-permute-start(f32[160,1280]{1,0:T(8,128)} %slice.159), channel_id=1, source_target_pairs={{0,24},{1,7},{2,26},{3,1},{4,28},{5,3},{6,30},{7,5},{8,0},{9,15},{... | collective-permute-start | bytes 2457608 | tf_op jit(solution)/shard_map/ppermute | solution.py:38
  54.4 17.2 %collective-permute-done.16 = f32[256,1280]{1,0:T(8,128)} collective-permute-done((f32[256,1280]{1,0:T(8,128)}, f32[256,1280]{1,0:T(8,128)}, u32[]{:S(2)}, u32[]{:S(2)}) %collective-permute-start.16) | collective-permute-done | bytes 1310752 | tf_op jit(solution)/shard_map/ppermute | solution.py:38
  75.5 2.7 %collective-permute-start.24 = (f32[128,1280]{1,0:T(8,128)}, f32[128,1280]{1,0:T(8,128)}, u32[]{:S(2)}, u32[]{:S(2)}) collective-permute-start(f32[128,1280]{1,0:T(8,128)} %slice.173), channel_id=1, source_target_pairs={{0,96},{1,97},{2,98},{3,99},{4,100},{5,101},{6,102},{7,103},{8,104... | collective-permute-start | bytes 1966088 | tf_op jit(solution)/shard_map/ppermute | solution.py:38
  79.7 3.0 %pad_maximum_fusion = f32[4,4,80,1280]{3,2,1,0:T(8,128)} fusion(f32[1,4,80,1280]{3,2,1,0:T(8,128)S(1)} %bitcast.55, f32[1,4,80,1280]{3,2,1,0:T(8,128)S(1)} %bitcast.53, f32[1,4,80,1280]{3,2,1,0:T(8,128)S(1)} %bitcast.56, f32[1,4,80,1280]{3,2,1,0:T(8,128)S(1)} %bitcast.52), kind=kLoop, calls=%fused_computation.3 | loop fusion | flops 4915200 | bytes 13107200 | tf_op jit(solution)/shard_map/stack | solution.py:84
  82.7 6.5 %gather_fusion = f32[4,4,80,1280]{3,2,1,0:T(8,128)} fusion(f32[4,4,80,1280]{3,2,1,0:T(8,128)} %pad_maximum_fusion, s32[1024]{0:T(1024)S(1)} %pad_clamp_fusion.2), kind=kCustom, calls=%fused_computation | custom fusion | bytes 13107216 | tf_op jit(solution)/shard_map/gather | solution.py:87
  89.3 6.6 %gather_fusion.1 = f32[4,4,80,1280]{3,2,1,0:T(8,128)} fusion(f32[4,4,80,1280]{3,2,1,0:T(8,128)} %gather_fusion, s32[1024]{0:T(1024)S(1)} %pad_clamp_fusion.1), kind=kCustom, calls=%fused_computation.1 | custom fusion | bytes 13107216 | tf_op jit(solution)/shard_map/gather | solution.py:88
  95.9 5.6 %bitcast_select_fusion = f32[4,4,80,1280]{3,2,1,0:T(8,128)S(1)} fusion(f32[4,4,80,1280]{3,2,1,0:T(8,128)} %gather_fusion.1, pred[]{:T(512)S(6)} %eq.22), kind=kLoop, calls=%fused_computation.4 | loop fusion | flops 1638400 | bytes 13107201 | tf_op jit(solution)/shard_map/jit(_where)/select_n | solution.py:89
  101.6 3.2 %fusion.24 = f32[256,1280]{1,0:T(8,128)S(1)} fusion(f32[1280,1280]{1,0:T(8,128)S(1)} %bitcast.48, f32[64,1280]{1,0:T(8,128)S(1)} %copy-done.10, f32[64,1280]{1,0:T(8,128)S(1)} %copy-done.8, f32[64,1280]{1,0:T(8,128)S(1)} %copy-done.6, f32[64,1280]{1,0:T(8,128)S(1)} %copy-done.3), kind=kOutput, calls=%fused_computation.94 | convolution fusion | flops 2517565440 | bytes 9175040 | tf_op jit(solution)/shard_map/dot_general | solution.py:93
  104.9 4.6 %fusion.25 = f32[256,1280]{1,0:T(8,128)S(1)} fusion(f32[256,1280]{1,0:T(8,128)} %collective-permute-done.16, f32[1280,1280]{1,0:T(8,128)S(1)} %bitcast.49), kind=kOutput, calls=%fused_computation.95 | convolution fusion | flops 2516582400 | bytes 9175040 | tf_op jit(solution)/shard_map/dot_general | solution.py:93
  109.5 3.9 %collective-permute-start.17 = (f32[32,1280]{1,0:T(8,128)S(1)}, f32[32,1280]{1,0:T(8,128)S(1)}, u32[]{:S(2)}, u32[]{:S(2)}) collective-permute-start(f32[32,1280]{1,0:T(8,128)S(1)} %slice.167), channel_id=1, source_target_pairs={{0,6},{1,25},{2,0},{3,27},{4,2},{5,29},{6,4},{7,31},{8,14},{9,1},{... | collective-permute-start | bytes 491528 | tf_op jit(solution)/shard_map/ppermute | solution.py:38
  113.4 4.5 %fusion = f32[256,1280]{1,0:T(8,128)S(1)} fusion(f32[1280,1280]{1,0:T(8,128)S(1)} %bitcast.50, f32[128,1280]{1,0:T(8,128)} %collective-permute-done.24, f32[128,1280]{1,0:T(8,128)} %collective-permute-done.22), kind=kOutput, calls=%fused_computation.24 | convolution fusion | flops 2516910080 | bytes 9175040 | tf_op jit(solution)/shard_map/dot_general | solution.py:93
  118.1 4.6 %fusion.26 = f32[256,1280]{1,0:T(8,128)S(1)} fusion(f32[256,1280]{1,0:T(8,128)} %collective-permute-done.23, f32[1280,1280]{1,0:T(8,128)S(1)} %bitcast.51), kind=kOutput, calls=%fused_computation.96 | convolution fusion | flops 2516582400 | bytes 9175040 | tf_op jit(solution)/shard_map/dot_general | solution.py:93
  126.9 2.5 %collective-permute-start.26 = (f32[64,1280]{1,0:T(8,128)S(1)}, f32[64,1280]{1,0:T(8,128)S(1)}, u32[]{:S(2)}, u32[]{:S(2)}) collective-permute-start(f32[64,1280]{1,0:T(8,128)S(1)} %pad_maximum_fusion.9), channel_id=1, source_target_pairs={{0,6},{1,25},{2,0},{3,27},{4,2},{5,29},{6,4},{7,31},{8,14},{9,1},{... | collective-permute-start | bytes 983048 | tf_op jit(solution)/shard_map/ppermute | solution.py:38
  135.0 5.6 %collective-permute-done.32 = f32[32,1280]{1,0:T(8,128)S(1)} collective-permute-done((f32[32,1280]{1,0:T(8,128)S(1)}, f32[32,1280]{1,0:T(8,128)S(1)}, u32[]{:S(2)}, u32[]{:S(2)}) %collective-permute-start.32) | collective-permute-done | bytes 163872 | tf_op jit(solution)/shard_map/ppermute | solution.py:38
  140.8 7.0 %collective-permute-done.20 = f32[64,1280]{1,0:T(8,128)S(1)} collective-permute-done((f32[64,1280]{1,0:T(8,128)S(1)}, f32[64,1280]{1,0:T(8,128)S(1)}, u32[]{:S(2)}, u32[]{:S(2)}) %collective-permute-start.20) | collective-permute-done | bytes 327712 | tf_op jit(solution)/shard_map/ppermute | solution.py:38
  147.9 7.0 %collective-permute-done.28 = f32[64,1280]{1,0:T(8,128)S(1)} collective-permute-done((f32[64,1280]{1,0:T(8,128)S(1)}, f32[64,1280]{1,0:T(8,128)S(1)}, u32[]{:S(2)}, u32[]{:S(2)}) %collective-permute-start.28) | collective-permute-done | bytes 327712 | tf_op jit(solution)/shard_map/ppermute | solution.py:38
  155.8 2.9 %collective-permute-done.33 = f32[64,1280]{1,0:T(8,128)S(1)} collective-permute-done((f32[64,1280]{1,0:T(8,128)S(1)}, f32[64,1280]{1,0:T(8,128)S(1)}, u32[]{:S(2)}, u32[]{:S(2)}) %collective-permute-start.33) | collective-permute-done | bytes 327712 | tf_op jit(solution)/shard_map/ppermute | solution.py:38
  162.9 3.8 %collective-permute-done.34 = f32[64,1280]{1,0:T(8,128)S(1)} collective-permute-done((f32[64,1280]{1,0:T(8,128)S(1)}, f32[64,1280]{1,0:T(8,128)S(1)}, u32[]{:S(2)}, u32[]{:S(2)}) %collective-permute-start.34) | collective-permute-done | bytes 327712 | tf_op jit(solution)/shard_map/ppermute | solution.py:38
  167.5 14.0 %collective-permute-start.35 = (f32[32,5120]{1,0:T(8,128)S(1)}, f32[32,5120]{1,0:T(8,128)S(1)}, u32[]{:S(2)}, u32[]{:S(2)}) collective-permute-start(f32[32,5120]{1,0:T(8,128)S(1)} %bitcast.58), channel_id=1, source_target_pairs={{0,1},{1,0},{2,3},{3,2},{4,5},{5,4},{6,7},{7,6},{8,9},{9,8},{10,11... | collective-permute-start | bytes 1966088 | tf_op jit(solution)/shard_map/ppermute | solution.py:38
  (133 shorter events, 51.1 us)
Async XLA Ops:
  6.4 12.5 %collective-permute-start.6 = (f32[80,1280]{1,0:T(8,128)S(1)}, f32[80,1280]{1,0:T(8,128)S(1)}, u32[]{:S(2)}, u32[]{:S(2)}) collective-permute-start(f32[80,1280]{1,0:T(8,128)S(1)} %get-tuple-element.9), channel_id=1, source_target_pairs={{0,4},{1,17},{2,6},{3,19},{4,0},{5,21},{6,2},{7,23},{8,12},{9,25},... | collective-permute-start | bytes 1228808 | tf_op jit(solution)/shard_map/ppermute | solution.py:38
  8.9 10.0 %collective-permute-start.7 = (f32[80,1280]{1,0:T(8,128)S(1)}, f32[80,1280]{1,0:T(8,128)S(1)}, u32[]{:S(2)}, u32[]{:S(2)}) collective-permute-start(f32[80,1280]{1,0:T(8,128)S(1)} %get-tuple-element.10), channel_id=1, source_target_pairs={{0,6},{1,25},{2,0},{3,27},{4,2},{5,29},{6,4},{7,31},{8,14},{9,1},{... | collective-permute-start | bytes 1228808 | tf_op jit(solution)/shard_map/ppermute | solution.py:38
  10.1 12.4 %collective-permute-start = (f32[32,5120]{1,0:T(8,128)S(1)}, f32[32,5120]{1,0:T(8,128)S(1)}, u32[]{:S(2)}, u32[]{:S(2)}) collective-permute-start(f32[32,5120]{1,0:T(8,128)S(1)} %get-tuple-element.35), channel_id=1, source_target_pairs={{0,1},{1,0},{2,3},{3,2},{4,5},{5,4},{6,7},{7,6},{8,9},{9,8},{10,11... | collective-permute-start | bytes 1966088 | tf_op jit(solution)/shard_map/ppermute | solution.py:38
  19.0 28.6 %collective-permute-start.10 = (f32[320,1280]{1,0:T(8,128)S(1)}, f32[320,1280]{1,0:T(8,128)S(1)}, u32[]{:S(2)}, u32[]{:S(2)}) collective-permute-start(f32[320,1280]{1,0:T(8,128)S(1)} %pad_maximum_fusion.1), channel_id=1, source_target_pairs={{0,24},{1,7},{2,26},{3,1},{4,28},{5,3},{6,30},{7,5},{8,0},{9,15},{... | collective-permute-start | bytes 4915208 | tf_op jit(solution)/shard_map/ppermute | solution.py:38
  22.6 29.6 %collective-permute-start.8 = (f32[320,1280]{1,0:T(8,128)S(1)}, f32[320,1280]{1,0:T(8,128)S(1)}, u32[]{:S(2)}, u32[]{:S(2)}) collective-permute-start(f32[320,1280]{1,0:T(8,128)S(1)} %pad_maximum_fusion.1), channel_id=1, source_target_pairs={{0,8},{1,3},{2,10},{3,5},{4,12},{5,7},{6,14},{7,1},{8,16},{9,11},{... | collective-permute-start | bytes 4915208 | tf_op jit(solution)/shard_map/ppermute | solution.py:38
  22.7 8.9 %collective-permute-start.1 = (f32[64,1280]{1,0:T(8,128)S(1)}, f32[64,1280]{1,0:T(8,128)S(1)}, u32[]{:S(2)}, u32[]{:S(2)}) collective-permute-start(f32[64,1280]{1,0:T(8,128)S(1)} %get-tuple-element.32), channel_id=1, source_target_pairs={{0,2},{1,9},{2,4},{3,11},{4,6},{5,13},{6,0},{7,15},{8,10},{9,17},{... | collective-permute-start | bytes 983048 | tf_op jit(solution)/shard_map/ppermute | solution.py:38
  24.1 17.1 %collective-permute-start.2 = (f32[64,1280]{1,0:T(8,128)S(1)}, f32[64,1280]{1,0:T(8,128)S(1)}, u32[]{:S(2)}, u32[]{:S(2)}) collective-permute-start(f32[64,1280]{1,0:T(8,128)S(1)} %get-tuple-element.33), channel_id=1, source_target_pairs={{0,4},{1,17},{2,6},{3,19},{4,0},{5,21},{6,2},{7,23},{8,12},{9,25},... | collective-permute-start | bytes 983048 | tf_op jit(solution)/shard_map/ppermute | solution.py:38
  26.2 15.1 %collective-permute-start.3 = (f32[64,1280]{1,0:T(8,128)S(1)}, f32[64,1280]{1,0:T(8,128)S(1)}, u32[]{:S(2)}, u32[]{:S(2)}) collective-permute-start(f32[64,1280]{1,0:T(8,128)S(1)} %get-tuple-element.34), channel_id=1, source_target_pairs={{0,6},{1,25},{2,0},{3,27},{4,2},{5,29},{6,4},{7,31},{8,14},{9,1},{... | collective-permute-start | bytes 983048 | tf_op jit(solution)/shard_map/ppermute | solution.py:38
  42.5 29.1 %collective-permute-start.16 = (f32[256,1280]{1,0:T(8,128)}, f32[256,1280]{1,0:T(8,128)}, u32[]{:S(2)}, u32[]{:S(2)}) collective-permute-start(f32[256,1280]{1,0:T(8,128)} %pad_maximum_fusion.3), channel_id=1, source_target_pairs={{0,32},{1,33},{2,34},{3,35},{4,36},{5,37},{6,38},{7,39},{8,40},{9,... | collective-permute-start | bytes 3932168 | tf_op jit(solution)/shard_map/ppermute | solution.py:38
  43.9 29.7 %collective-permute-start.23 = (f32[256,1280]{1,0:T(8,128)}, f32[256,1280]{1,0:T(8,128)}, u32[]{:S(2)}, u32[]{:S(2)}) collective-permute-start(f32[256,1280]{1,0:T(8,128)} %pad_maximum_fusion.3), channel_id=1, source_target_pairs={{0,96},{1,97},{2,98},{3,99},{4,100},{5,101},{6,102},{7,103},{8,104... | collective-permute-start | bytes 3932168 | tf_op jit(solution)/shard_map/ppermute | solution.py:38
  48.6 29.6 %collective-permute-start.11 = (f32[160,1280]{1,0:T(8,128)}, f32[160,1280]{1,0:T(8,128)}, u32[]{:S(2)}, u32[]{:S(2)}) collective-permute-start(f32[160,1280]{1,0:T(8,128)} %slice.159), channel_id=1, source_target_pairs={{0,24},{1,7},{2,26},{3,1},{4,28},{5,3},{6,30},{7,5},{8,0},{9,15},{... | collective-permute-start | bytes 2457608 | tf_op jit(solution)/shard_map/ppermute | solution.py:38
  54.3 23.9 %collective-permute-start.9 = (f32[160,1280]{1,0:T(8,128)}, f32[160,1280]{1,0:T(8,128)}, u32[]{:S(2)}, u32[]{:S(2)}) collective-permute-start(f32[160,1280]{1,0:T(8,128)} %slice.158), channel_id=1, source_target_pairs={{0,8},{1,3},{2,10},{3,5},{4,12},{5,7},{6,14},{7,1},{8,16},{9,11},{... | collective-permute-start | bytes 2457608 | tf_op jit(solution)/shard_map/ppermute | solution.py:38
  73.5 39.9 %collective-permute-start.22 = (f32[128,1280]{1,0:T(8,128)}, f32[128,1280]{1,0:T(8,128)}, u32[]{:S(2)}, u32[]{:S(2)}) collective-permute-start(f32[128,1280]{1,0:T(8,128)} %slice.172), channel_id=1, source_target_pairs={{0,32},{1,33},{2,34},{3,35},{4,36},{5,37},{6,38},{7,39},{8,40},{9,... | collective-permute-start | bytes 1966088 | tf_op jit(solution)/shard_map/ppermute | solution.py:38
  75.5 37.9 %collective-permute-start.24 = (f32[128,1280]{1,0:T(8,128)}, f32[128,1280]{1,0:T(8,128)}, u32[]{:S(2)}, u32[]{:S(2)}) collective-permute-start(f32[128,1280]{1,0:T(8,128)} %slice.173), channel_id=1, source_target_pairs={{0,96},{1,97},{2,98},{3,99},{4,100},{5,101},{6,102},{7,103},{8,104... | collective-permute-start | bytes 1966088 | tf_op jit(solution)/shard_map/ppermute | solution.py:38
  104.9 17.9 %collective-permute-start.12 = (f32[32,1280]{1,0:T(8,128)S(1)}, f32[32,1280]{1,0:T(8,128)S(1)}, u32[]{:S(2)}, u32[]{:S(2)}) collective-permute-start(f32[32,1280]{1,0:T(8,128)S(1)} %slice.161), channel_id=1, source_target_pairs={{0,6},{1,25},{2,0},{3,27},{4,2},{5,29},{6,4},{7,31},{8,14},{9,1},{... | collective-permute-start | bytes 491528 | tf_op jit(solution)/shard_map/ppermute | solution.py:38
  109.5 14.9 %collective-permute-start.17 = (f32[32,1280]{1,0:T(8,128)S(1)}, f32[32,1280]{1,0:T(8,128)S(1)}, u32[]{:S(2)}, u32[]{:S(2)}) collective-permute-start(f32[32,1280]{1,0:T(8,128)S(1)} %slice.167), channel_id=1, source_target_pairs={{0,6},{1,25},{2,0},{3,27},{4,2},{5,29},{6,4},{7,31},{8,14},{9,1},{... | collective-permute-start | bytes 491528 | tf_op jit(solution)/shard_map/ppermute | solution.py:38
  118.0 8.6 %collective-permute-start.25 = (f32[32,1280]{1,0:T(8,128)S(1)}, f32[32,1280]{1,0:T(8,128)S(1)}, u32[]{:S(2)}, u32[]{:S(2)}) collective-permute-start(f32[32,1280]{1,0:T(8,128)S(1)} %slice.175), channel_id=1, source_target_pairs={{0,6},{1,25},{2,0},{3,27},{4,2},{5,29},{6,4},{7,31},{8,14},{9,1},{... | collective-permute-start | bytes 491528 | tf_op jit(solution)/shard_map/ppermute | solution.py:38
  122.8 36.0 %collective-permute-start.13 = (f32[64,1280]{1,0:T(8,128)S(1)}, f32[64,1280]{1,0:T(8,128)S(1)}, u32[]{:S(2)}, u32[]{:S(2)}) collective-permute-start(f32[64,1280]{1,0:T(8,128)S(1)} %pad_maximum_fusion.5), channel_id=1, source_target_pairs={{0,6},{1,25},{2,0},{3,27},{4,2},{5,29},{6,4},{7,31},{8,14},{9,1},{... | collective-permute-start | bytes 983048 | tf_op jit(solution)/shard_map/ppermute | solution.py:38
  124.5 16.2 %collective-permute-start.18 = (f32[64,1280]{1,0:T(8,128)S(1)}, f32[64,1280]{1,0:T(8,128)S(1)}, u32[]{:S(2)}, u32[]{:S(2)}) collective-permute-start(f32[64,1280]{1,0:T(8,128)S(1)} %pad_maximum_fusion.7), channel_id=1, source_target_pairs={{0,6},{1,25},{2,0},{3,27},{4,2},{5,29},{6,4},{7,31},{8,14},{9,1},{... | collective-permute-start | bytes 983048 | tf_op jit(solution)/shard_map/ppermute | solution.py:38
  126.9 20.9 %collective-permute-start.26 = (f32[64,1280]{1,0:T(8,128)S(1)}, f32[64,1280]{1,0:T(8,128)S(1)}, u32[]{:S(2)}, u32[]{:S(2)}) collective-permute-start(f32[64,1280]{1,0:T(8,128)S(1)} %pad_maximum_fusion.9), channel_id=1, source_target_pairs={{0,6},{1,25},{2,0},{3,27},{4,2},{5,29},{6,4},{7,31},{8,14},{9,1},{... | collective-permute-start | bytes 983048 | tf_op jit(solution)/shard_map/ppermute | solution.py:38
  131.9 23.4 %collective-permute-start.31 = (f32[64,1280]{1,0:T(8,128)S(1)}, f32[64,1280]{1,0:T(8,128)S(1)}, u32[]{:S(2)}, u32[]{:S(2)}) collective-permute-start(f32[64,1280]{1,0:T(8,128)S(1)} %pad_maximum_fusion.11), channel_id=1, source_target_pairs={{0,6},{1,25},{2,0},{3,27},{4,2},{5,29},{6,4},{7,31},{8,14},{9,1},{... | collective-permute-start | bytes 983048 | tf_op jit(solution)/shard_map/ppermute | solution.py:38
  140.7 18.1 %collective-permute-start.15 = (f32[64,1280]{1,0:T(8,128)S(1)}, f32[64,1280]{1,0:T(8,128)S(1)}, u32[]{:S(2)}, u32[]{:S(2)}) collective-permute-start(f32[64,1280]{1,0:T(8,128)S(1)} %pad_maximum_fusion.6), channel_id=1, source_target_pairs={{0,2},{1,9},{2,4},{3,11},{4,6},{5,13},{6,0},{7,15},{8,10},{9,17},{... | collective-permute-start | bytes 983048 | tf_op jit(solution)/shard_map/ppermute | solution.py:38
  147.9 10.9 %collective-permute-start.33 = (f32[64,1280]{1,0:T(8,128)S(1)}, f32[64,1280]{1,0:T(8,128)S(1)}, u32[]{:S(2)}, u32[]{:S(2)}) collective-permute-start(f32[64,1280]{1,0:T(8,128)S(1)} %pad_maximum_fusion.12), channel_id=1, source_target_pairs={{0,2},{1,9},{2,4},{3,11},{4,6},{5,13},{6,0},{7,15},{8,10},{9,17},{... | collective-permute-start | bytes 983048 | tf_op jit(solution)/shard_map/ppermute | solution.py:38
  167.5 15.7 %collective-permute-start.35 = (f32[32,5120]{1,0:T(8,128)S(1)}, f32[32,5120]{1,0:T(8,128)S(1)}, u32[]{:S(2)}, u32[]{:S(2)}) collective-permute-start(f32[32,5120]{1,0:T(8,128)S(1)} %bitcast.58), channel_id=1, source_target_pairs={{0,1},{1,0},{2,3},{3,2},{4,5},{5,4},{6,7},{7,6},{8,9},{9,8},{10,11... | collective-permute-start | bytes 1966088 | tf_op jit(solution)/shard_map/ppermute | solution.py:38
  (26 other events, 147.9 us)

commit v2 on v1

v2 whole, which is shorter than its diff:
```python
import functools

import jax
import jax.numpy as jnp
from jax import lax
from jax.experimental import pallas as pl
from jax.experimental.pallas import tpu as pltpu
from jax.sharding import PartitionSpec as P

AXES = ("y", "x", "z", "c")
SIDE = 4


def routes(target):
    pairs = []
    for y in range(SIDE):
        for x in range(SIDE):
            for z in range(SIDE):
                for c in range(2):
                    ty, tx, tz, tc = target(y, x, z, c)
                    source = ((y * SIDE + x) * SIDE + z) * 2 + c
                    pairs.append((source, ((ty % SIDE * SIDE + tx % SIDE) * SIDE + tz % SIDE) * 2 + tc % 2))
    return pairs


def along_y(step):
    return routes(lambda y, x, z, c: (y + step, x, z, c))


def along_k(step):
    return routes(lambda y, x, z, c: (y, x, z + step, c) if c == 0 else (y, x + step, z, c))


def along_m(step):
    return routes(lambda y, x, z, c: (y, x + step, z, c) if c == 0 else (y, x, z + step, c))


OTHER_CORE = routes(lambda y, x, z, c: (y, x, z, c + 1))
VMEM_SPEC = pl.BlockSpec(memory_space=pltpu.VMEM)
SMEM_SPEC = pl.BlockSpec(memory_space=pltpu.SMEM)


def send(value, route):
    return lax.ppermute(value, AXES, route)


def contracted_split(rows, k_index):
    depth = rows.shape[1] // SIDE
    blocks = [lax.dynamic_slice_in_dim(rows, (k_index + s) % SIDE * depth, depth, axis=1) for s in range(SIDE)]
    moved = {s: send(blocks[s], along_k(s)) for s in (1, 3, 2)}
    return jnp.concatenate([blocks[0], moved[1], moved[2], moved[3]], axis=0)


def ring_gather(block, along):
    half = block.shape[0] // 2
    before = send(block, along(1))
    after = send(block, along(-1))
    return block, before, send(before[:half], along(1)), send(after[half:], along(-1)), after


def place_kernel(where_ref, own_ref, before_ref, far0_ref, far1_ref, after_ref, high_ref, low_ref):
    c, k_index, m_index = where_ref[0], where_ref[1], where_ref[2]
    wide = own_ref.shape[0] // SIDE
    half = wide // 2
    sources = [
        (own_ref, 0, 0, SIDE),
        (before_ref, 1, 0, SIDE),
        (far0_ref, 2, 0, SIDE // 2),
        (far1_ref, 2, SIDE // 2, SIDE // 2),
        (after_ref, 3, 0, SIDE),
    ]
    for ref, t, first, count in sources:
        m = (m_index - t + SIDE) % SIDE

        def body(i, carry, ref=ref, m=m, first=first):
            k = (k_index - i - first + SIDE) % SIDE
            row = jnp.where(c == 0, m * SIDE + k, k * SIDE + m) * wide
            front = ref[pl.ds(pl.multiple_of(i * wide + c * half, 8), half), :]
            back = ref[pl.ds(pl.multiple_of(i * wide + (1 - c) * half, 8), half), :]
            block = jnp.concatenate([front, back], axis=0)
            high = block.astype(jnp.bfloat16)
            low = (block - high.astype(jnp.float32)).astype(jnp.bfloat16)
            high_ref[pl.ds(pl.multiple_of(row, 16), wide), :] = high
            low_ref[pl.ds(pl.multiple_of(row, 16), wide), :] = low
            return carry

        lax.fori_loop(0, count, body, 0)


def place(where, blocks):
    depth = blocks[0].shape[1]
    total = blocks[0].shape[0] * SIDE
    size = total * depth
    return pl.pallas_call(
        place_kernel,
        out_shape=[jax.ShapeDtypeStruct((total, depth), jnp.bfloat16)] * 2,
        in_specs=[SMEM_SPEC] + [VMEM_SPEC] * 5,
        out_specs=[VMEM_SPEC] * 2,
        cost_estimate=pl.CostEstimate(flops=4 * size, bytes_accessed=8 * size, transcendentals=0),
        name="place",
    )(where, *blocks)


def product_kernel(spans, n_in, *refs):
    a_refs, (high_ref, low_ref), rest = refs[:n_in], refs[n_in : n_in + 2], refs[n_in + 2 :]
    out_refs, (a_ref,) = rest[:-1], rest[-1:]
    rows = a_ref.shape[0] // 2
    at = 0
    for source, first, count, _, _ in spans:
        value = a_refs[source][first : first + count, :]
        high = value.astype(jnp.bfloat16)
        a_ref[at : at + count, :] = high
        a_ref[rows + at : rows + at + count, :] = (value - high.astype(jnp.float32)).astype(jnp.bfloat16)
        at += count
    tile = 256
    dims = (((1,), (1,)), ((), ()))

    def body(j, carry):
        cols = pl.ds(pl.multiple_of(j * tile, tile), tile)
        both = lax.dot_general(a_ref[...], high_ref[cols, :], dims, preferred_element_type=jnp.float32)
        rest_of = lax.dot_general(a_ref[:rows, :], low_ref[cols, :], dims, preferred_element_type=jnp.float32)
        value = both[:rows] + (both[rows:] + rest_of)
        at = 0
        for _, _, count, out, out_first in spans:
            out_refs[out][out_first : out_first + count, cols] = value[at : at + count]
            at += count
        return carry

    lax.fori_loop(0, high_ref.shape[0] // tile, body, 0)


def product(sources, spans, out_rows, high, low, name):
    width, depth = high.shape
    rows = sum(span[2] for span in spans)
    return pl.pallas_call(
        functools.partial(product_kernel, spans, len(sources)),
        out_shape=[jax.ShapeDtypeStruct((count, width), jnp.float32) for count in out_rows],
        in_specs=[VMEM_SPEC] * (len(sources) + 2),
        out_specs=[VMEM_SPEC] * len(out_rows),
        scratch_shapes=[pltpu.VMEM((2 * rows, depth), jnp.bfloat16)],
        cost_estimate=pl.CostEstimate(
            flops=6 * rows * width * depth, bytes_accessed=4 * (rows * (width + depth) + width * depth), transcendentals=0
        ),
        name=name,
    )(*sources, high, low)


def span_list(tops, unit):
    spans, filled = [], [0] * 5
    for source, first, s_of in tops:
        for i, s in enumerate(s_of):
            if s == 2:
                for part, out in ((0, 3), (1, 4)):
                    spans.append((source, first + i * unit + part * unit // 2, unit // 2, out, filled[out]))
                    filled[out] += unit // 2
            else:
                out = {0: 0, 1: 1, 3: 2}[s]
                spans.append((source, first + i * unit, unit, out, filled[out]))
                filled[out] += unit
    return spans, filled


def ring_reduce(parts, halves):
    p0, p1, p3, front, back = parts
    low = send(front, along_k(-1))
    high = send(back, along_k(1))
    pick = halves
    p1 = p1 + jnp.concatenate(
        sum([[low[i * pick : (i + 1) * pick], jnp.zeros_like(low[:pick])] for i in range(low.shape[0] // pick)], []), axis=0
    )
    p3 = p3 + jnp.concatenate(
        sum([[jnp.zeros_like(high[:pick]), high[i * pick : (i + 1) * pick]] for i in range(high.shape[0] // pick)], []), axis=0
    )
    return p0 + send(p1, along_k(-1)) + send(p3, along_k(1))


def finish_kernel(where_ref, r0_ref, q1_ref, q2_ref, q3_ref, near_ref, far_ref, row_ref, col_ref, out_ref):
    c, y = where_ref[0], where_ref[3]
    half, width = q2_ref.shape[0] // 2, q2_ref.shape[1]
    for t, ref in enumerate((r0_ref, q1_ref, q2_ref, q3_ref)):
        cols = pl.ds(pl.multiple_of((y + t) % SIDE * width, 128), width)
        theirs = far_ref[...] if t == 2 else near_ref[{0: 0, 1: 1, 3: 2}[t]]
        for g, value in ((c, ref[:half, :]), (1 - c, theirs)):
            out_ref[g, :, cols] = value / (row_ref[g] + col_ref[g, :, cols])


def finish(where, r0, q1, q2, q3, near, far, row_gap, col_gap):
    half, width = far.shape
    size = 2 * half * SIDE * width
    return pl.pallas_call(
        finish_kernel,
        out_shape=jax.ShapeDtypeStruct((2, half, SIDE * width), jnp.float32),
        in_specs=[SMEM_SPEC] + [VMEM_SPEC] * 8,
        out_specs=VMEM_SPEC,
        cost_estimate=pl.CostEstimate(flops=3 * size, bytes_accessed=8 * size, transcendentals=0),
        name="finish",
    )(where, r0, q1, q2, q3, near, far, row_gap[:, :, None], col_gap[:, None, :])


def per_device(amplitudes, integrals, row_gap, col_gap):
    y, x, z, c = (lax.axis_index(name) for name in AXES)
    k_index = jnp.where(c == 0, z, x)
    m_index = jnp.where(c == 0, x, z)
    where = jnp.stack([c, k_index, m_index, y]).astype(jnp.int32)
    columns = jnp.swapaxes(integrals, 1, 2)

    def both_cores(value):
        own = lax.dynamic_index_in_dim(value, c, 0, keepdims=False)
        other = send(lax.dynamic_index_in_dim(value, 1 - c, 0, keepdims=False), OTHER_CORE)
        return jnp.concatenate([own, other], axis=0)

    rows = both_cores(amplitudes)
    cols = both_cores(columns)
    a_own, a_before, a_far0, a_far1, a_after = ring_gather(contracted_split(rows, k_index), along_y)
    high, low = place(where, ring_gather(contracted_split(cols, k_index), along_m))

    unit = rows.shape[0]
    spans, filled = span_list([(0, 0, range(SIDE))], unit)
    own = ring_reduce(product([a_own], spans, filled, high, low, "product_own"), unit // 2)
    spans, filled = span_list([(0, 0, range(SIDE)), (1, 0, range(SIDE))], unit)
    near = ring_reduce(product([a_before, a_after], spans, filled, high, low, "product_near"), unit // 2)
    spans, filled = span_list([(0, 0, (0, 1)), (1, 0, (2, 3))], unit)
    far = ring_reduce(product([a_far0, a_far1], spans, filled, high, low, "product_far"), unit // 2)

    q1 = send(near[:unit], along_y(-1))
    q3 = send(near[unit:], along_y(1))
    q2 = send(far, along_y(2))
    half = unit // 2
    near_theirs = send(jnp.stack([own[half:], q1[half:], q3[half:]]), OTHER_CORE)
    far_theirs = send(q2[half:], OTHER_CORE)
    return finish(where, own, q1, q2, q3, near_theirs, far_theirs, row_gap, col_gap)


def solution(mesh):
    fine = jax.sharding.Mesh(mesh.devices.reshape(SIDE, SIDE, SIDE, 2), AXES)
    placed = (P(None, AXES, None), P(None, None, AXES), P(None, AXES), P())
    return jax.shard_map(
        per_device, mesh=fine, in_specs=placed, out_specs=P(None, AXES, None), check_vma=False
    )
```

time: 186 us -> 163 us (0.88)
  Pallas kernels: 0 us -> 37.9 us
  matrix products: 16.9 us -> 0 us
  local copies, waits for them, and re-layouts: 23.2 us -> 10 us
  waiting for transfers between devices: 78.6 us -> 66.4 us
  other arithmetic: 14.1 us -> 2.55 us
  starting transfers between devices: 52.1 us -> 45.4 us
    pallas_call x0 -> x5, Pallas kernels: none -> 37.9 us  [the longest x3 28.3 us: product(): pl.pallas_call(functools.partial(product_kernel, spans, len(sources)), ou...]
    dot_general x4 -> x0, matrix products: 16.9 us -> none  [per_device(): lax.dot_general(amp_block, xz, (((1,), (1,)), ((), ())), precision=lax.Pr...]
    gather x3 -> x0, local copies, waits for them, and re-layouts: 13.8 us -> none  [the longest x1 6.63 us: per_device(): by_mk = by_m[:, (k_index - order) % SIDE]]
    ppermute x36 -> x33, waiting for transfers between devices: 78.6 us -> 66.4 us  [send(): return lax.ppermute(value, AXES, route)]
    ppermute x36 -> x33, starting transfers between devices: 52.1 us -> 45.4 us  [send(): return lax.ppermute(value, AXES, route)]
    select_n x5 -> x0, other arithmetic: 5.81 us -> none  [the longest x1 5.64 us: per_device(): jnp.where(c == 0, by_mk, jnp.swapaxes(by_mk, 0, 1))]
    another operation x4 -> x2, other arithmetic: 3.3 us -> 0.68 us  [the longest x1 0.65 us: per_device(): where = jnp.stack([c, k_index, m_index, y]).astype(jnp.int32)]
  transfers between devices with their start and end apart: 36 -> 33, of which waited for: 19 -> 15; matrix products, arithmetic and copies ran while one was open for 26% -> 5% of each run, Pallas kernels for 0% -> 22%
where the time goes in v2:
time: 163 us
  waiting for transfers between devices  66.4 us (41%)
  starting transfers between devices  45.4 us (28%)
  Pallas kernels  37.9 us (23%)
  local copies, waits for them, and re-layouts  10 us (6%)
  other arithmetic  2.55 us (2%)
    ppermute x33, waiting for transfers between devices, send(): return lax.ppermute(value, AXES, route)  66.4 us
    ppermute x33, starting transfers between devices, send(): return lax.ppermute(value, AXES, route)  45.4 us
    pallas_call x3, Pallas kernels, product(): pl.pallas_call(functools.partial(product_kernel, spans, len(sources)), ou...  28.3 us
    pallas_call x1, Pallas kernels, place(): pl.pallas_call(place_kernel, out_shape=[jax.ShapeDtypeStruct((total, dept...  6.85 us
    unnamed x44, local copies, waits for them, and re-layouts  3.59 us
  transfers between devices with their start and end apart: 33, of which 15 were waited for; matrix products, arithmetic and copies ran while one was open for 5% of the time, Pallas kernels for 22%

profile of v2, /device:TPU:1, one launch (start us, length us, event | category | flops | bytes accessed | tf_op | source)
XLA Modules:
  0.0 162.7 jit_solution(6668783426623885425)
XLA Ops:
  5.1 2.6 %collective-permute-start.7 = (f32[80,1280]{1,0:T(8,128)S(1)}, f32[80,1280]{1,0:T(8,128)S(1)}, u32[]{:S(2)}, u32[]{:S(2)}) collective-permute-start(f32[80,1280]{1,0:T(8,128)S(1)} %get-tuple-element.42), channel_id=1, source_target_pairs={{0,6},{1,25},{2,0},{3,27},{4,2},{5,29},{6,4},{7,31},{8,14},{9,1},{... | collective-permute-start | bytes 1228808 | tf_op jit(solution)/shard_map/ppermute | solution.py:44
  11.1 5.9 %collective-permute-done.7 = f32[80,1280]{1,0:T(8,128)S(1)} collective-permute-done((f32[80,1280]{1,0:T(8,128)S(1)}, f32[80,1280]{1,0:T(8,128)S(1)}, u32[]{:S(2)}, u32[]{:S(2)}) %collective-permute-start.7) | collective-permute-done | bytes 409632 | tf_op jit(solution)/shard_map/ppermute | solution.py:44
  17.0 3.7 %collective-permute-done.5 = f32[80,1280]{1,0:T(8,128)S(1)} collective-permute-done((f32[80,1280]{1,0:T(8,128)S(1)}, f32[80,1280]{1,0:T(8,128)S(1)}, u32[]{:S(2)}, u32[]{:S(2)}) %collective-permute-start.5) | collective-permute-done | bytes 409632 | tf_op jit(solution)/shard_map/ppermute | solution.py:44
  26.3 7.4 %collective-permute-done.3 = f32[64,1280]{1,0:T(8,128)S(1)} collective-permute-done((f32[64,1280]{1,0:T(8,128)S(1)}, f32[64,1280]{1,0:T(8,128)S(1)}, u32[]{:S(2)}, u32[]{:S(2)}) %collective-permute-start.3) | collective-permute-done | bytes 327712 | tf_op jit(solution)/shard_map/ppermute | solution.py:44
  33.6 2.8 %collective-permute-done.2 = f32[64,1280]{1,0:T(8,128)S(1)} collective-permute-done((f32[64,1280]{1,0:T(8,128)S(1)}, f32[64,1280]{1,0:T(8,128)S(1)}, u32[]{:S(2)}, u32[]{:S(2)}) %collective-permute-start.2) | collective-permute-done | bytes 327712 | tf_op jit(solution)/shard_map/ppermute | solution.py:44
  36.4 3.8 %collective-permute-done.1 = f32[64,1280]{1,0:T(8,128)S(1)} collective-permute-done((f32[64,1280]{1,0:T(8,128)S(1)}, f32[64,1280]{1,0:T(8,128)S(1)}, u32[]{:S(2)}, u32[]{:S(2)}) %collective-permute-start.1) | collective-permute-done | bytes 327712 | tf_op jit(solution)/shard_map/ppermute | solution.py:44
  44.1 6.2 %collective-permute-done.8.before_ref = f32[320,1280]{1,0:T(8,128)S(1)} collective-permute-done((f32[320,1280]{1,0:T(8,128)S(1)}, f32[320,1280]{1,0:T(8,128)S(1)}, u32[]{:S(2)}, u32[]{:S(2)}) %collective-permute-start.8) | collective-permute-done | bytes 1638432 | tf_op jit(solution)/shard_map/ppermute | solution.py:44
  52.6 2.7 %collective-permute-start.11 = (f32[160,1280]{1,0:T(8,128)S(1)}, f32[160,1280]{1,0:T(8,128)S(1)}, u32[]{:S(2)}, u32[]{:S(2)}) collective-permute-start(f32[160,1280]{1,0:T(8,128)S(1)} %slice.57), channel_id=1, source_target_pairs={{0,24},{1,7},{2,26},{3,1},{4,28},{5,3},{6,30},{7,5},{8,0},{9,15},{... | collective-permute-start | bytes 2457608 | tf_op jit(solution)/shard_map/ppermute | solution.py:44
  56.0 14.1 %collective-permute-done.16.refs_0_ = f32[256,1280]{1,0:T(8,128)} collective-permute-done((f32[256,1280]{1,0:T(8,128)}, f32[256,1280]{1,0:T(8,128)}, u32[]{:S(2)}, u32[]{:S(2)}) %collective-permute-start.16) | collective-permute-done | bytes 1310752 | tf_op jit(solution)/shard_map/ppermute | solution.py:44
  72.4 2.7 %collective-permute-start.24 = (f32[128,1280]{1,0:T(8,128)S(1)}, f32[128,1280]{1,0:T(8,128)}, u32[]{:S(2)}, u32[]{:S(2)}) collective-permute-start(f32[128,1280]{1,0:T(8,128)S(1)} %slice.64), channel_id=1, source_target_pairs={{0,96},{1,97},{2,98},{3,99},{4,100},{5,101},{6,102},{7,103},{8,104... | collective-permute-start | bytes 1966088 | tf_op jit(solution)/shard_map/ppermute | solution.py:44
  76.0 6.9 %place.1 = (bf16[1280,1280]{1,0:T(8,128)(2,1)}, bf16[1280,1280]{1,0:T(8,128)(2,1)}) custom-call(s32[4]{0:T(128)} %pad_add_fusion.4.where_ref, f32[320,1280]{1,0:T(8,128)} %copy-done, f32[320,1280]{1,0:T(8,128)} %copy-done.1, f32[160,1280]{1,0:T(8,128)} %collective-permute-done.9.far0_ref, f32[160,1280]{1,0:T(8,128)} %copy-done.5, f32[320,1280]{1,0:T(8,128)} %copy-done.2), custom_call_target="tpu_custom_call" | custom-call | flops 6553600 | bytes 13107200 | tf_op jit(solution)/shard_map/place/pallas_call | solution.py:94
  82.9 8.3 %product_own.1 = (f32[64,1280]{1,0:T(8,128)}, f32[64,1280]{1,0:T(8,128)}, f32[64,1280]{1,0:T(8,128)}, f32[32,1280]{1,0:T(8,128)}, f32[32,1280]{1,0:T(8,128)}) custom-call(f32[256,1280]{1,0:T(8,128)} %pad_maximum_fusion.1.refs_0_, bf16[1280,1280]{1,0:T(8,128)(2,1)} %get-tuple-element.22.refs_1_.refs_2_, bf16[1280,1280]{1,0:T(8,128)(2,1)} %get-tuple-element.23.refs_2_.refs_3_), custom_call_target="tpu_custom_call" | custom-call | flops 2516582400 | bytes 9175040 | tf_op jit(solution)/shard_map/product_own/pallas_call | solution.py:135
  91.2 4.4 %collective-permute-start.14 = (f32[32,1280]{1,0:T(8,128)}, f32[32,1280]{1,0:T(8,128)S(1)}, u32[]{:S(2)}, u32[]{:S(2)}) collective-permute-start(f32[32,1280]{1,0:T(8,128)} %get-tuple-element.28), channel_id=1, source_target_pairs={{0,2},{1,9},{2,4},{3,11},{4,6},{5,13},{6,0},{7,15},{8,10},{9,17},{... | collective-permute-start | bytes 491528 | tf_op jit(solution)/shard_map/ppermute | solution.py:44
  96.9 11.6 %product_near.1 = (f32[128,1280]{1,0:T(8,128)}, f32[128,1280]{1,0:T(8,128)}, f32[128,1280]{1,0:T(8,128)}, f32[64,1280]{1,0:T(8,128)}, f32[64,1280]{1,0:T(8,128)}) custom-call(f32[256,1280]{1,0:T(8,128)} %collective-permute-done.16.refs_0_, f32[256,1280]{1,0:T(8,128)} %collective-permute-done.17.refs_1_, ...), custom_call_target="tpu_custom_call" | custom-call | flops 5033164800 | bytes 11796480 | tf_op jit(solution)/shard_map/product_near/pallas_call | solution.py:135
  110.0 8.3 %product_far.1 = (f32[64,1280]{1,0:T(8,128)}, f32[64,1280]{1,0:T(8,128)}, f32[64,1280]{1,0:T(8,128)}, f32[32,1280]{1,0:T(8,128)}, f32[32,1280]{1,0:T(8,128)}) custom-call(f32[128,1280]{1,0:T(8,128)} %collective-permute-done.23.refs_0_, f32[128,1280]{1,0:T(8,128)} %collective-permute-done.24.refs_1_, bf16[1280,1280]{1,0:T(8,128)(2,1)} %get-tuple-element.22.refs_1_.refs_2_, ...), custom_call_target="tpu_custom_call" | custom-call | flops 2516582400 | bytes 9175040 | tf_op jit(solution)/shard_map/product_far/pallas_call | solution.py:135
  118.5 2.7 %collective-permute-start.25 = (f32[32,1280]{1,0:T(8,128)}, f32[32,1280]{1,0:T(8,128)S(1)}, u32[]{:S(2)}, u32[]{:S(2)}) collective-permute-start(f32[32,1280]{1,0:T(8,128)} %get-tuple-element.36), channel_id=1, source_target_pairs={{0,6},{1,25},{2,0},{3,27},{4,2},{5,29},{6,4},{7,31},{8,14},{9,1},{... | collective-permute-start | bytes 491528 | tf_op jit(solution)/shard_map/ppermute | solution.py:44
  121.5 2.5 %collective-permute-done.27 = f32[32,1280]{1,0:T(8,128)S(1)} collective-permute-done((f32[32,1280]{1,0:T(8,128)}, f32[32,1280]{1,0:T(8,128)S(1)}, u32[]{:S(2)}, u32[]{:S(2)}) %collective-permute-start.27) | collective-permute-done | bytes 163872 | tf_op jit(solution)/shard_map/ppermute | solution.py:44
  125.6 2.7 %collective-permute-start.26 = (f32[64,1280]{1,0:T(8,128)S(1)}, f32[64,1280]{1,0:T(8,128)S(1)}, u32[]{:S(2)}, u32[]{:S(2)}) collective-permute-start(f32[64,1280]{1,0:T(8,128)S(1)} %pad_add_fusion.1), channel_id=1, source_target_pairs={{0,6},{1,25},{2,0},{3,27},{4,2},{5,29},{6,4},{7,31},{8,14},{9,1},{... | collective-permute-start | bytes 983048 | tf_op jit(solution)/shard_map/ppermute | solution.py:44
  128.6 4.0 %collective-permute-done.28 = f32[64,1280]{1,0:T(8,128)S(1)} collective-permute-done((f32[64,1280]{1,0:T(8,128)S(1)}, f32[64,1280]{1,0:T(8,128)S(1)}, u32[]{:S(2)}, u32[]{:S(2)}) %collective-permute-start.28) | collective-permute-done | bytes 327712 | tf_op jit(solution)/shard_map/ppermute | solution.py:44
  134.3 5.7 %collective-permute-done.21 = f32[128,1280]{1,0:T(8,128)S(1)} collective-permute-done((f32[128,1280]{1,0:T(8,128)S(1)}, f32[128,1280]{1,0:T(8,128)S(1)}, u32[]{:S(2)}, u32[]{:S(2)}) %collective-permute-start.21) | collective-permute-done | bytes 655392 | tf_op jit(solution)/shard_map/ppermute | solution.py:44
  142.6 2.7 %collective-permute-start.22 = (f32[64,1280]{1,0:T(8,128)S(1)}, f32[64,1280]{1,0:T(8,128)S(1)}, u32[]{:S(2)}, u32[]{:S(2)}) collective-permute-start(f32[64,1280]{1,0:T(8,128)S(1)} %get-tuple-element.52), channel_id=1, source_target_pairs={{0,96},{1,97},{2,98},{3,99},{4,100},{5,101},{6,102},{7,103},{8,104... | collective-permute-start | bytes 983048 | tf_op jit(solution)/shard_map/ppermute | solution.py:44
  145.4 5.1 %collective-permute-done.30.q3_ref = f32[64,1280]{1,0:T(8,128)S(1)} collective-permute-done((f32[64,1280]{1,0:T(8,128)S(1)}, f32[64,1280]{1,0:T(8,128)S(1)}, u32[]{:S(2)}, u32[]{:S(2)}) %collective-permute-start.30) | collective-permute-done | bytes 327712 | tf_op jit(solution)/shard_map/ppermute | solution.py:44
  150.6 6.1 %collective-permute-start.31 = (f32[3,32,1280]{2,1,0:T(8,128)S(1)}, f32[3,32,1280]{2,1,0:T(8,128)S(1)}, u32[]{:S(2)}, u32[]{:S(2)}) collective-permute-start(f32[3,32,1280]{2,1,0:T(8,128)S(1)} %pad_maximum_fusion.2), channel_id=1, source_target_pairs={{0,1},{1,0},{2,3},{3,2},{4,5},{5,4},{6,7},{7,6},{8,9},{9,8},{10,11... | collective-permute-start | bytes 1474568 | tf_op jit(solution)/shard_map/ppermute | solution.py:44
  159.9 2.8 %finish.1 = f32[2,32,5120]{2,1,0:T(8,128)} custom-call(s32[4]{0:T(128)} %pad_add_fusion.4.where_ref, f32[64,1280]{1,0:T(8,128)} %copy-done.3, f32[64,1280]{1,0:T(8,128)} %copy-done.8, f32[64,1280]{1,0:T(8,128)} %copy-done.6, f32[64,1280]{1,0:T(8,128)} %copy-done.7, f32[3,32,1280]{2,1,0:T(8,128)} %copy-done.12, f32[32,1280]{1,0:T(8,128)} %copy-done.19, ...), custom_call_target="tpu_custom_call" | custom-call | flops 983040 | bytes 2621440 | tf_op jit(solution)/shard_map/finish/pallas_call | solution.py:190
  (121 shorter events, 36.5 us)
Async XLA Ops:
  5.1 11.9 %collective-permute-start.7 = (f32[80,1280]{1,0:T(8,128)S(1)}, f32[80,1280]{1,0:T(8,128)S(1)}, u32[]{:S(2)}, u32[]{:S(2)}) collective-permute-start(f32[80,1280]{1,0:T(8,128)S(1)} %get-tuple-element.42), channel_id=1, source_target_pairs={{0,6},{1,25},{2,0},{3,27},{4,2},{5,29},{6,4},{7,31},{8,14},{9,1},{... | collective-permute-start | bytes 1228808 | tf_op jit(solution)/shard_map/ppermute | solution.py:44
  7.7 9.3 %collective-permute-start.6 = (f32[80,1280]{1,0:T(8,128)S(1)}, f32[80,1280]{1,0:T(8,128)S(1)}, u32[]{:S(2)}, u32[]{:S(2)}) collective-permute-start(f32[80,1280]{1,0:T(8,128)S(1)} %get-tuple-element.41), channel_id=1, source_target_pairs={{0,4},{1,17},{2,6},{3,19},{4,0},{5,21},{6,2},{7,23},{8,12},{9,25},... | collective-permute-start | bytes 1228808 | tf_op jit(solution)/shard_map/ppermute | solution.py:44
  8.2 12.5 %collective-permute-start.5 = (f32[80,1280]{1,0:T(8,128)S(1)}, f32[80,1280]{1,0:T(8,128)S(1)}, u32[]{:S(2)}, u32[]{:S(2)}) collective-permute-start(f32[80,1280]{1,0:T(8,128)S(1)} %get-tuple-element.40), channel_id=1, source_target_pairs={{0,2},{1,9},{2,4},{3,11},{4,6},{5,13},{6,0},{7,15},{8,10},{9,17},{... | collective-permute-start | bytes 1228808 | tf_op jit(solution)/shard_map/ppermute | solution.py:44
  8.9 15.5 %collective-permute-start = (f32[32,5120]{1,0:T(8,128)S(1)}, f32[32,5120]{1,0:T(8,128)S(1)}, u32[]{:S(2)}, u32[]{:S(2)}) collective-permute-start(f32[32,5120]{1,0:T(8,128)S(1)} %get-tuple-element.49), channel_id=1, source_target_pairs={{0,1},{1,0},{2,3},{3,2},{4,5},{5,4},{6,7},{7,6},{8,9},{9,8},{10,11... | collective-permute-start | bytes 1966088 | tf_op jit(solution)/shard_map/ppermute | solution.py:44
  20.8 29.5 %collective-permute-start.8 = (f32[320,1280]{1,0:T(8,128)S(1)}, f32[320,1280]{1,0:T(8,128)S(1)}, u32[]{:S(2)}, u32[]{:S(2)}) collective-permute-start(f32[320,1280]{1,0:T(8,128)S(1)} %pad_maximum_fusion.own_ref), channel_id=1, source_target_pairs={{0,8},{1,3},{2,10},{3,5},{4,12},{5,7},{6,14},{7,1},{8,16},{9,11},{... | collective-permute-start | bytes 4915208 | tf_op jit(solution)/shard_map/ppermute | solution.py:44
  22.2 29.1 %collective-permute-start.10 = (f32[320,1280]{1,0:T(8,128)S(1)}, f32[320,1280]{1,0:T(8,128)S(1)}, u32[]{:S(2)}, u32[]{:S(2)}) collective-permute-start(f32[320,1280]{1,0:T(8,128)S(1)} %pad_maximum_fusion.own_ref), channel_id=1, source_target_pairs={{0,24},{1,7},{2,26},{3,1},{4,28},{5,3},{6,30},{7,5},{8,0},{9,15},{... | collective-permute-start | bytes 4915208 | tf_op jit(solution)/shard_map/ppermute | solution.py:44
  24.5 9.1 %collective-permute-start.3 = (f32[64,1280]{1,0:T(8,128)S(1)}, f32[64,1280]{1,0:T(8,128)S(1)}, u32[]{:S(2)}, u32[]{:S(2)}) collective-permute-start(f32[64,1280]{1,0:T(8,128)S(1)} %get-tuple-element.48), channel_id=1, source_target_pairs={{0,6},{1,25},{2,0},{3,27},{4,2},{5,29},{6,4},{7,31},{8,14},{9,1},{... | collective-permute-start | bytes 983048 | tf_op jit(solution)/shard_map/ppermute | solution.py:44
  25.2 11.2 %collective-permute-start.2 = (f32[64,1280]{1,0:T(8,128)S(1)}, f32[64,1280]{1,0:T(8,128)S(1)}, u32[]{:S(2)}, u32[]{:S(2)}) collective-permute-start(f32[64,1280]{1,0:T(8,128)S(1)} %get-tuple-element.47), channel_id=1, source_target_pairs={{0,4},{1,17},{2,6},{3,19},{4,0},{5,21},{6,2},{7,23},{8,12},{9,25},... | collective-permute-start | bytes 983048 | tf_op jit(solution)/shard_map/ppermute | solution.py:44
  25.8 14.5 %collective-permute-start.1 = (f32[64,1280]{1,0:T(8,128)S(1)}, f32[64,1280]{1,0:T(8,128)S(1)}, u32[]{:S(2)}, u32[]{:S(2)}) collective-permute-start(f32[64,1280]{1,0:T(8,128)S(1)} %get-tuple-element.46), channel_id=1, source_target_pairs={{0,2},{1,9},{2,4},{3,11},{4,6},{5,13},{6,0},{7,15},{8,10},{9,17},{... | collective-permute-start | bytes 983048 | tf_op jit(solution)/shard_map/ppermute | solution.py:44
  41.4 28.6 %collective-permute-start.16 = (f32[256,1280]{1,0:T(8,128)}, f32[256,1280]{1,0:T(8,128)}, u32[]{:S(2)}, u32[]{:S(2)}) collective-permute-start(f32[256,1280]{1,0:T(8,128)} %pad_maximum_fusion.1.refs_0_), channel_id=1, source_target_pairs={{0,32},{1,33},{2,34},{3,35},{4,36},{5,37},{6,38},{7,39},{8,40},{9,... | collective-permute-start | bytes 3932168 | tf_op jit(solution)/shard_map/ppermute | solution.py:44
  42.7 28.6 %collective-permute-start.17 = (f32[256,1280]{1,0:T(8,128)}, f32[256,1280]{1,0:T(8,128)}, u32[]{:S(2)}, u32[]{:S(2)}) collective-permute-start(f32[256,1280]{1,0:T(8,128)} %pad_maximum_fusion.1.refs_0_), channel_id=1, source_target_pairs={{0,96},{1,97},{2,98},{3,99},{4,100},{5,101},{6,102},{7,103},{8,104... | collective-permute-start | bytes 3932168 | tf_op jit(solution)/shard_map/ppermute | solution.py:44
  51.3 23.8 %collective-permute-start.9 = (f32[160,1280]{1,0:T(8,128)}, f32[160,1280]{1,0:T(8,128)}, u32[]{:S(2)}, u32[]{:S(2)}) collective-permute-start(f32[160,1280]{1,0:T(8,128)} %slice.56), channel_id=1, source_target_pairs={{0,8},{1,3},{2,10},{3,5},{4,12},{5,7},{6,14},{7,1},{8,16},{9,11},{... | collective-permute-start | bytes 2457608 | tf_op jit(solution)/shard_map/ppermute | solution.py:44
  52.6 22.5 %collective-permute-start.11 = (f32[160,1280]{1,0:T(8,128)S(1)}, f32[160,1280]{1,0:T(8,128)S(1)}, u32[]{:S(2)}, u32[]{:S(2)}) collective-permute-start(f32[160,1280]{1,0:T(8,128)S(1)} %slice.57), channel_id=1, source_target_pairs={{0,24},{1,7},{2,26},{3,1},{4,28},{5,3},{6,30},{7,5},{8,0},{9,15},{... | collective-permute-start | bytes 2457608 | tf_op jit(solution)/shard_map/ppermute | solution.py:44
  71.2 38.8 %collective-permute-start.23 = (f32[128,1280]{1,0:T(8,128)S(1)}, f32[128,1280]{1,0:T(8,128)}, u32[]{:S(2)}, u32[]{:S(2)}) collective-permute-start(f32[128,1280]{1,0:T(8,128)S(1)} %slice.63), channel_id=1, source_target_pairs={{0,32},{1,33},{2,34},{3,35},{4,36},{5,37},{6,38},{7,39},{8,40},{9,... | collective-permute-start | bytes 1966088 | tf_op jit(solution)/shard_map/ppermute | solution.py:44
  72.4 37.6 %collective-permute-start.24 = (f32[128,1280]{1,0:T(8,128)S(1)}, f32[128,1280]{1,0:T(8,128)}, u32[]{:S(2)}, u32[]{:S(2)}) collective-permute-start(f32[128,1280]{1,0:T(8,128)S(1)} %slice.64), channel_id=1, source_target_pairs={{0,96},{1,97},{2,98},{3,99},{4,100},{5,101},{6,102},{7,103},{8,104... | collective-permute-start | bytes 1966088 | tf_op jit(solution)/shard_map/ppermute | solution.py:44
  91.2 27.3 %collective-permute-start.14 = (f32[32,1280]{1,0:T(8,128)}, f32[32,1280]{1,0:T(8,128)S(1)}, u32[]{:S(2)}, u32[]{:S(2)}) collective-permute-start(f32[32,1280]{1,0:T(8,128)} %get-tuple-element.28), channel_id=1, source_target_pairs={{0,2},{1,9},{2,4},{3,11},{4,6},{5,13},{6,0},{7,15},{8,10},{9,17},{... | collective-permute-start | bytes 491528 | tf_op jit(solution)/shard_map/ppermute | solution.py:44
  95.6 25.7 %collective-permute-start.12 = (f32[32,1280]{1,0:T(8,128)}, f32[32,1280]{1,0:T(8,128)S(1)}, u32[]{:S(2)}, u32[]{:S(2)}) collective-permute-start(f32[32,1280]{1,0:T(8,128)} %get-tuple-element.26), channel_id=1, source_target_pairs={{0,6},{1,25},{2,0},{3,27},{4,2},{5,29},{6,4},{7,31},{8,14},{9,1},{... | collective-permute-start | bytes 491528 | tf_op jit(solution)/shard_map/ppermute | solution.py:44
  108.5 17.1 %collective-permute-start.18 = (f32[64,1280]{1,0:T(8,128)}, f32[64,1280]{1,0:T(8,128)S(1)}, u32[]{:S(2)}, u32[]{:S(2)}) collective-permute-start(f32[64,1280]{1,0:T(8,128)} %get-tuple-element.31), channel_id=1, source_target_pairs={{0,6},{1,25},{2,0},{3,27},{4,2},{5,29},{6,4},{7,31},{8,14},{9,1},{... | collective-permute-start | bytes 983048 | tf_op jit(solution)/shard_map/ppermute | solution.py:44
  110.0 18.3 %collective-permute-start.20 = (f32[64,1280]{1,0:T(8,128)}, f32[64,1280]{1,0:T(8,128)S(1)}, u32[]{:S(2)}, u32[]{:S(2)}) collective-permute-start(f32[64,1280]{1,0:T(8,128)} %get-tuple-element.33), channel_id=1, source_target_pairs={{0,2},{1,9},{2,4},{3,11},{4,6},{5,13},{6,0},{7,15},{8,10},{9,17},{... | collective-permute-start | bytes 983048 | tf_op jit(solution)/shard_map/ppermute | solution.py:44
  121.3 12.9 %collective-permute-start.15 = (f32[64,1280]{1,0:T(8,128)S(1)}, f32[64,1280]{1,0:T(8,128)S(1)}, u32[]{:S(2)}, u32[]{:S(2)}) collective-permute-start(f32[64,1280]{1,0:T(8,128)S(1)} %pad_add_fusion.2), channel_id=1, source_target_pairs={{0,2},{1,9},{2,4},{3,11},{4,6},{5,13},{6,0},{7,15},{8,10},{9,17},{... | collective-permute-start | bytes 983048 | tf_op jit(solution)/shard_map/ppermute | solution.py:44
  124.0 10.2 %collective-permute-start.13 = (f32[64,1280]{1,0:T(8,128)S(1)}, f32[64,1280]{1,0:T(8,128)S(1)}, u32[]{:S(2)}, u32[]{:S(2)}) collective-permute-start(f32[64,1280]{1,0:T(8,128)S(1)} %pad_add_fusion.3), channel_id=1, source_target_pairs={{0,6},{1,25},{2,0},{3,27},{4,2},{5,29},{6,4},{7,31},{8,14},{9,1},{... | collective-permute-start | bytes 983048 | tf_op jit(solution)/shard_map/ppermute | solution.py:44
  128.5 11.4 %collective-permute-start.21 = (f32[128,1280]{1,0:T(8,128)S(1)}, f32[128,1280]{1,0:T(8,128)S(1)}, u32[]{:S(2)}, u32[]{:S(2)}) collective-permute-start(f32[128,1280]{1,0:T(8,128)S(1)} %get-tuple-element.58), channel_id=1, source_target_pairs={{0,2},{1,9},{2,4},{3,11},{4,6},{5,13},{6,0},{7,15},{8,10},{9,17},{... | collective-permute-start | bytes 1966088 | tf_op jit(solution)/shard_map/ppermute | solution.py:44
  132.6 9.7 %collective-permute-start.19 = (f32[128,1280]{1,0:T(8,128)S(1)}, f32[128,1280]{1,0:T(8,128)S(1)}, u32[]{:S(2)}, u32[]{:S(2)}) collective-permute-start(f32[128,1280]{1,0:T(8,128)S(1)} %get-tuple-element.57), channel_id=1, source_target_pairs={{0,6},{1,25},{2,0},{3,27},{4,2},{5,29},{6,4},{7,31},{8,14},{9,1},{... | collective-permute-start | bytes 1966088 | tf_op jit(solution)/shard_map/ppermute | solution.py:44
  133.8 23.0 %collective-permute-start.29 = (f32[64,1280]{1,0:T(8,128)S(1)}, f32[64,1280]{1,0:T(8,128)S(1)}, u32[]{:S(2)}, u32[]{:S(2)}) collective-permute-start(f32[64,1280]{1,0:T(8,128)S(1)} %add_add_fusion.1), channel_id=1, source_target_pairs={{0,64},{1,65},{2,66},{3,67},{4,68},{5,69},{6,70},{7,71},{8,72},{9,... | collective-permute-start | bytes 983048 | tf_op jit(solution)/shard_map/ppermute | solution.py:44
  (31 other events, 218.3 us)

commit v3 on v2

--- a/solution.py
+++ b/solution.py
@@ -38,46 +38,58 @@
 OTHER_CORE = routes(lambda y, x, z, c: (y, x, z, c + 1))
 VMEM_SPEC = pl.BlockSpec(memory_space=pltpu.VMEM)
 SMEM_SPEC = pl.BlockSpec(memory_space=pltpu.SMEM)
+GRANT = pltpu.CompilerParams(vmem_limit_bytes=20 * 2**20)
 
 
 def send(value, route):
     return lax.ppermute(value, AXES, route)
 
 
-def contracted_split(rows, k_index):
-    depth = rows.shape[1] // SIDE
-    blocks = [lax.dynamic_slice_in_dim(rows, (k_index + s) % SIDE * depth, depth, axis=1) for s in range(SIDE)]
-    moved = {s: send(blocks[s], along_k(s)) for s in (1, 3, 2)}
-    return jnp.concatenate([blocks[0], moved[1], moved[2], moved[3]], axis=0)
+def after(value, *earlier):
+    return lax.optimization_barrier((value, *earlier))[0]
 
 
 def ring_gather(block, along):
     half = block.shape[0] // 2
-    before = send(block, along(1))
-    after = send(block, along(-1))
-    return block, before, send(before[:half], along(1)), send(after[half:], along(-1)), after
-
-
-def place_kernel(where_ref, own_ref, before_ref, far0_ref, far1_ref, after_ref, high_ref, low_ref):
+    low, high = send(block, along(1)), send(block, along(-1))
+    return block, low, send(low[:half], along(1)), send(high[half:], along(-1)), high
+
+
+def pack_kernel(where_ref, rows_ref, cols_ref, other_ref, *out_refs):
+    c, k_index = where_ref[0], where_ref[1]
+    tall, half, depth = rows_ref.shape[1], cols_ref.shape[1], out_refs[0].shape[1]
+    for s, out_ref in enumerate(out_refs):
+        span = pl.ds(pl.multiple_of((k_index + s) % SIDE * depth, 128), depth)
+        out_ref[:tall, :] = rows_ref[c, :, span]
+        out_ref[tall : 2 * tall, :] = other_ref[:tall, span]
+        out_ref[pl.ds(pl.multiple_of(2 * tall + c * half, 8), half), :] = cols_ref[c, :, span]
+        out_ref[pl.ds(pl.multiple_of(2 * tall + (1 - c) * half, 8), half), :] = other_ref[tall:, span]
+
+
+def pack(where, rows, cols, other):
+    height, depth = 2 * other.shape[0], other.shape[1] // SIDE
+    return pl.pallas_call(
+        pack_kernel,
+        out_shape=[jax.ShapeDtypeStruct((height, depth), jnp.float32)] * SIDE,
+        in_specs=[SMEM_SPEC] + [VMEM_SPEC] * 3,
+        out_specs=[VMEM_SPEC] * SIDE,
+        cost_estimate=pl.CostEstimate(flops=0, bytes_accessed=8 * height * depth * SIDE, transcendentals=0),
+        compiler_params=GRANT,
+        name="pack",
+    )(where, rows, cols, other)
+
+
+def place_kernel(sources, where_ref, *refs):
+    refs, high_ref, low_ref = refs[: len(sources)], refs[-2], refs[-1]
     c, k_index, m_index = where_ref[0], where_ref[1], where_ref[2]
-    wide = own_ref.shape[0] // SIDE
-    half = wide // 2
-    sources = [
-        (own_ref, 0, 0, SIDE),
-        (before_ref, 1, 0, SIDE),
-        (far0_ref, 2, 0, SIDE // 2),
-        (far1_ref, 2, SIDE // 2, SIDE // 2),
-        (after_ref, 3, 0, SIDE),
-    ]
-    for ref, t, first, count in sources:
+    for ref, (t, first, count) in zip(refs, sources):
+        wide = ref.shape[0] // count
         m = (m_index - t + SIDE) % SIDE
 
         def body(i, carry, ref=ref, m=m, first=first):
             k = (k_index - i - first + SIDE) % SIDE
             row = jnp.where(c == 0, m * SIDE + k, k * SIDE + m) * wide
-            front = ref[pl.ds(pl.multiple_of(i * wide + c * half, 8), half), :]
-            back = ref[pl.ds(pl.multiple_of(i * wide + (1 - c) * half, 8), half), :]
-            block = jnp.concatenate([front, back], axis=0)
+            block = ref[pl.ds(pl.multiple_of(i * wide, 8), wide), :]
             high = block.astype(jnp.bfloat16)
             low = (block - high.astype(jnp.float32)).astype(jnp.bfloat16)
             high_ref[pl.ds(pl.multiple_of(row, 16), wide), :] = high
@@ -87,18 +99,20 @@
         lax.fori_loop(0, count, body, 0)
 
 
-def place(where, blocks):
+def place(where, blocks, sources, total, into=()):
     depth = blocks[0].shape[1]
-    total = blocks[0].shape[0] * SIDE
-    size = total * depth
-    return pl.pallas_call(
-        place_kernel,
+    size = sum(block.shape[0] for block in blocks) * depth
+    n = len(blocks)
+    return pl.pallas_call(
+        functools.partial(place_kernel, sources),
         out_shape=[jax.ShapeDtypeStruct((total, depth), jnp.bfloat16)] * 2,
-        in_specs=[SMEM_SPEC] + [VMEM_SPEC] * 5,
+        in_specs=[SMEM_SPEC] + [VMEM_SPEC] * (n + len(into)),
         out_specs=[VMEM_SPEC] * 2,
+        input_output_aliases={n + 1 + i: i for i in range(len(into))},
         cost_estimate=pl.CostEstimate(flops=4 * size, bytes_accessed=8 * size, transcendentals=0),
-        name="place",
-    )(where, *blocks)
+        compiler_params=GRANT,
+        name="place_far" if into else "place_near",
+    )(where, *blocks, *into)
 
 
 def product_kernel(spans, n_in, *refs):
@@ -141,6 +155,7 @@
         cost_estimate=pl.CostEstimate(
             flops=6 * rows * width * depth, bytes_accessed=4 * (rows * (width + depth) + width * depth), transcendentals=0
         ),
+        compiler_params=GRANT,
         name=name,
     )(*sources, high, low)
 
@@ -174,6 +189,11 @@
     return p0 + send(p1, along_k(-1)) + send(p3, along_k(1))
 
 
+def direct_reduce(parts):
+    p0, p1, p2, p3 = parts
+    return p0 + send(p1, along_k(-1)) + send(p3, along_k(1)) + send(p2, along_k(2))
+
+
 def finish_kernel(where_ref, r0_ref, q1_ref, q2_ref, q3_ref, near_ref, far_ref, row_ref, col_ref, out_ref):
     c, y = where_ref[0], where_ref[3]
     half, width = q2_ref.shape[0] // 2, q2_ref.shape[1]
@@ -193,8 +213,9 @@
         in_specs=[SMEM_SPEC] + [VMEM_SPEC] * 8,
         out_specs=VMEM_SPEC,
         cost_estimate=pl.CostEstimate(flops=3 * size, bytes_accessed=8 * size, transcendentals=0),
+        compiler_params=GRANT,
         name="finish",
-    )(where, r0, q1, q2, q3, near, far, row_gap[:, :, None], col_gap[:, None, :])
+    )(where, r0, q1, q2, q3, near, far, row_gap, col_gap)
 
 
 def per_device(amplitudes, integrals, row_gap, col_gap):
@@ -204,23 +225,29 @@
     where = jnp.stack([c, k_index, m_index, y]).astype(jnp.int32)
     columns = jnp.swapaxes(integrals, 1, 2)
 
-    def both_cores(value):
-        own = lax.dynamic_index_in_dim(value, c, 0, keepdims=False)
-        other = send(lax.dynamic_index_in_dim(value, 1 - c, 0, keepdims=False), OTHER_CORE)
-        return jnp.concatenate([own, other], axis=0)
-
-    rows = both_cores(amplitudes)
-    cols = both_cores(columns)
-    a_own, a_before, a_far0, a_far1, a_after = ring_gather(contracted_split(rows, k_index), along_y)
-    high, low = place(where, ring_gather(contracted_split(cols, k_index), along_m))
-
-    unit = rows.shape[0]
+    tall = amplitudes.shape[1]
+    other = send(jnp.concatenate([value[1 - c] for value in (amplitudes, columns)], axis=0), OTHER_CORE)
+    packed = pack(where, amplitudes, columns, other)
+    moved = [packed[0]] + [send(packed[s], along_k(s)) for s in (1, 2, 3)]
+    a_block = jnp.concatenate([block[: 2 * tall] for block in moved], axis=0)
+    b_block = jnp.concatenate([block[2 * tall :] for block in moved], axis=0)
+    a_own, a_before, a_far0, a_far1, a_after = ring_gather(a_block, along_y)
+    b_own, b_before, b_far0, b_far1, b_after = ring_gather(b_block, along_m)
+
+    total = b_own.shape[0] * SIDE
+    where, row_gap, col_gap = lax.optimization_barrier((where, row_gap[:, :, None], col_gap[:, None, :]))
+    placed = place(where, [b_own, b_before, b_after], [(0, 0, 4), (1, 0, 4), (3, 0, 4)], total)
+    high, low = place(where, [b_far0, b_far1], [(2, 0, 2), (2, 2, 2)], total, placed)
+
+    unit = 2 * tall
     spans, filled = span_list([(0, 0, range(SIDE))], unit)
-    own = ring_reduce(product([a_own], spans, filled, high, low, "product_own"), unit // 2)
+    own_parts = product([a_own], spans, filled, high, low, "product_own")
+    own = ring_reduce(own_parts, unit // 2)
     spans, filled = span_list([(0, 0, range(SIDE)), (1, 0, range(SIDE))], unit)
-    near = ring_reduce(product([a_before, a_after], spans, filled, high, low, "product_near"), unit // 2)
-    spans, filled = span_list([(0, 0, (0, 1)), (1, 0, (2, 3))], unit)
-    far = ring_reduce(product([a_far0, a_far1], spans, filled, high, low, "product_far"), unit // 2)
+    near_parts = product([after(a_before, own_parts[0]), a_after], spans, filled, high, low, "product_near")
+    near = ring_reduce(near_parts, unit // 2)
+    spans = [(s // 2, s % 2 * unit, unit, s, 0) for s in range(SIDE)]
+    far = direct_reduce(product([after(a_far0, near_parts[0]), a_far1], spans, [unit] * SIDE, high, low, "product_far"))
 
     q1 = send(near[:unit], along_y(-1))
     q3 = send(near[unit:], along_y(1))

time: 163 us -> 130 us (0.80)
  Pallas kernels: 37.9 us -> 20.1 us
  starting transfers between devices: 45.4 us -> 37.7 us
  local copies, waits for them, and re-layouts: 10 us -> 3.18 us
    pallas_call x3, Pallas kernels: 28.3 us -> 14.4 us  [product(): pl.pallas_call(functools.partial(product_kernel, spans, len(sources)), ou...]
    ppermute x33 -> x28, starting transfers between devices: 45.4 us -> 37.7 us  [send(): return lax.ppermute(value, AXES, route)]
    unnamed x44 -> x10, local copies, waits for them, and re-layouts: 3.59 us -> 0.28 us
    pallas_call x1 -> x3, Pallas kernels: 6.85 us -> 3.89 us  [the longest x2 2.31 us: place(): pl.pallas_call(functools.partial(place_kernel, sources), out_shape=[jax.S...]
    slice x4 -> x13, local copies, waits for them, and re-layouts: 3.35 us -> 1.28 us  [the longest x5 0.97 us: per_device(): a_block = jnp.concatenate([block[:2 * tall] for block in moved], axis=0)]
    ppermute x33 -> x28, waiting for transfers between devices: 66.4 us -> 66.4 us  [send(): return lax.ppermute(value, AXES, route)]
  transfers between devices with their start and end apart: 33 -> 28, of which waited for: 15 -> 11; matrix products, arithmetic and copies ran while one was open for 5% -> 1% of each run, Pallas kernels for 22% -> 13%
where the time goes in v3:
time: 130 us
  waiting for transfers between devices  66.4 us (51%)
  starting transfers between devices  37.7 us (29%)
  Pallas kernels  20.1 us (15%)
  local copies, waits for them, and re-layouts  3.18 us (2%)
  other arithmetic  2.07 us (2%)
    ppermute x28, waiting for transfers between devices, send(): return lax.ppermute(value, AXES, route)  66.4 us
    ppermute x28, starting transfers between devices, send(): return lax.ppermute(value, AXES, route)  37.7 us
    pallas_call x3, Pallas kernels, product(): pl.pallas_call(functools.partial(product_kernel, spans, len(sources)), ou...  14.4 us
  transfers between devices with their start and end apart: 28, of which 11 were waited for; matrix products, arithmetic and copies ran while one was open for 1% of the time, Pallas kernels for 13%

profile of v3, /device:TPU:1, one launch (start us, length us, event | category | flops | bytes accessed | tf_op | source)
XLA Modules:
  0.0 129.8 jit_solution(1441469540533572813)
XLA Ops:
  4.4 3.2 %collective-permute-done.other_ref = f32[72,5120]{1,0:T(8,128)} collective-permute-done((f32[72,5120]{1,0:T(8,128)}, f32[72,5120]{1,0:T(8,128)}, u32[]{:S(2)}, u32[]{:S(2)}) %collective-permute-start) | collective-permute-done | bytes 1474592 | tf_op jit(solution)/shard_map/ppermute | solution.py:45
  7.6 1.6 %pack.1 = (f32[144,1280]{1,0:T(8,128)S(1)}, f32[144,1280]{1,0:T(8,128)S(1)}, f32[144,1280]{1,0:T(8,128)S(1)}, f32[144,1280]{1,0:T(8,128)S(1)}) custom-call(s32[4]{0:T(128)S(1)} %pad_add_fusion.2.where_ref, f32[2,32,5120]{2,1,0:T(8,128)S(1)} %copy-done.1, f32[2,40,5120]{2,1,0:T(8,128)S(1)} %bitcast.18, f32[72,5120]{1,0:T(8,128)} %collective-permute-done.other_ref), custom_call_target="tpu_custom_call" | custom-call | bytes 5898240 | tf_op jit(solution)/shard_map/pack/pallas_call | solution.py:71
  9.2 2.6 %collective-permute-start.3 = (f32[144,1280]{1,0:T(8,128)S(1)}, f32[144,1280]{1,0:T(8,128)S(1)}, u32[]{:S(2)}, u32[]{:S(2)}) collective-permute-start(f32[144,1280]{1,0:T(8,128)S(1)} %get-tuple-element.36), channel_id=1, source_target_pairs={{0,6},{1,25},{2,0},{3,27},{4,2},{5,29},{6,4},{7,31},{8,14},{9,1},{... | collective-permute-start | bytes 2211848 | tf_op jit(solution)/shard_map/ppermute | solution.py:45
  12.9 15.2 %collective-permute-done.3 = f32[144,1280]{1,0:T(8,128)S(1)} collective-permute-done((f32[144,1280]{1,0:T(8,128)S(1)}, f32[144,1280]{1,0:T(8,128)S(1)}, u32[]{:S(2)}, u32[]{:S(2)}) %collective-permute-start.3) | collective-permute-done | bytes 737312 | tf_op jit(solution)/shard_map/ppermute | solution.py:45
  28.2 3.6 %collective-permute-done.1 = f32[144,1280]{1,0:T(8,128)S(1)} collective-permute-done((f32[144,1280]{1,0:T(8,128)S(1)}, f32[144,1280]{1,0:T(8,128)S(1)}, u32[]{:S(2)}, u32[]{:S(2)}) %collective-permute-start.1) | collective-permute-done | bytes 737312 | tf_op jit(solution)/shard_map/ppermute | solution.py:45
  33.4 2.2 %collective-permute-start.6 = (f32[320,1280]{1,0:T(8,128)S(1)}, f32[320,1280]{1,0:T(8,128)S(1)}, u32[]{:S(2)}, u32[]{:S(2)}) collective-permute-start(f32[320,1280]{1,0:T(8,128)S(1)} %pad_maximum_fusion.refs_0_), channel_id=1, source_target_pairs={{0,24},{1,7},{2,26},{3,1},{4,28},{5,3},{6,30},{7,5},{8,0},{9,15},{... | collective-permute-start | bytes 4915208 | tf_op jit(solution)/shard_map/ppermute | solution.py:45
  38.0 1.5 %collective-permute-start.13 = (f32[256,1280]{1,0:T(8,128)S(1)}, f32[256,1280]{1,0:T(8,128)S(1)}, u32[]{:S(2)}, u32[]{:S(2)}) collective-permute-start(f32[256,1280]{1,0:T(8,128)S(1)} %pad_maximum_fusion.2.refs_0_), channel_id=1, source_target_pairs={{0,96},{1,97},{2,98},{3,99},{4,100},{5,101},{6,102},{7,103},{8,104... | collective-permute-start | bytes 3932168 | tf_op jit(solution)/shard_map/ppermute | solution.py:45
  39.6 14.7 %collective-permute-done.4.refs_1_ = f32[320,1280]{1,0:T(8,128)S(1)} collective-permute-done((f32[320,1280]{1,0:T(8,128)S(1)}, f32[320,1280]{1,0:T(8,128)S(1)}, u32[]{:S(2)}, u32[]{:S(2)}) %collective-permute-start.4) | collective-permute-done | bytes 1638432 | tf_op jit(solution)/shard_map/ppermute | solution.py:45
  54.5 2.7 %collective-permute-start.7 = (f32[160,1280]{1,0:T(8,128)S(1)}, f32[160,1280]{1,0:T(8,128)S(1)}, u32[]{:S(2)}, u32[]{:S(2)}) collective-permute-start(f32[160,1280]{1,0:T(8,128)S(1)} %slice.95), channel_id=1, source_target_pairs={{0,24},{1,7},{2,26},{3,1},{4,28},{5,3},{6,30},{7,5},{8,0},{9,15},{... | collective-permute-start | bytes 2457608 | tf_op jit(solution)/shard_map/ppermute | solution.py:45
  57.3 8.9 %collective-permute-done.12.refs_0_ = f32[256,1280]{1,0:T(8,128)S(1)} collective-permute-done((f32[256,1280]{1,0:T(8,128)S(1)}, f32[256,1280]{1,0:T(8,128)S(1)}, u32[]{:S(2)}, u32[]{:S(2)}) %collective-permute-start.12) | collective-permute-done | bytes 1310752 | tf_op jit(solution)/shard_map/ppermute | solution.py:45
  66.4 2.7 %collective-permute-start.20 = (f32[128,1280]{1,0:T(8,128)S(1)}, f32[128,1280]{1,0:T(8,128)S(1)}, u32[]{:S(2)}, u32[]{:S(2)}) collective-permute-start(f32[128,1280]{1,0:T(8,128)S(1)} %slice.102), channel_id=1, source_target_pairs={{0,96},{1,97},{2,98},{3,99},{4,100},{5,101},{6,102},{7,103},{8,104... | collective-permute-start | bytes 1966088 | tf_op jit(solution)/shard_map/ppermute | solution.py:45
  71.4 3.9 %product_own.1 = (f32[64,1280]{1,0:T(8,128)S(1)}, f32[64,1280]{1,0:T(8,128)S(1)}, f32[64,1280]{1,0:T(8,128)S(1)}, f32[32,1280]{1,0:T(8,128)S(1)}, f32[32,1280]{1,0:T(8,128)S(1)}) custom-call(f32[256,1280]{1,0:T(8,128)S(1)} %pad_maximum_fusion.2.refs_0_, bf16[1280,1280]{1,0:T(8,128)(2,1)S(1)} %get-tuple-element.39.refs_1_.refs_2_, ...), custom_call_target="tpu_custom_call" | custom-call | flops 2516582400 | bytes 9175040 | tf_op jit(solution)/shard_map/product_own/pallas_call | solution.py:149
  75.4 2.7 %collective-permute-start.8 = (f32[32,1280]{1,0:T(8,128)S(1)}, f32[32,1280]{1,0:T(8,128)S(1)}, u32[]{:S(2)}, u32[]{:S(2)}) collective-permute-start(f32[32,1280]{1,0:T(8,128)S(1)} %get-tuple-element.43), channel_id=1, source_target_pairs={{0,6},{1,25},{2,0},{3,27},{4,2},{5,29},{6,4},{7,31},{8,14},{9,1},{... | collective-permute-start | bytes 491528 | tf_op jit(solution)/shard_map/ppermute | solution.py:45
  78.1 6.5 %product_near.1 = (f32[128,1280]{1,0:T(8,128)S(1)}, f32[128,1280]{1,0:T(8,128)S(1)}, f32[128,1280]{1,0:T(8,128)S(1)}, f32[64,1280]{1,0:T(8,128)S(1)}, f32[64,1280]{1,0:T(8,128)S(1)}) custom-call(f32[256,1280]{1,0:T(8,128)S(1)} %collective-permute-done.12.refs_0_, f32[256,1280]{1,0:T(8,128)S(1)} %collective-permute-done.13.refs_1_, ...), custom_call_target="tpu_custom_call" | custom-call | flops 5033164800 | bytes 11796480 | tf_op jit(solution)/shard_map/product_near/pallas_call | solution.py:149
  86.2 3.9 %product_far.1 = (f32[64,1280]{1,0:T(8,128)S(1)}, f32[64,1280]{1,0:T(8,128)S(1)}, f32[64,1280]{1,0:T(8,128)S(1)}, f32[64,1280]{1,0:T(8,128)S(1)}) custom-call(f32[128,1280]{1,0:T(8,128)S(1)} %collective-permute-done.19.refs_0_, f32[128,1280]{1,0:T(8,128)S(1)} %collective-permute-done.20.refs_1_, bf16[1280,1280]{1,0:T(8,128)(2,1)S(1)} %get-tuple-element.39.refs_1_.refs_2_, ...), custom_call_target="tpu_custom_call" | custom-call | flops 2516582400 | bytes 9175040 | tf_op jit(solution)/shard_map/product_far/pallas_call | solution.py:149
  90.2 1.9 %collective-permute-start.22 = (f32[64,1280]{1,0:T(8,128)S(1)}, f32[64,1280]{1,0:T(8,128)S(1)}, u32[]{:S(2)}, u32[]{:S(2)}) collective-permute-start(f32[64,1280]{1,0:T(8,128)S(1)} %get-tuple-element.55), channel_id=1, source_target_pairs={{0,2},{1,9},{2,4},{3,11},{4,6},{5,13},{6,0},{7,15},{8,10},{9,17},{... | collective-permute-start | bytes 983048 | tf_op jit(solution)/shard_map/ppermute | solution.py:45
  93.8 2.3 %collective-permute-start.9 = (f32[64,1280]{1,0:T(8,128)S(1)}, f32[64,1280]{1,0:T(8,128)S(1)}, u32[]{:S(2)}, u32[]{:S(2)}) collective-permute-start(f32[64,1280]{1,0:T(8,128)S(1)} %pad_add_fusion.1), channel_id=1, source_target_pairs={{0,6},{1,25},{2,0},{3,27},{4,2},{5,29},{6,4},{7,31},{8,14},{9,1},{... | collective-permute-start | bytes 983048 | tf_op jit(solution)/shard_map/ppermute | solution.py:45
  97.7 3.5 %collective-permute-done.22 = f32[64,1280]{1,0:T(8,128)S(1)} collective-permute-done((f32[64,1280]{1,0:T(8,128)S(1)}, f32[64,1280]{1,0:T(8,128)S(1)}, u32[]{:S(2)}, u32[]{:S(2)}) %collective-permute-start.22) | collective-permute-done | bytes 327712 | tf_op jit(solution)/shard_map/ppermute | solution.py:45
  102.3 2.4 %collective-permute-done.11 = f32[64,1280]{1,0:T(8,128)S(1)} collective-permute-done((f32[64,1280]{1,0:T(8,128)S(1)}, f32[64,1280]{1,0:T(8,128)S(1)}, u32[]{:S(2)}, u32[]{:S(2)}) %collective-permute-start.11) | collective-permute-done | bytes 327712 | tf_op jit(solution)/shard_map/ppermute | solution.py:45
  104.8 6.9 %collective-permute-done.17 = f32[128,1280]{1,0:T(8,128)S(1)} collective-permute-done((f32[128,1280]{1,0:T(8,128)S(1)}, f32[128,1280]{1,0:T(8,128)S(1)}, u32[]{:S(2)}, u32[]{:S(2)}) %collective-permute-start.17) | collective-permute-done | bytes 655392 | tf_op jit(solution)/shard_map/ppermute | solution.py:45
  112.0 2.7 %collective-permute-start.18 = (f32[64,1280]{1,0:T(8,128)S(1)}, f32[64,1280]{1,0:T(8,128)S(1)}, u32[]{:S(2)}, u32[]{:S(2)}) collective-permute-start(f32[64,1280]{1,0:T(8,128)S(1)} %get-tuple-element.60), channel_id=1, source_target_pairs={{0,96},{1,97},{2,98},{3,99},{4,100},{5,101},{6,102},{7,103},{8,104... | collective-permute-start | bytes 983048 | tf_op jit(solution)/shard_map/ppermute | solution.py:45
  114.7 5.1 %collective-permute-done.25.q3_ref = f32[64,1280]{1,0:T(8,128)S(1)} collective-permute-done((f32[64,1280]{1,0:T(8,128)S(1)}, f32[64,1280]{1,0:T(8,128)S(1)}, u32[]{:S(2)}, u32[]{:S(2)}) %collective-permute-start.25) | collective-permute-done | bytes 327712 | tf_op jit(solution)/shard_map/ppermute | solution.py:45
  119.9 6.4 %collective-permute-start.26 = (f32[3,32,1280]{2,1,0:T(8,128)S(1)}, f32[3,32,1280]{2,1,0:T(8,128)S(1)}, u32[]{:S(2)}, u32[]{:S(2)}) collective-permute-start(f32[3,32,1280]{2,1,0:T(8,128)S(1)} %pad_maximum_fusion.3), channel_id=1, source_target_pairs={{0,1},{1,0},{2,3},{3,2},{4,5},{5,4},{6,7},{7,6},{8,9},{9,8},{10,11... | collective-permute-start | bytes 1474568 | tf_op jit(solution)/shard_map/ppermute | solution.py:45
  128.0 1.8 %finish.1 = f32[2,32,5120]{2,1,0:T(8,128)} custom-call(s32[4]{0:T(128)S(1)} %pad_add_fusion.2.where_ref, f32[64,1280]{1,0:T(8,128)S(1)} %add_add_fusion.2.r0_ref, f32[64,1280]{1,0:T(8,128)S(1)} %collective-permute-done.18.q1_ref, f32[64,1280]{1,0:T(8,128)S(1)} %collective-permute-done.24.q2_ref, f32[64,1280]{1,0:T(8,128)S(1)} %collective-permute-done.25.q3_ref, ...), custom_call_target="tpu_custom_call" | custom-call | flops 983040 | bytes 2621440 | tf_op jit(solution)/shard_map/finish/pallas_call | solution.py:210
  (85 shorter events, 20.4 us)
Async XLA Ops:
  9.2 18.9 %collective-permute-start.3 = (f32[144,1280]{1,0:T(8,128)S(1)}, f32[144,1280]{1,0:T(8,128)S(1)}, u32[]{:S(2)}, u32[]{:S(2)}) collective-permute-start(f32[144,1280]{1,0:T(8,128)S(1)} %get-tuple-element.36), channel_id=1, source_target_pairs={{0,6},{1,25},{2,0},{3,27},{4,2},{5,29},{6,4},{7,31},{8,14},{9,1},{... | collective-permute-start | bytes 2211848 | tf_op jit(solution)/shard_map/ppermute | solution.py:45
  11.8 16.3 %collective-permute-start.2 = (f32[144,1280]{1,0:T(8,128)S(1)}, f32[144,1280]{1,0:T(8,128)S(1)}, u32[]{:S(2)}, u32[]{:S(2)}) collective-permute-start(f32[144,1280]{1,0:T(8,128)S(1)} %get-tuple-element.35), channel_id=1, source_target_pairs={{0,4},{1,17},{2,6},{3,19},{4,0},{5,21},{6,2},{7,23},{8,12},{9,25},... | collective-permute-start | bytes 2211848 | tf_op jit(solution)/shard_map/ppermute | solution.py:45
  12.3 19.5 %collective-permute-start.1 = (f32[144,1280]{1,0:T(8,128)S(1)}, f32[144,1280]{1,0:T(8,128)S(1)}, u32[]{:S(2)}, u32[]{:S(2)}) collective-permute-start(f32[144,1280]{1,0:T(8,128)S(1)} %get-tuple-element.34), channel_id=1, source_target_pairs={{0,2},{1,9},{2,4},{3,11},{4,6},{5,13},{6,0},{7,15},{8,10},{9,17},{... | collective-permute-start | bytes 2211848 | tf_op jit(solution)/shard_map/ppermute | solution.py:45
  32.0 22.3 %collective-permute-start.4 = (f32[320,1280]{1,0:T(8,128)S(1)}, f32[320,1280]{1,0:T(8,128)S(1)}, u32[]{:S(2)}, u32[]{:S(2)}) collective-permute-start(f32[320,1280]{1,0:T(8,128)S(1)} %pad_maximum_fusion.refs_0_), channel_id=1, source_target_pairs={{0,8},{1,3},{2,10},{3,5},{4,12},{5,7},{6,14},{7,1},{8,16},{9,11},{... | collective-permute-start | bytes 4915208 | tf_op jit(solution)/shard_map/ppermute | solution.py:45
  33.4 21.1 %collective-permute-start.6 = (f32[320,1280]{1,0:T(8,128)S(1)}, f32[320,1280]{1,0:T(8,128)S(1)}, u32[]{:S(2)}, u32[]{:S(2)}) collective-permute-start(f32[320,1280]{1,0:T(8,128)S(1)} %pad_maximum_fusion.refs_0_), channel_id=1, source_target_pairs={{0,24},{1,7},{2,26},{3,1},{4,28},{5,3},{6,30},{7,5},{8,0},{9,15},{... | collective-permute-start | bytes 4915208 | tf_op jit(solution)/shard_map/ppermute | solution.py:45
  36.7 29.5 %collective-permute-start.12 = (f32[256,1280]{1,0:T(8,128)S(1)}, f32[256,1280]{1,0:T(8,128)S(1)}, u32[]{:S(2)}, u32[]{:S(2)}) collective-permute-start(f32[256,1280]{1,0:T(8,128)S(1)} %pad_maximum_fusion.2.refs_0_), channel_id=1, source_target_pairs={{0,32},{1,33},{2,34},{3,35},{4,36},{5,37},{6,38},{7,39},{8,40},{9,... | collective-permute-start | bytes 3932168 | tf_op jit(solution)/shard_map/ppermute | solution.py:45
  38.0 28.3 %collective-permute-start.13 = (f32[256,1280]{1,0:T(8,128)S(1)}, f32[256,1280]{1,0:T(8,128)S(1)}, u32[]{:S(2)}, u32[]{:S(2)}) collective-permute-start(f32[256,1280]{1,0:T(8,128)S(1)} %pad_maximum_fusion.2.refs_0_), channel_id=1, source_target_pairs={{0,96},{1,97},{2,98},{3,99},{4,100},{5,101},{6,102},{7,103},{8,104... | collective-permute-start | bytes 3932168 | tf_op jit(solution)/shard_map/ppermute | solution.py:45
  54.3 16.2 %collective-permute-start.5 = (f32[160,1280]{1,0:T(8,128)S(1)}, f32[160,1280]{1,0:T(8,128)S(1)}, u32[]{:S(2)}, u32[]{:S(2)}) collective-permute-start(f32[160,1280]{1,0:T(8,128)S(1)} %slice.94), channel_id=1, source_target_pairs={{0,8},{1,3},{2,10},{3,5},{4,12},{5,7},{6,14},{7,1},{8,16},{9,11},{... | collective-permute-start | bytes 2457608 | tf_op jit(solution)/shard_map/ppermute | solution.py:45
  54.5 16.1 %collective-permute-start.7 = (f32[160,1280]{1,0:T(8,128)S(1)}, f32[160,1280]{1,0:T(8,128)S(1)}, u32[]{:S(2)}, u32[]{:S(2)}) collective-permute-start(f32[160,1280]{1,0:T(8,128)S(1)} %slice.95), channel_id=1, source_target_pairs={{0,24},{1,7},{2,26},{3,1},{4,28},{5,3},{6,30},{7,5},{8,0},{9,15},{... | collective-permute-start | bytes 2457608 | tf_op jit(solution)/shard_map/ppermute | solution.py:45
  66.2 18.5 %collective-permute-start.19 = (f32[128,1280]{1,0:T(8,128)S(1)}, f32[128,1280]{1,0:T(8,128)S(1)}, u32[]{:S(2)}, u32[]{:S(2)}) collective-permute-start(f32[128,1280]{1,0:T(8,128)S(1)} %slice.101), channel_id=1, source_target_pairs={{0,32},{1,33},{2,34},{3,35},{4,36},{5,37},{6,38},{7,39},{8,40},{9,... | collective-permute-start | bytes 1966088 | tf_op jit(solution)/shard_map/ppermute | solution.py:45
  66.4 19.8 %collective-permute-start.20 = (f32[128,1280]{1,0:T(8,128)S(1)}, f32[128,1280]{1,0:T(8,128)S(1)}, u32[]{:S(2)}, u32[]{:S(2)}) collective-permute-start(f32[128,1280]{1,0:T(8,128)S(1)} %slice.102), channel_id=1, source_target_pairs={{0,96},{1,97},{2,98},{3,99},{4,100},{5,101},{6,102},{7,103},{8,104... | collective-permute-start | bytes 1966088 | tf_op jit(solution)/shard_map/ppermute | solution.py:45
  75.3 14.8 %collective-permute-start.10 = (f32[32,1280]{1,0:T(8,128)S(1)}, f32[32,1280]{1,0:T(8,128)S(1)}, u32[]{:S(2)}, u32[]{:S(2)}) collective-permute-start(f32[32,1280]{1,0:T(8,128)S(1)} %get-tuple-element.45), channel_id=1, source_target_pairs={{0,2},{1,9},{2,4},{3,11},{4,6},{5,13},{6,0},{7,15},{8,10},{9,17},{... | collective-permute-start | bytes 491528 | tf_op jit(solution)/shard_map/ppermute | solution.py:45
  75.4 16.7 %collective-permute-start.8 = (f32[32,1280]{1,0:T(8,128)S(1)}, f32[32,1280]{1,0:T(8,128)S(1)}, u32[]{:S(2)}, u32[]{:S(2)}) collective-permute-start(f32[32,1280]{1,0:T(8,128)S(1)} %get-tuple-element.43), channel_id=1, source_target_pairs={{0,6},{1,25},{2,0},{3,27},{4,2},{5,29},{6,4},{7,31},{8,14},{9,1},{... | collective-permute-start | bytes 491528 | tf_op jit(solution)/shard_map/ppermute | solution.py:45
  84.6 8.5 %collective-permute-start.14 = (f32[64,1280]{1,0:T(8,128)S(1)}, f32[64,1280]{1,0:T(8,128)S(1)}, u32[]{:S(2)}, u32[]{:S(2)}) collective-permute-start(f32[64,1280]{1,0:T(8,128)S(1)} %get-tuple-element.49), channel_id=1, source_target_pairs={{0,6},{1,25},{2,0},{3,27},{4,2},{5,29},{6,4},{7,31},{8,14},{9,1},{... | collective-permute-start | bytes 983048 | tf_op jit(solution)/shard_map/ppermute | solution.py:45
  84.7 9.1 %collective-permute-start.16 = (f32[64,1280]{1,0:T(8,128)S(1)}, f32[64,1280]{1,0:T(8,128)S(1)}, u32[]{:S(2)}, u32[]{:S(2)}) collective-permute-start(f32[64,1280]{1,0:T(8,128)S(1)} %get-tuple-element.51), channel_id=1, source_target_pairs={{0,2},{1,9},{2,4},{3,11},{4,6},{5,13},{6,0},{7,15},{8,10},{9,17},{... | collective-permute-start | bytes 983048 | tf_op jit(solution)/shard_map/ppermute | solution.py:45
  90.2 11.0 %collective-permute-start.22 = (f32[64,1280]{1,0:T(8,128)S(1)}, f32[64,1280]{1,0:T(8,128)S(1)}, u32[]{:S(2)}, u32[]{:S(2)}) collective-permute-start(f32[64,1280]{1,0:T(8,128)S(1)} %get-tuple-element.55), channel_id=1, source_target_pairs={{0,2},{1,9},{2,4},{3,11},{4,6},{5,13},{6,0},{7,15},{8,10},{9,17},{... | collective-permute-start | bytes 983048 | tf_op jit(solution)/shard_map/ppermute | solution.py:45
  92.1 9.6 %collective-permute-start.21 = (f32[64,1280]{1,0:T(8,128)S(1)}, f32[64,1280]{1,0:T(8,128)S(1)}, u32[]{:S(2)}, u32[]{:S(2)}) collective-permute-start(f32[64,1280]{1,0:T(8,128)S(1)} %get-tuple-element.54), channel_id=1, source_target_pairs={{0,6},{1,25},{2,0},{3,27},{4,2},{5,29},{6,4},{7,31},{8,14},{9,1},{... | collective-permute-start | bytes 983048 | tf_op jit(solution)/shard_map/ppermute | solution.py:45
  93.1 11.6 %collective-permute-start.11 = (f32[64,1280]{1,0:T(8,128)S(1)}, f32[64,1280]{1,0:T(8,128)S(1)}, u32[]{:S(2)}, u32[]{:S(2)}) collective-permute-start(f32[64,1280]{1,0:T(8,128)S(1)} %pad_add_fusion), channel_id=1, source_target_pairs={{0,2},{1,9},{2,4},{3,11},{4,6},{5,13},{6,0},{7,15},{8,10},{9,17},{... | collective-permute-start | bytes 983048 | tf_op jit(solution)/shard_map/ppermute | solution.py:45
  93.8 10.9 %collective-permute-start.9 = (f32[64,1280]{1,0:T(8,128)S(1)}, f32[64,1280]{1,0:T(8,128)S(1)}, u32[]{:S(2)}, u32[]{:S(2)}) collective-permute-start(f32[64,1280]{1,0:T(8,128)S(1)} %pad_add_fusion.1), channel_id=1, source_target_pairs={{0,6},{1,25},{2,0},{3,27},{4,2},{5,29},{6,4},{7,31},{8,14},{9,1},{... | collective-permute-start | bytes 983048 | tf_op jit(solution)/shard_map/ppermute | solution.py:45
  97.7 14.0 %collective-permute-start.17 = (f32[128,1280]{1,0:T(8,128)S(1)}, f32[128,1280]{1,0:T(8,128)S(1)}, u32[]{:S(2)}, u32[]{:S(2)}) collective-permute-start(f32[128,1280]{1,0:T(8,128)S(1)} %get-tuple-element.66), channel_id=1, source_target_pairs={{0,2},{1,9},{2,4},{3,11},{4,6},{5,13},{6,0},{7,15},{8,10},{9,17},{... | collective-permute-start | bytes 1966088 | tf_op jit(solution)/shard_map/ppermute | solution.py:45
  101.2 10.5 %collective-permute-start.15 = (f32[128,1280]{1,0:T(8,128)S(1)}, f32[128,1280]{1,0:T(8,128)S(1)}, u32[]{:S(2)}, u32[]{:S(2)}) collective-permute-start(f32[128,1280]{1,0:T(8,128)S(1)} %get-tuple-element.65), channel_id=1, source_target_pairs={{0,6},{1,25},{2,0},{3,27},{4,2},{5,29},{6,4},{7,31},{8,14},{9,1},{... | collective-permute-start | bytes 1966088 | tf_op jit(solution)/shard_map/ppermute | solution.py:45
  101.8 24.4 %collective-permute-start.24 = (f32[64,1280]{1,0:T(8,128)S(1)}, f32[64,1280]{1,0:T(8,128)S(1)}, u32[]{:S(2)}, u32[]{:S(2)}) collective-permute-start(f32[64,1280]{1,0:T(8,128)S(1)} %add_add_fusion.1), channel_id=1, source_target_pairs={{0,64},{1,65},{2,66},{3,67},{4,68},{5,69},{6,70},{7,71},{8,72},{9,... | collective-permute-start | bytes 983048 | tf_op jit(solution)/shard_map/ppermute | solution.py:45
  111.9 7.9 %collective-permute-start.25 = (f32[64,1280]{1,0:T(8,128)S(1)}, f32[64,1280]{1,0:T(8,128)S(1)}, u32[]{:S(2)}, u32[]{:S(2)}) collective-permute-start(f32[64,1280]{1,0:T(8,128)S(1)} %get-tuple-element.59), channel_id=1, source_target_pairs={{0,32},{1,33},{2,34},{3,35},{4,36},{5,37},{6,38},{7,39},{8,40},{9,... | collective-permute-start | bytes 983048 | tf_op jit(solution)/shard_map/ppermute | solution.py:45
  119.9 8.1 %collective-permute-start.26 = (f32[3,32,1280]{2,1,0:T(8,128)S(1)}, f32[3,32,1280]{2,1,0:T(8,128)S(1)}, u32[]{:S(2)}, u32[]{:S(2)}) collective-permute-start(f32[3,32,1280]{2,1,0:T(8,128)S(1)} %pad_maximum_fusion.3), channel_id=1, source_target_pairs={{0,1},{1,0},{2,3},{3,2},{4,5},{5,4},{6,7},{7,6},{8,9},{9,8},{10,11... | collective-permute-start | bytes 1474568 | tf_op jit(solution)/shard_map/ppermute | solution.py:45
  (10 other events, 72.8 us)

commit v4 on v3

--- a/solution.py
+++ b/solution.py
@@ -49,34 +49,83 @@
     return lax.optimization_barrier((value, *earlier))[0]
 
 
-def ring_gather(block, along):
-    half = block.shape[0] // 2
-    low, high = send(block, along(1)), send(block, along(-1))
-    return block, low, send(low[:half], along(1)), send(high[half:], along(-1)), high
+def ring_near(block, along):
+    return send(block, along(1)), send(block, along(-1))
+
+
+def ring_far(low, high, along):
+    half = low.shape[0] // 2
+    return send(low[:half], along(1)), send(high[half:], along(-1))
 
 
 def pack_kernel(where_ref, rows_ref, cols_ref, other_ref, *out_refs):
     c, k_index = where_ref[0], where_ref[1]
-    tall, half, depth = rows_ref.shape[1], cols_ref.shape[1], out_refs[0].shape[1]
+    tall, depth = rows_ref.shape[1], out_refs[0].shape[1]
+    other_ref[:tall, :] = rows_ref[1 - c]
+    other_ref[tall:, :] = cols_ref[1 - c]
     for s, out_ref in enumerate(out_refs):
         span = pl.ds(pl.multiple_of((k_index + s) % SIDE * depth, 128), depth)
         out_ref[:tall, :] = rows_ref[c, :, span]
-        out_ref[tall : 2 * tall, :] = other_ref[:tall, span]
-        out_ref[pl.ds(pl.multiple_of(2 * tall + c * half, 8), half), :] = cols_ref[c, :, span]
-        out_ref[pl.ds(pl.multiple_of(2 * tall + (1 - c) * half, 8), half), :] = other_ref[tall:, span]
-
-
-def pack(where, rows, cols, other):
-    height, depth = 2 * other.shape[0], other.shape[1] // SIDE
+        out_ref[tall:, :] = cols_ref[c, :, span]
+
+
+def pack(where, rows, cols):
+    height, depth = rows.shape[1] + cols.shape[1], rows.shape[2] // SIDE
     return pl.pallas_call(
         pack_kernel,
+        out_shape=[jax.ShapeDtypeStruct((height, depth * SIDE), jnp.float32)]
+        + [jax.ShapeDtypeStruct((height, depth), jnp.float32)] * SIDE,
+        in_specs=[SMEM_SPEC] + [VMEM_SPEC] * 2,
+        out_specs=[VMEM_SPEC] * (1 + SIDE),
+        cost_estimate=pl.CostEstimate(flops=0, bytes_accessed=16 * height * depth * SIDE, transcendentals=0),
+        compiler_params=GRANT,
+        name="pack",
+    )(where, rows, cols)
+
+
+def split_kernel(where_ref, in_ref, *out_refs):
+    k_index, depth = where_ref[1], out_refs[0].shape[1]
+    for s, out_ref in enumerate(out_refs):
+        out_ref[...] = in_ref[:, pl.ds(pl.multiple_of((k_index + s) % SIDE * depth, 128), depth)]
+
+
+def split(where, value):
+    height, depth = value.shape[0], value.shape[1] // SIDE
+    return pl.pallas_call(
+        split_kernel,
         out_shape=[jax.ShapeDtypeStruct((height, depth), jnp.float32)] * SIDE,
-        in_specs=[SMEM_SPEC] + [VMEM_SPEC] * 3,
+        in_specs=[SMEM_SPEC, VMEM_SPEC],
         out_specs=[VMEM_SPEC] * SIDE,
         cost_estimate=pl.CostEstimate(flops=0, bytes_accessed=8 * height * depth * SIDE, transcendentals=0),
         compiler_params=GRANT,
-        name="pack",
-    )(where, rows, cols, other)
+        name="split",
+    )(where, value)
+
+
+def join_kernel(own, tall, where_ref, *refs):
+    c = where_ref[0]
+    core = c if own else 1 - c
+    a_ref, b_ref = refs[-2:]
+    half = refs[0].shape[0] - tall
+    for s, ref in enumerate(refs[:SIDE]):
+        start = 2 * tall * s + (0 if own else tall)
+        a_ref[start : start + tall, :] = ref[:tall, :]
+        b_ref[pl.ds(pl.multiple_of(2 * half * s + core * half, 8), half), :] = ref[tall:, :]
+
+
+def join(where, blocks, tall, into=()):
+    height, depth = blocks[0].shape
+    shapes = [(2 * tall * SIDE, depth), (2 * (height - tall) * SIDE, depth)]
+    return pl.pallas_call(
+        functools.partial(join_kernel, not into, tall),
+        out_shape=[jax.ShapeDtypeStruct(shape, jnp.float32) for shape in shapes],
+        in_specs=[SMEM_SPEC] + [VMEM_SPEC] * (SIDE + len(into)),
+        out_specs=[VMEM_SPEC] * 2,
+        input_output_aliases={SIDE + 1 + i: i for i in range(len(into))},
+        cost_estimate=pl.CostEstimate(flops=0, bytes_accessed=8 * height * depth * SIDE, transcendentals=0),
+        compiler_params=GRANT,
+        name="join_other" if into else "join_own",
+    )(where, *blocks, *into)
 
 
 def place_kernel(sources, where_ref, *refs):
@@ -160,52 +209,23 @@
     )(*sources, high, low)
 
 
-def span_list(tops, unit):
-    spans, filled = [], [0] * 5
-    for source, first, s_of in tops:
-        for i, s in enumerate(s_of):
-            if s == 2:
-                for part, out in ((0, 3), (1, 4)):
-                    spans.append((source, first + i * unit + part * unit // 2, unit // 2, out, filled[out]))
-                    filled[out] += unit // 2
-            else:
-                out = {0: 0, 1: 1, 3: 2}[s]
-                spans.append((source, first + i * unit, unit, out, filled[out]))
-                filled[out] += unit
-    return spans, filled
-
-
-def ring_reduce(parts, halves):
-    p0, p1, p3, front, back = parts
-    low = send(front, along_k(-1))
-    high = send(back, along_k(1))
-    pick = halves
-    p1 = p1 + jnp.concatenate(
-        sum([[low[i * pick : (i + 1) * pick], jnp.zeros_like(low[:pick])] for i in range(low.shape[0] // pick)], []), axis=0
-    )
-    p3 = p3 + jnp.concatenate(
-        sum([[jnp.zeros_like(high[:pick]), high[i * pick : (i + 1) * pick]] for i in range(high.shape[0] // pick)], []), axis=0
-    )
-    return p0 + send(p1, along_k(-1)) + send(p3, along_k(1))
-
-
 def direct_reduce(parts):
     p0, p1, p2, p3 = parts
     return p0 + send(p1, along_k(-1)) + send(p3, along_k(1)) + send(p2, along_k(2))
 
 
-def finish_kernel(where_ref, r0_ref, q1_ref, q2_ref, q3_ref, near_ref, far_ref, row_ref, col_ref, out_ref):
+def finish_kernel(where_ref, r0_ref, q1_ref, q2_ref, q3_ref, near_ref, last_ref, row_ref, col_ref, out_ref):
     c, y = where_ref[0], where_ref[3]
     half, width = q2_ref.shape[0] // 2, q2_ref.shape[1]
     for t, ref in enumerate((r0_ref, q1_ref, q2_ref, q3_ref)):
         cols = pl.ds(pl.multiple_of((y + t) % SIDE * width, 128), width)
-        theirs = far_ref[...] if t == 2 else near_ref[{0: 0, 1: 1, 3: 2}[t]]
+        theirs = near_ref[t // 2] if t % 2 else last_ref[t // 2]
         for g, value in ((c, ref[:half, :]), (1 - c, theirs)):
             out_ref[g, :, cols] = value / (row_ref[g] + col_ref[g, :, cols])
 
 
-def finish(where, r0, q1, q2, q3, near, far, row_gap, col_gap):
-    half, width = far.shape
+def finish(where, r0, q1, q2, q3, near, last, row_gap, col_gap):
+    _, half, width = last.shape
     size = 2 * half * SIDE * width
     return pl.pallas_call(
         finish_kernel,
@@ -215,7 +235,7 @@
         cost_estimate=pl.CostEstimate(flops=3 * size, bytes_accessed=8 * size, transcendentals=0),
         compiler_params=GRANT,
         name="finish",
-    )(where, r0, q1, q2, q3, near, far, row_gap, col_gap)
+    )(where, r0, q1, q2, q3, near, last, row_gap, col_gap)
 
 
 def per_device(amplitudes, integrals, row_gap, col_gap):
@@ -226,36 +246,41 @@
     columns = jnp.swapaxes(integrals, 1, 2)
 
     tall = amplitudes.shape[1]
-    other = send(jnp.concatenate([value[1 - c] for value in (amplitudes, columns)], axis=0), OTHER_CORE)
-    packed = pack(where, amplitudes, columns, other)
-    moved = [packed[0]] + [send(packed[s], along_k(s)) for s in (1, 2, 3)]
-    a_block = jnp.concatenate([block[: 2 * tall] for block in moved], axis=0)
-    b_block = jnp.concatenate([block[2 * tall :] for block in moved], axis=0)
-    a_own, a_before, a_far0, a_far1, a_after = ring_gather(a_block, along_y)
-    b_own, b_before, b_far0, b_far1, b_after = ring_gather(b_block, along_m)
-
+    other, *packed = pack(where, amplitudes, columns)
+    other_packed = split(where, send(other, OTHER_CORE))
+    own_moved, other_moved = (
+        [blocks[0]] + [send(blocks[s], along_k(s)) for s in (1, 2, 3)] for blocks in (packed, other_packed)
+    )
+    a_own, b_own = join(where, other_moved, tall, join(where, own_moved, tall))
+
+    a_near = ring_near(a_own, along_y)
+    b_near = ring_near(b_own, along_m)
+    b_far = ring_far(*b_near, along_m)
     total = b_own.shape[0] * SIDE
     where, row_gap, col_gap = lax.optimization_barrier((where, row_gap[:, :, None], col_gap[:, None, :]))
-    placed = place(where, [b_own, b_before, b_after], [(0, 0, 4), (1, 0, 4), (3, 0, 4)], total)
-    high, low = place(where, [b_far0, b_far1], [(2, 0, 2), (2, 2, 2)], total, placed)
+    placed = place(where, [b_own, *b_near], [(0, 0, 4), (1, 0, 4), (3, 0, 4)], total)
+    a_near, placed = lax.optimization_barrier((a_near, placed))
+    a_far = ring_far(*a_near, along_y)
+    high, low = place(where, b_far, [(2, 0, 2), (2, 2, 2)], total, placed)
 
     unit = 2 * tall
-    spans, filled = span_list([(0, 0, range(SIDE))], unit)
-    own_parts = product([a_own], spans, filled, high, low, "product_own")
-    own = ring_reduce(own_parts, unit // 2)
-    spans, filled = span_list([(0, 0, range(SIDE)), (1, 0, range(SIDE))], unit)
-    near_parts = product([after(a_before, own_parts[0]), a_after], spans, filled, high, low, "product_near")
-    near = ring_reduce(near_parts, unit // 2)
-    spans = [(s // 2, s % 2 * unit, unit, s, 0) for s in range(SIDE)]
-    far = direct_reduce(product([after(a_far0, near_parts[0]), a_far1], spans, [unit] * SIDE, high, low, "product_far"))
-
+    spans = [(t, s * unit, unit, s, t * unit) for t in range(2) for s in range(SIDE)]
+    near_parts = product(a_near, spans, [2 * unit] * SIDE, high, low, "product_near")
+    near = direct_reduce(near_parts)
     q1 = send(near[:unit], along_y(-1))
     q3 = send(near[unit:], along_y(1))
+    spans = [(s // 2, s % 2 * unit, unit, s, 0) for s in range(SIDE)]
+    far_parts = product([after(a_far[0], near_parts[0]), a_far[1]], spans, [unit] * SIDE, high, low, "product_far")
+    far = direct_reduce([after(far_parts[0], near), *far_parts[1:]])
     q2 = send(far, along_y(2))
-    half = unit // 2
-    near_theirs = send(jnp.stack([own[half:], q1[half:], q3[half:]]), OTHER_CORE)
-    far_theirs = send(q2[half:], OTHER_CORE)
-    return finish(where, own, q1, q2, q3, near_theirs, far_theirs, row_gap, col_gap)
+    spans = [(0, s * unit, unit, s, 0) for s in range(SIDE)]
+    own_parts = product([after(a_own, far_parts[0])], spans, [unit] * SIDE, high, low, "product_own")
+    own_parts = [after(own_parts[0], far, q1, q3)] + [after(part, near) for part in own_parts[1:]]
+    own = direct_reduce(own_parts)
+
+    near_theirs = send(jnp.stack([q1[tall:], q3[tall:]]), OTHER_CORE)
+    last_theirs = send(jnp.stack([own[tall:], q2[tall:]]), OTHER_CORE)
+    return finish(where, own, q1, q2, q3, near_theirs, last_theirs, row_gap, col_gap)
 
 
 def solution(mesh):

time: 130 us -> 118 us (0.908)
  waiting for transfers between devices: 66.4 us -> 53.1 us
  other arithmetic: 2.07 us -> 0.45 us
    ppermute x28 -> x29, waiting for transfers between devices: 66.4 us -> 53.1 us  [send(): return lax.ppermute(value, AXES, route)]
    unnamed x10 -> x8, local copies, waits for them, and re-layouts: 0.28 us -> 2.76 us
    pallas_call x0 -> x3, Pallas kernels: none -> 1.93 us  [the longest x2 1.28 us: join(): pl.pallas_call(functools.partial(join_kernel, not into, tall), out_shape=...]
    concatenate x3 -> x0, other arithmetic: 1.48 us -> none  [the longest x1 1.28 us: per_device(): jnp.concatenate([value[1 - c] for value in (amplitudes, columns)], axis=0)]
    squeeze x2 -> x0, local copies, waits for them, and re-layouts: 1.35 us -> none  [per_device(): value[1 - c]]
    ppermute x28 -> x29, starting transfers between devices: 37.7 us -> 38.6 us  [send(): return lax.ppermute(value, AXES, route)]
  transfers between devices with their start and end apart: 28 -> 29, of which waited for: 11 -> 13; matrix products, arithmetic and copies ran while one was open for 1% -> 1% of each run, Pallas kernels for 13% -> 15%
where the time goes in v4:
time: 118 us; the launch traced here: 117 us
  waiting for transfers between devices  53.1 us (45%)
  starting transfers between devices  38.6 us (33%)
  Pallas kernels  21.2 us (18%)
  local copies, waits for them, and re-layouts  3.17 us (3%)
    ppermute x29, waiting for transfers between devices, send(): return lax.ppermute(value, AXES, route)  53.1 us
    ppermute x29, starting transfers between devices, send(): return lax.ppermute(value, AXES, route)  38.6 us
    pallas_call x3, Pallas kernels, product(): pl.pallas_call(functools.partial(product_kernel, spans, len(sources)), ou...  14.4 us
    unnamed x8, local copies, waits for them, and re-layouts  2.76 us
  transfers between devices with their start and end apart: 29, of which 13 were waited for; matrix products, arithmetic and copies ran while one was open for 1% of the time, Pallas kernels for 15%

profile of v4, /device:TPU:1, one launch (start us, length us, event | category | flops | bytes accessed | tf_op | source)
XLA Modules:
  0.0 116.8 jit_solution(14742395090437881934)
XLA Ops:
  3.6 1.5 %collective-permute-start = (f32[72,5120]{1,0:T(8,128)S(1)}, f32[72,5120]{1,0:T(8,128)S(1)}, u32[]{:S(2)}, u32[]{:S(2)}) collective-permute-start(f32[72,5120]{1,0:T(8,128)S(1)} %get-tuple-element.49), channel_id=1, source_target_pairs={{0,1},{1,0},{2,3},{3,2},{4,5},{5,4},{6,7},{7,6},{8,9},{9,8},{10,11... | collective-permute-start | bytes 4423688 | tf_op jit(solution)/shard_map/ppermute | solution.py:45
  6.4 2.5 %collective-permute-start.5 = (f32[72,1280]{1,0:T(8,128)S(1)}, f32[72,1280]{1,0:T(8,128)S(1)}, u32[]{:S(2)}, u32[]{:S(2)}) collective-permute-start(f32[72,1280]{1,0:T(8,128)S(1)} %get-tuple-element.56), channel_id=1, source_target_pairs={{0,4},{1,17},{2,6},{3,19},{4,0},{5,21},{6,2},{7,23},{8,12},{9,25},... | collective-permute-start | bytes 1105928 | tf_op jit(solution)/shard_map/ppermute | solution.py:45
  14.3 3.7 %collective-permute-done.5.refs_2_ = f32[72,1280]{1,0:T(8,128)S(1)} collective-permute-done((f32[72,1280]{1,0:T(8,128)S(1)}, f32[72,1280]{1,0:T(8,128)S(1)}, u32[]{:S(2)}, u32[]{:S(2)}) %collective-permute-start.5) | collective-permute-done | bytes 368672 | tf_op jit(solution)/shard_map/ppermute | solution.py:45
  18.7 3.3 %collective-permute-done.1.refs_1_ = f32[72,1280]{1,0:T(8,128)S(1)} collective-permute-done((f32[72,1280]{1,0:T(8,128)S(1)}, f32[72,1280]{1,0:T(8,128)S(1)}, u32[]{:S(2)}, u32[]{:S(2)}) %collective-permute-start.1) | collective-permute-done | bytes 368672 | tf_op jit(solution)/shard_map/ppermute | solution.py:45
  21.9 4.0 %collective-permute-done.2.refs_2_ = f32[72,1280]{1,0:T(8,128)S(1)} collective-permute-done((f32[72,1280]{1,0:T(8,128)S(1)}, f32[72,1280]{1,0:T(8,128)S(1)}, u32[]{:S(2)}, u32[]{:S(2)}) %collective-permute-start.2) | collective-permute-done | bytes 368672 | tf_op jit(solution)/shard_map/ppermute | solution.py:45
  28.0 2.2 %collective-permute-start.10 = (f32[320,1280]{1,0:T(8,128)S(1)}, f32[320,1280]{1,0:T(8,128)S(1)}, u32[]{:S(2)}, u32[]{:S(2)}) collective-permute-start(f32[320,1280]{1,0:T(8,128)S(1)} %get-tuple-element.61.refs_0_), channel_id=1, source_target_pairs={{0,24},{1,7},{2,26},{3,1},{4,28},{5,3},{6,30},{7,5},{8,0},{9,15},{... | collective-permute-start | bytes 4915208 | tf_op jit(solution)/shard_map/ppermute | solution.py:45
  31.5 1.4 %collective-permute-start.8 = (f32[256,1280]{1,0:T(8,128)S(1)}, f32[256,1280]{1,0:T(8,128)S(1)}, u32[]{:S(2)}, u32[]{:S(2)}) collective-permute-start(f32[256,1280]{1,0:T(8,128)S(1)} %get-tuple-element.73.refs_0_), channel_id=1, source_target_pairs={{0,96},{1,97},{2,98},{3,99},{4,100},{5,101},{6,102},{7,103},{8,104... | collective-permute-start | bytes 3932168 | tf_op jit(solution)/shard_map/ppermute | solution.py:45
  32.9 16.0 %collective-permute-done.9.refs_1_ = f32[320,1280]{1,0:T(8,128)S(1)} collective-permute-done((f32[320,1280]{1,0:T(8,128)S(1)}, f32[320,1280]{1,0:T(8,128)S(1)}, u32[]{:S(2)}, u32[]{:S(2)}) %collective-permute-start.9) | collective-permute-done | bytes 1638432 | tf_op jit(solution)/shard_map/ppermute | solution.py:45
  49.1 2.7 %collective-permute-start.13 = (f32[160,1280]{1,0:T(8,128)S(1)}, f32[160,1280]{1,0:T(8,128)S(1)}, u32[]{:S(2)}, u32[]{:S(2)}) collective-permute-start(f32[160,1280]{1,0:T(8,128)S(1)} %slice.41), channel_id=1, source_target_pairs={{0,24},{1,7},{2,26},{3,1},{4,28},{5,3},{6,30},{7,5},{8,0},{9,15},{... | collective-permute-start | bytes 2457608 | tf_op jit(solution)/shard_map/ppermute | solution.py:45
  51.9 1.5 %place_near.1 = (bf16[1280,1280]{1,0:T(8,128)(2,1)S(1)}, bf16[1280,1280]{1,0:T(8,128)(2,1)S(1)}) custom-call(s32[4]{0:T(128)S(1)} %pad_add_fusion.where_ref, f32[320,1280]{1,0:T(8,128)S(1)} %get-tuple-element.61.refs_0_, f32[320,1280]{1,0:T(8,128)S(1)} %collective-permute-done.9.refs_1_, f32[320,1280]{1,0:T(8,128)S(1)} %collective-permute-done.10.refs_2_), custom_call_target="tpu_custom_call" | custom-call | flops 4915200 | bytes 9830400 | tf_op jit(solution)/shard_map/place_near/pallas_call | solution.py:155
  53.3 6.5 %collective-permute-done.7.refs_0_ = f32[256,1280]{1,0:T(8,128)S(1)} collective-permute-done((f32[256,1280]{1,0:T(8,128)S(1)}, f32[256,1280]{1,0:T(8,128)S(1)}, u32[]{:S(2)}, u32[]{:S(2)}) %collective-permute-start.7) | collective-permute-done | bytes 1310752 | tf_op jit(solution)/shard_map/ppermute | solution.py:45
  61.0 1.8 %collective-permute-start.14 = (f32[128,1280]{1,0:T(8,128)S(1)}, f32[128,1280]{1,0:T(8,128)S(1)}, u32[]{:S(2)}, u32[]{:S(2)}) collective-permute-start(f32[128,1280]{1,0:T(8,128)S(1)} %slice.33), channel_id=1, source_target_pairs={{0,96},{1,97},{2,98},{3,99},{4,100},{5,101},{6,102},{7,103},{8,104... | collective-permute-start | bytes 1966088 | tf_op jit(solution)/shard_map/ppermute | solution.py:45
  63.6 6.5 %product_near.1 = (f32[128,1280]{1,0:T(8,128)S(1)}, f32[128,1280]{1,0:T(8,128)S(1)}, f32[128,1280]{1,0:T(8,128)S(1)}, f32[128,1280]{1,0:T(8,128)S(1)}) custom-call(f32[256,1280]{1,0:T(8,128)S(1)} %collective-permute-done.7.refs_0_, f32[256,1280]{1,0:T(8,128)S(1)} %collective-permute-done.8.refs_1_, bf16[1280,1280]{1,0:T(8,128)(2,1)S(1)} %get-tuple-element.68.refs_2_.refs_1_, ...), custom_call_target="tpu_custom_call" | custom-call | flops 5033164800 | bytes 11796480 | tf_op jit(solution)/shard_map/product_near/pallas_call | solution.py:198
  70.2 3.3 %collective-permute-start.15 = (f32[128,1280]{1,0:T(8,128)S(1)}, f32[128,1280]{1,0:T(8,128)S(1)}, u32[]{:S(2)}, u32[]{:S(2)}) collective-permute-start(f32[128,1280]{1,0:T(8,128)S(1)} %get-tuple-element.75), channel_id=1, source_target_pairs={{0,6},{1,25},{2,0},{3,27},{4,2},{5,29},{6,4},{7,31},{8,14},{9,1},{... | collective-permute-start | bytes 1966088 | tf_op jit(solution)/shard_map/ppermute | solution.py:45
  73.5 2.1 %collective-permute-start.17 = (f32[128,1280]{1,0:T(8,128)S(1)}, f32[128,1280]{1,0:T(8,128)S(1)}, u32[]{:S(2)}, u32[]{:S(2)}) collective-permute-start(f32[128,1280]{1,0:T(8,128)S(1)} %get-tuple-element.77), channel_id=1, source_target_pairs={{0,4},{1,17},{2,6},{3,19},{4,0},{5,21},{6,2},{7,23},{8,12},{9,25},... | collective-permute-start | bytes 1966088 | tf_op jit(solution)/shard_map/ppermute | solution.py:45
  75.6 3.9 %product_far.1 = (f32[64,1280]{1,0:T(8,128)S(1)}, f32[64,1280]{1,0:T(8,128)S(1)}, f32[64,1280]{1,0:T(8,128)S(1)}, f32[64,1280]{1,0:T(8,128)S(1)}) custom-call(f32[128,1280]{1,0:T(8,128)S(1)} %collective-permute-done.11.refs_0_, f32[128,1280]{1,0:T(8,128)S(1)} %collective-permute-done.14.refs_1_, bf16[1280,1280]{1,0:T(8,128)(2,1)S(1)} %get-tuple-element.68.refs_2_.refs_1_, ...), custom_call_target="tpu_custom_call" | custom-call | flops 2516582400 | bytes 9175040 | tf_op jit(solution)/shard_map/product_far/pallas_call | solution.py:198
  79.5 3.3 %collective-permute-start.18 = (f32[64,1280]{1,0:T(8,128)S(1)}, f32[64,1280]{1,0:T(8,128)S(1)}, u32[]{:S(2)}, u32[]{:S(2)}) collective-permute-start(f32[64,1280]{1,0:T(8,128)S(1)} %get-tuple-element.79), channel_id=1, source_target_pairs={{0,6},{1,25},{2,0},{3,27},{4,2},{5,29},{6,4},{7,31},{8,14},{9,1},{... | collective-permute-start | bytes 983048 | tf_op jit(solution)/shard_map/ppermute | solution.py:45
  82.8 3.9 %product_own.1 = (f32[64,1280]{1,0:T(8,128)S(1)}, f32[64,1280]{1,0:T(8,128)S(1)}, f32[64,1280]{1,0:T(8,128)S(1)}, f32[64,1280]{1,0:T(8,128)S(1)}) custom-call(f32[256,1280]{1,0:T(8,128)S(1)} %get-tuple-element.73.refs_0_, bf16[1280,1280]{1,0:T(8,128)(2,1)S(1)} %get-tuple-element.68.refs_2_.refs_1_, bf16[1280,1280]{1,0:T(8,128)(2,1)S(1)} %get-tuple-element.69.refs_3_.refs_2_), custom_call_target="tpu_custom_call" | custom-call | flops 2516582400 | bytes 9175040 | tf_op jit(solution)/shard_map/product_own/pallas_call | solution.py:198
  89.2 2.3 %collective-permute-done.16 = f32[128,1280]{1,0:T(8,128)S(1)} collective-permute-done((f32[128,1280]{1,0:T(8,128)S(1)}, f32[128,1280]{1,0:T(8,128)S(1)}, u32[]{:S(2)}, u32[]{:S(2)}) %collective-permute-start.16) | collective-permute-done | bytes 655392 | tf_op jit(solution)/shard_map/ppermute | solution.py:45
  91.7 1.9 %collective-permute-start.21 = (f32[64,1280]{1,0:T(8,128)S(1)}, f32[64,1280]{1,0:T(8,128)S(1)}, u32[]{:S(2)}, u32[]{:S(2)}) collective-permute-start(f32[64,1280]{1,0:T(8,128)S(1)} %get-tuple-element.92), channel_id=1, source_target_pairs={{0,96},{1,97},{2,98},{3,99},{4,100},{5,101},{6,102},{7,103},{8,104... | collective-permute-start | bytes 983048 | tf_op jit(solution)/shard_map/ppermute | solution.py:45
  93.6 4.8 %collective-permute-done.19 = f32[64,1280]{1,0:T(8,128)S(1)} collective-permute-done((f32[64,1280]{1,0:T(8,128)S(1)}, f32[64,1280]{1,0:T(8,128)S(1)}, u32[]{:S(2)}, u32[]{:S(2)}) %collective-permute-start.19) | collective-permute-done | bytes 327712 | tf_op jit(solution)/shard_map/ppermute | solution.py:45
  100.8 8.6 %collective-permute-done.24 = f32[64,1280]{1,0:T(8,128)S(1)} collective-permute-done((f32[64,1280]{1,0:T(8,128)S(1)}, f32[64,1280]{1,0:T(8,128)S(1)}, u32[]{:S(2)}, u32[]{:S(2)}) %collective-permute-start.24) | collective-permute-done | bytes 327712 | tf_op jit(solution)/shard_map/ppermute | solution.py:45
  109.6 3.6 %collective-permute-start.28 = (f32[2,32,1280]{2,1,0:T(8,128)S(1)}, f32[2,32,1280]{2,1,0:T(8,128)S(1)}, u32[]{:S(2)}, u32[]{:S(2)}) collective-permute-start(f32[2,32,1280]{2,1,0:T(8,128)S(1)} %pad_maximum_fusion.1), channel_id=1, source_target_pairs={{0,1},{1,0},{2,3},{3,2},{4,5},{5,4},{6,7},{7,6},{8,9},{9,8},{10,11... | collective-permute-start | bytes 983048 | tf_op jit(solution)/shard_map/ppermute | solution.py:45
  114.9 1.8 %finish.1 = f32[2,32,5120]{2,1,0:T(8,128)} custom-call(s32[4]{0:T(128)S(1)} %pad_add_fusion.where_ref, f32[64,1280]{1,0:T(8,128)S(1)} %add_add_fusion.1.r0_ref, f32[64,1280]{1,0:T(8,128)S(1)} %collective-permute-done.21.q1_ref, f32[64,1280]{1,0:T(8,128)S(1)} %collective-permute-done.26.q2_ref, f32[64,1280]{1,0:T(8,128)S(1)} %collective-permute-done.22.q3_ref, ...), custom_call_target="tpu_custom_call" | custom-call | flops 983040 | bytes 2621440 | tf_op jit(solution)/shard_map/finish/pallas_call | solution.py:230
  (69 shorter events, 23.4 us)
Async XLA Ops:
  5.1 7.9 %collective-permute-start.4 = (f32[72,1280]{1,0:T(8,128)S(1)}, f32[72,1280]{1,0:T(8,128)S(1)}, u32[]{:S(2)}, u32[]{:S(2)}) collective-permute-start(f32[72,1280]{1,0:T(8,128)S(1)} %get-tuple-element.55), channel_id=1, source_target_pairs={{0,2},{1,9},{2,4},{3,11},{4,6},{5,13},{6,0},{7,15},{8,10},{9,17},{... | collective-permute-start | bytes 1105928 | tf_op jit(solution)/shard_map/ppermute | solution.py:45
  6.4 11.6 %collective-permute-start.5 = (f32[72,1280]{1,0:T(8,128)S(1)}, f32[72,1280]{1,0:T(8,128)S(1)}, u32[]{:S(2)}, u32[]{:S(2)}) collective-permute-start(f32[72,1280]{1,0:T(8,128)S(1)} %get-tuple-element.56), channel_id=1, source_target_pairs={{0,4},{1,17},{2,6},{3,19},{4,0},{5,21},{6,2},{7,23},{8,12},{9,25},... | collective-permute-start | bytes 1105928 | tf_op jit(solution)/shard_map/ppermute | solution.py:45
  8.8 9.2 %collective-permute-start.6 = (f32[72,1280]{1,0:T(8,128)S(1)}, f32[72,1280]{1,0:T(8,128)S(1)}, u32[]{:S(2)}, u32[]{:S(2)}) collective-permute-start(f32[72,1280]{1,0:T(8,128)S(1)} %get-tuple-element.57), channel_id=1, source_target_pairs={{0,6},{1,25},{2,0},{3,27},{4,2},{5,29},{6,4},{7,31},{8,14},{9,1},{... | collective-permute-start | bytes 1105928 | tf_op jit(solution)/shard_map/ppermute | solution.py:45
  10.6 11.3 %collective-permute-start.1 = (f32[72,1280]{1,0:T(8,128)S(1)}, f32[72,1280]{1,0:T(8,128)S(1)}, u32[]{:S(2)}, u32[]{:S(2)}) collective-permute-start(f32[72,1280]{1,0:T(8,128)S(1)} %get-tuple-element.51), channel_id=1, source_target_pairs={{0,2},{1,9},{2,4},{3,11},{4,6},{5,13},{6,0},{7,15},{8,10},{9,17},{... | collective-permute-start | bytes 1105928 | tf_op jit(solution)/shard_map/ppermute | solution.py:45
  11.0 14.9 %collective-permute-start.2 = (f32[72,1280]{1,0:T(8,128)S(1)}, f32[72,1280]{1,0:T(8,128)S(1)}, u32[]{:S(2)}, u32[]{:S(2)}) collective-permute-start(f32[72,1280]{1,0:T(8,128)S(1)} %get-tuple-element.52), channel_id=1, source_target_pairs={{0,4},{1,17},{2,6},{3,19},{4,0},{5,21},{6,2},{7,23},{8,12},{9,25},... | collective-permute-start | bytes 1105928 | tf_op jit(solution)/shard_map/ppermute | solution.py:45
  12.9 13.0 %collective-permute-start.3 = (f32[72,1280]{1,0:T(8,128)S(1)}, f32[72,1280]{1,0:T(8,128)S(1)}, u32[]{:S(2)}, u32[]{:S(2)}) collective-permute-start(f32[72,1280]{1,0:T(8,128)S(1)} %get-tuple-element.53), channel_id=1, source_target_pairs={{0,6},{1,25},{2,0},{3,27},{4,2},{5,29},{6,4},{7,31},{8,14},{9,1},{... | collective-permute-start | bytes 1105928 | tf_op jit(solution)/shard_map/ppermute | solution.py:45
  26.6 22.3 %collective-permute-start.9 = (f32[320,1280]{1,0:T(8,128)S(1)}, f32[320,1280]{1,0:T(8,128)S(1)}, u32[]{:S(2)}, u32[]{:S(2)}) collective-permute-start(f32[320,1280]{1,0:T(8,128)S(1)} %get-tuple-element.61.refs_0_), channel_id=1, source_target_pairs={{0,8},{1,3},{2,10},{3,5},{4,12},{5,7},{6,14},{7,1},{8,16},{9,11},{... | collective-permute-start | bytes 4915208 | tf_op jit(solution)/shard_map/ppermute | solution.py:45
  28.0 21.1 %collective-permute-start.10 = (f32[320,1280]{1,0:T(8,128)S(1)}, f32[320,1280]{1,0:T(8,128)S(1)}, u32[]{:S(2)}, u32[]{:S(2)}) collective-permute-start(f32[320,1280]{1,0:T(8,128)S(1)} %get-tuple-element.61.refs_0_), channel_id=1, source_target_pairs={{0,24},{1,7},{2,26},{3,1},{4,28},{5,3},{6,30},{7,5},{8,0},{9,15},{... | collective-permute-start | bytes 4915208 | tf_op jit(solution)/shard_map/ppermute | solution.py:45
  30.2 29.7 %collective-permute-start.7 = (f32[256,1280]{1,0:T(8,128)S(1)}, f32[256,1280]{1,0:T(8,128)S(1)}, u32[]{:S(2)}, u32[]{:S(2)}) collective-permute-start(f32[256,1280]{1,0:T(8,128)S(1)} %get-tuple-element.73.refs_0_), channel_id=1, source_target_pairs={{0,32},{1,33},{2,34},{3,35},{4,36},{5,37},{6,38},{7,39},{8,40},{9,... | collective-permute-start | bytes 3932168 | tf_op jit(solution)/shard_map/ppermute | solution.py:45
  31.5 28.4 %collective-permute-start.8 = (f32[256,1280]{1,0:T(8,128)S(1)}, f32[256,1280]{1,0:T(8,128)S(1)}, u32[]{:S(2)}, u32[]{:S(2)}) collective-permute-start(f32[256,1280]{1,0:T(8,128)S(1)} %get-tuple-element.73.refs_0_), channel_id=1, source_target_pairs={{0,96},{1,97},{2,98},{3,99},{4,100},{5,101},{6,102},{7,103},{8,104... | collective-permute-start | bytes 3932168 | tf_op jit(solution)/shard_map/ppermute | solution.py:45
  48.9 13.8 %collective-permute-start.12 = (f32[160,1280]{1,0:T(8,128)S(1)}, f32[160,1280]{1,0:T(8,128)S(1)}, u32[]{:S(2)}, u32[]{:S(2)}) collective-permute-start(f32[160,1280]{1,0:T(8,128)S(1)} %slice.40), channel_id=1, source_target_pairs={{0,8},{1,3},{2,10},{3,5},{4,12},{5,7},{6,14},{7,1},{8,16},{9,11},{... | collective-permute-start | bytes 2457608 | tf_op jit(solution)/shard_map/ppermute | solution.py:45
  49.1 13.7 %collective-permute-start.13 = (f32[160,1280]{1,0:T(8,128)S(1)}, f32[160,1280]{1,0:T(8,128)S(1)}, u32[]{:S(2)}, u32[]{:S(2)}) collective-permute-start(f32[160,1280]{1,0:T(8,128)S(1)} %slice.41), channel_id=1, source_target_pairs={{0,24},{1,7},{2,26},{3,1},{4,28},{5,3},{6,30},{7,5},{8,0},{9,15},{... | collective-permute-start | bytes 2457608 | tf_op jit(solution)/shard_map/ppermute | solution.py:45
  59.9 15.7 %collective-permute-start.11 = (f32[128,1280]{1,0:T(8,128)S(1)}, f32[128,1280]{1,0:T(8,128)S(1)}, u32[]{:S(2)}, u32[]{:S(2)}) collective-permute-start(f32[128,1280]{1,0:T(8,128)S(1)} %slice.30), channel_id=1, source_target_pairs={{0,32},{1,33},{2,34},{3,35},{4,36},{5,37},{6,38},{7,39},{8,40},{9,... | collective-permute-start | bytes 1966088 | tf_op jit(solution)/shard_map/ppermute | solution.py:45
  61.0 14.6 %collective-permute-start.14 = (f32[128,1280]{1,0:T(8,128)S(1)}, f32[128,1280]{1,0:T(8,128)S(1)}, u32[]{:S(2)}, u32[]{:S(2)}) collective-permute-start(f32[128,1280]{1,0:T(8,128)S(1)} %slice.33), channel_id=1, source_target_pairs={{0,96},{1,97},{2,98},{3,99},{4,100},{5,101},{6,102},{7,103},{8,104... | collective-permute-start | bytes 1966088 | tf_op jit(solution)/shard_map/ppermute | solution.py:45
  70.2 17.8 %collective-permute-start.15 = (f32[128,1280]{1,0:T(8,128)S(1)}, f32[128,1280]{1,0:T(8,128)S(1)}, u32[]{:S(2)}, u32[]{:S(2)}) collective-permute-start(f32[128,1280]{1,0:T(8,128)S(1)} %get-tuple-element.75), channel_id=1, source_target_pairs={{0,6},{1,25},{2,0},{3,27},{4,2},{5,29},{6,4},{7,31},{8,14},{9,1},{... | collective-permute-start | bytes 1966088 | tf_op jit(solution)/shard_map/ppermute | solution.py:45
  73.5 18.0 %collective-permute-start.16 = (f32[128,1280]{1,0:T(8,128)S(1)}, f32[128,1280]{1,0:T(8,128)S(1)}, u32[]{:S(2)}, u32[]{:S(2)}) collective-permute-start(f32[128,1280]{1,0:T(8,128)S(1)} %get-tuple-element.76), channel_id=1, source_target_pairs={{0,2},{1,9},{2,4},{3,11},{4,6},{5,13},{6,0},{7,15},{8,10},{9,17},{... | collective-permute-start | bytes 1966088 | tf_op jit(solution)/shard_map/ppermute | solution.py:45
  73.5 18.0 %collective-permute-start.17 = (f32[128,1280]{1,0:T(8,128)S(1)}, f32[128,1280]{1,0:T(8,128)S(1)}, u32[]{:S(2)}, u32[]{:S(2)}) collective-permute-start(f32[128,1280]{1,0:T(8,128)S(1)} %get-tuple-element.77), channel_id=1, source_target_pairs={{0,4},{1,17},{2,6},{3,19},{4,0},{5,21},{6,2},{7,23},{8,12},{9,25},... | collective-permute-start | bytes 1966088 | tf_op jit(solution)/shard_map/ppermute | solution.py:45
  79.5 14.1 %collective-permute-start.18 = (f32[64,1280]{1,0:T(8,128)S(1)}, f32[64,1280]{1,0:T(8,128)S(1)}, u32[]{:S(2)}, u32[]{:S(2)}) collective-permute-start(f32[64,1280]{1,0:T(8,128)S(1)} %get-tuple-element.79), channel_id=1, source_target_pairs={{0,6},{1,25},{2,0},{3,27},{4,2},{5,29},{6,4},{7,31},{8,14},{9,1},{... | collective-permute-start | bytes 983048 | tf_op jit(solution)/shard_map/ppermute | solution.py:45
  82.8 15.6 %collective-permute-start.19 = (f32[64,1280]{1,0:T(8,128)S(1)}, f32[64,1280]{1,0:T(8,128)S(1)}, u32[]{:S(2)}, u32[]{:S(2)}) collective-permute-start(f32[64,1280]{1,0:T(8,128)S(1)} %get-tuple-element.80), channel_id=1, source_target_pairs={{0,2},{1,9},{2,4},{3,11},{4,6},{5,13},{6,0},{7,15},{8,10},{9,17},{... | collective-permute-start | bytes 983048 | tf_op jit(solution)/shard_map/ppermute | solution.py:45
  88.0 10.4 %collective-permute-start.20 = (f32[64,1280]{1,0:T(8,128)S(1)}, f32[64,1280]{1,0:T(8,128)S(1)}, u32[]{:S(2)}, u32[]{:S(2)}) collective-permute-start(f32[64,1280]{1,0:T(8,128)S(1)} %get-tuple-element.81), channel_id=1, source_target_pairs={{0,4},{1,17},{2,6},{3,19},{4,0},{5,21},{6,2},{7,23},{8,12},{9,25},... | collective-permute-start | bytes 983048 | tf_op jit(solution)/shard_map/ppermute | solution.py:45
  91.6 9.1 %collective-permute-start.23 = (f32[64,1280]{1,0:T(8,128)S(1)}, f32[64,1280]{1,0:T(8,128)S(1)}, u32[]{:S(2)}, u32[]{:S(2)}) collective-permute-start(f32[64,1280]{1,0:T(8,128)S(1)} %get-tuple-element.84), channel_id=1, source_target_pairs={{0,6},{1,25},{2,0},{3,27},{4,2},{5,29},{6,4},{7,31},{8,14},{9,1},{... | collective-permute-start | bytes 983048 | tf_op jit(solution)/shard_map/ppermute | solution.py:45
  98.5 10.9 %collective-permute-start.24 = (f32[64,1280]{1,0:T(8,128)S(1)}, f32[64,1280]{1,0:T(8,128)S(1)}, u32[]{:S(2)}, u32[]{:S(2)}) collective-permute-start(f32[64,1280]{1,0:T(8,128)S(1)} %get-tuple-element.86), channel_id=1, source_target_pairs={{0,2},{1,9},{2,4},{3,11},{4,6},{5,13},{6,0},{7,15},{8,10},{9,17},{... | collective-permute-start | bytes 983048 | tf_op jit(solution)/shard_map/ppermute | solution.py:45
  98.5 10.9 %collective-permute-start.25 = (f32[64,1280]{1,0:T(8,128)S(1)}, f32[64,1280]{1,0:T(8,128)S(1)}, u32[]{:S(2)}, u32[]{:S(2)}) collective-permute-start(f32[64,1280]{1,0:T(8,128)S(1)} %get-tuple-element.88), channel_id=1, source_target_pairs={{0,4},{1,17},{2,6},{3,19},{4,0},{5,21},{6,2},{7,23},{8,12},{9,25},... | collective-permute-start | bytes 983048 | tf_op jit(solution)/shard_map/ppermute | solution.py:45
  99.0 10.5 %collective-permute-start.26 = (f32[64,1280]{1,0:T(8,128)S(1)}, f32[64,1280]{1,0:T(8,128)S(1)}, u32[]{:S(2)}, u32[]{:S(2)}) collective-permute-start(f32[64,1280]{1,0:T(8,128)S(1)} %add_add_fusion.2), channel_id=1, source_target_pairs={{0,64},{1,65},{2,66},{3,67},{4,68},{5,69},{6,70},{7,71},{8,72},{9,... | collective-permute-start | bytes 983048 | tf_op jit(solution)/shard_map/ppermute | solution.py:45
  (9 other events, 55.6 us)

commit v5 on v4

--- a/solution.py
+++ b/solution.py
@@ -214,28 +214,36 @@
     return p0 + send(p1, along_k(-1)) + send(p3, along_k(1)) + send(p2, along_k(2))
 
 
-def finish_kernel(where_ref, r0_ref, q1_ref, q2_ref, q3_ref, near_ref, last_ref, row_ref, col_ref, out_ref):
+def finish_kernel(turns, where_ref, *refs):
+    mine_refs, (theirs_ref, row_ref, col_ref) = refs[:2], refs[2:5]
+    out_ref, value_ref, sems = refs[-3:]
     c, y = where_ref[0], where_ref[3]
-    half, width = q2_ref.shape[0] // 2, q2_ref.shape[1]
-    for t, ref in enumerate((r0_ref, q1_ref, q2_ref, q3_ref)):
+    half, width = theirs_ref.shape[1:]
+    copies = []
+    for i, t in enumerate(turns):
         cols = pl.ds(pl.multiple_of((y + t) % SIDE * width, 128), width)
-        theirs = near_ref[t // 2] if t % 2 else last_ref[t // 2]
-        for g, value in ((c, ref[:half, :]), (1 - c, theirs)):
-            out_ref[g, :, cols] = value / (row_ref[g] + col_ref[g, :, cols])
-
-
-def finish(where, r0, q1, q2, q3, near, last, row_gap, col_gap):
-    _, half, width = last.shape
-    size = 2 * half * SIDE * width
-    return pl.pallas_call(
-        finish_kernel,
+        for j, (g, value) in enumerate(((c, mine_refs[i][:half, :]), (1 - c, theirs_ref[i]))):
+            value_ref[i, j] = value / (row_ref[g] + col_ref[g, :, cols])
+            copies.append(pltpu.make_async_copy(value_ref.at[i, j], out_ref.at[g, :, cols], sems.at[i, j]))
+            copies[-1].start()
+    for copy in copies:
+        copy.wait()
+
+
+def finish(where, mine, theirs, row_gap, col_gap, turns, into=()):
+    _, half, width = theirs.shape
+    size = 4 * half * width
+    return pl.pallas_call(
+        functools.partial(finish_kernel, turns),
         out_shape=jax.ShapeDtypeStruct((2, half, SIDE * width), jnp.float32),
-        in_specs=[SMEM_SPEC] + [VMEM_SPEC] * 8,
-        out_specs=VMEM_SPEC,
+        in_specs=[SMEM_SPEC] + [VMEM_SPEC] * 5 + [pl.BlockSpec(memory_space=pl.ANY)] * len(into),
+        out_specs=pl.BlockSpec(memory_space=pl.ANY),
+        scratch_shapes=[pltpu.VMEM((2, 2, half, width), jnp.float32), pltpu.SemaphoreType.DMA((2, 2))],
+        input_output_aliases={6: 0} if into else {},
         cost_estimate=pl.CostEstimate(flops=3 * size, bytes_accessed=8 * size, transcendentals=0),
         compiler_params=GRANT,
-        name="finish",
-    )(where, r0, q1, q2, q3, near, last, row_gap, col_gap)
+        name="finish_last" if into else "finish_near",
+    )(where, *mine, theirs, row_gap, col_gap, *into)
 
 
 def per_device(amplitudes, integrals, row_gap, col_gap):
@@ -275,12 +283,13 @@
     q2 = send(far, along_y(2))
     spans = [(0, s * unit, unit, s, 0) for s in range(SIDE)]
     own_parts = product([after(a_own, far_parts[0])], spans, [unit] * SIDE, high, low, "product_own")
-    own_parts = [after(own_parts[0], far, q1, q3)] + [after(part, near) for part in own_parts[1:]]
+    near_theirs = send(jnp.stack([q1[tall:], q3[tall:]]), OTHER_CORE)
+    done = finish(where, [q1, q3], near_theirs, row_gap, col_gap, (1, 3))
+    own_parts = [after(own_parts[0], far, near_theirs)] + [after(part, near) for part in own_parts[1:]]
     own = direct_reduce(own_parts)
 
-    near_theirs = send(jnp.stack([q1[tall:], q3[tall:]]), OTHER_CORE)
     last_theirs = send(jnp.stack([own[tall:], q2[tall:]]), OTHER_CORE)
-    return finish(where, own, q1, q2, q3, near_theirs, last_theirs, row_gap, col_gap)
+    return finish(where, [own, q2], last_theirs, row_gap, col_gap, (0, 2), (done,))
 
 
 def solution(mesh):

time: 118 us -> 117 us (level)
  waiting for transfers between devices: 53.1 us -> 44.9 us
  starting transfers between devices: 38.6 us -> 45.1 us
  Pallas kernels: 21.2 us -> 22.4 us
    ppermute x29, waiting for transfers between devices: 53.1 us -> 44.9 us  [send(): return lax.ppermute(value, AXES, route)]
    ppermute x29, starting transfers between devices: 38.6 us -> 45.1 us  [send(): return lax.ppermute(value, AXES, route)]
    pallas_call x1 -> x2, Pallas kernels: 1.85 us -> 3.01 us  [finish(): pl.pallas_call(functools.partial(finish_kernel, turns), out_shape=jax.Sha...]
  transfers between devices with their start and end apart: 29 -> 29, of which waited for: 13 -> 12; matrix products, arithmetic and copies ran while one was open for 1% -> 1% of each run, Pallas kernels for 15% -> 17%
where the time goes in v5:
time: 117 us; the launch traced here: 116 us
  starting transfers between devices  45.1 us (39%)
  waiting for transfers between devices  44.9 us (38%)
  Pallas kernels  22.4 us (19%)
  local copies, waits for them, and re-layouts  3.17 us (3%)
    ppermute x29, starting transfers between devices, send(): return lax.ppermute(value, AXES, route)  45.1 us
    ppermute x29, waiting for transfers between devices, send(): return lax.ppermute(value, AXES, route)  44.9 us
    pallas_call x3, Pallas kernels, product(): pl.pallas_call(functools.partial(product_kernel, spans, len(sources)), ou...  14.4 us
    pallas_call x2, Pallas kernels, finish(): pl.pallas_call(functools.partial(finish_kernel, turns), out_shape=jax.Sha...  3.01 us
    unnamed x8, local copies, waits for them, and re-layouts  2.76 us
  transfers between devices with their start and end apart: 29, of which 12 were waited for; matrix products, arithmetic and copies ran while one was open for 1% of the time, Pallas kernels for 17%

profile of v5, /device:TPU:1, one launch (start us, length us, event | category | flops | bytes accessed | tf_op | source)
XLA Modules:
  0.0 116.4 jit_solution(5849725088048053137)
XLA Ops:
  3.6 1.5 %collective-permute-start = (f32[72,5120]{1,0:T(8,128)S(1)}, f32[72,5120]{1,0:T(8,128)S(1)}, u32[]{:S(2)}, u32[]{:S(2)}) collective-permute-start(f32[72,5120]{1,0:T(8,128)S(1)} %get-tuple-element.49), channel_id=1, source_target_pairs={{0,1},{1,0},{2,3},{3,2},{4,5},{5,4},{6,7},{7,6},{8,9},{9,8},{10,11... | collective-permute-start | bytes 4423688 | tf_op jit(solution)/shard_map/ppermute | solution.py:45
  6.4 2.5 %collective-permute-start.5 = (f32[72,1280]{1,0:T(8,128)S(1)}, f32[72,1280]{1,0:T(8,128)S(1)}, u32[]{:S(2)}, u32[]{:S(2)}) collective-permute-start(f32[72,1280]{1,0:T(8,128)S(1)} %get-tuple-element.56), channel_id=1, source_target_pairs={{0,4},{1,17},{2,6},{3,19},{4,0},{5,21},{6,2},{7,23},{8,12},{9,25},... | collective-permute-start | bytes 1105928 | tf_op jit(solution)/shard_map/ppermute | solution.py:45
  14.3 3.7 %collective-permute-done.5.refs_2_ = f32[72,1280]{1,0:T(8,128)S(1)} collective-permute-done((f32[72,1280]{1,0:T(8,128)S(1)}, f32[72,1280]{1,0:T(8,128)S(1)}, u32[]{:S(2)}, u32[]{:S(2)}) %collective-permute-start.5) | collective-permute-done | bytes 368672 | tf_op jit(solution)/shard_map/ppermute | solution.py:45
  18.7 3.3 %collective-permute-done.1.refs_1_ = f32[72,1280]{1,0:T(8,128)S(1)} collective-permute-done((f32[72,1280]{1,0:T(8,128)S(1)}, f32[72,1280]{1,0:T(8,128)S(1)}, u32[]{:S(2)}, u32[]{:S(2)}) %collective-permute-start.1) | collective-permute-done | bytes 368672 | tf_op jit(solution)/shard_map/ppermute | solution.py:45
  21.9 4.0 %collective-permute-done.2.refs_2_ = f32[72,1280]{1,0:T(8,128)S(1)} collective-permute-done((f32[72,1280]{1,0:T(8,128)S(1)}, f32[72,1280]{1,0:T(8,128)S(1)}, u32[]{:S(2)}, u32[]{:S(2)}) %collective-permute-start.2) | collective-permute-done | bytes 368672 | tf_op jit(solution)/shard_map/ppermute | solution.py:45
  28.0 2.2 %collective-permute-start.10 = (f32[320,1280]{1,0:T(8,128)S(1)}, f32[320,1280]{1,0:T(8,128)S(1)}, u32[]{:S(2)}, u32[]{:S(2)}) collective-permute-start(f32[320,1280]{1,0:T(8,128)S(1)} %get-tuple-element.61.refs_0_), channel_id=1, source_target_pairs={{0,24},{1,7},{2,26},{3,1},{4,28},{5,3},{6,30},{7,5},{8,0},{9,15},{... | collective-permute-start | bytes 4915208 | tf_op jit(solution)/shard_map/ppermute | solution.py:45
  32.9 16.0 %collective-permute-done.9.refs_1_ = f32[320,1280]{1,0:T(8,128)S(1)} collective-permute-done((f32[320,1280]{1,0:T(8,128)S(1)}, f32[320,1280]{1,0:T(8,128)S(1)}, u32[]{:S(2)}, u32[]{:S(2)}) %collective-permute-start.9) | collective-permute-done | bytes 1638432 | tf_op jit(solution)/shard_map/ppermute | solution.py:45
  49.1 2.7 %collective-permute-start.13 = (f32[160,1280]{1,0:T(8,128)S(1)}, f32[160,1280]{1,0:T(8,128)S(1)}, u32[]{:S(2)}, u32[]{:S(2)}) collective-permute-start(f32[160,1280]{1,0:T(8,128)S(1)} %slice.41), channel_id=1, source_target_pairs={{0,24},{1,7},{2,26},{3,1},{4,28},{5,3},{6,30},{7,5},{8,0},{9,15},{... | collective-permute-start | bytes 2457608 | tf_op jit(solution)/shard_map/ppermute | solution.py:45
  53.3 6.5 %collective-permute-done.7.refs_0_ = f32[256,1280]{1,0:T(8,128)S(1)} collective-permute-done((f32[256,1280]{1,0:T(8,128)S(1)}, f32[256,1280]{1,0:T(8,128)S(1)}, u32[]{:S(2)}, u32[]{:S(2)}) %collective-permute-start.7) | collective-permute-done | bytes 1310752 | tf_op jit(solution)/shard_map/ppermute | solution.py:45
  61.0 1.8 %collective-permute-start.14 = (f32[128,1280]{1,0:T(8,128)S(1)}, f32[128,1280]{1,0:T(8,128)S(1)}, u32[]{:S(2)}, u32[]{:S(2)}) collective-permute-start(f32[128,1280]{1,0:T(8,128)S(1)} %slice.33), channel_id=1, source_target_pairs={{0,96},{1,97},{2,98},{3,99},{4,100},{5,101},{6,102},{7,103},{8,104... | collective-permute-start | bytes 1966088 | tf_op jit(solution)/shard_map/ppermute | solution.py:45
  63.6 6.5 %product_near.1 = (f32[128,1280]{1,0:T(8,128)S(1)}, f32[128,1280]{1,0:T(8,128)S(1)}, f32[128,1280]{1,0:T(8,128)S(1)}, f32[128,1280]{1,0:T(8,128)S(1)}) custom-call(f32[256,1280]{1,0:T(8,128)S(1)} %collective-permute-done.7.refs_0_, f32[256,1280]{1,0:T(8,128)S(1)} %collective-permute-done.8.refs_1_, bf16[1280,1280]{1,0:T(8,128)(2,1)S(1)} %get-tuple-element.68.refs_2_.refs_1_, ...), custom_call_target="tpu_custom_call" | custom-call | flops 5033164800 | bytes 11796480 | tf_op jit(solution)/shard_map/product_near/pallas_call | solution.py:198
  70.2 3.3 %collective-permute-start.15 = (f32[128,1280]{1,0:T(8,128)S(1)}, f32[128,1280]{1,0:T(8,128)S(1)}, u32[]{:S(2)}, u32[]{:S(2)}) collective-permute-start(f32[128,1280]{1,0:T(8,128)S(1)} %get-tuple-element.75), channel_id=1, source_target_pairs={{0,6},{1,25},{2,0},{3,27},{4,2},{5,29},{6,4},{7,31},{8,14},{9,1},{... | collective-permute-start | bytes 1966088 | tf_op jit(solution)/shard_map/ppermute | solution.py:45
  73.5 2.1 %collective-permute-start.17 = (f32[128,1280]{1,0:T(8,128)S(1)}, f32[128,1280]{1,0:T(8,128)S(1)}, u32[]{:S(2)}, u32[]{:S(2)}) collective-permute-start(f32[128,1280]{1,0:T(8,128)S(1)} %get-tuple-element.77), channel_id=1, source_target_pairs={{0,4},{1,17},{2,6},{3,19},{4,0},{5,21},{6,2},{7,23},{8,12},{9,25},... | collective-permute-start | bytes 1966088 | tf_op jit(solution)/shard_map/ppermute | solution.py:45
  75.6 3.9 %product_far.1 = (f32[64,1280]{1,0:T(8,128)S(1)}, f32[64,1280]{1,0:T(8,128)S(1)}, f32[64,1280]{1,0:T(8,128)S(1)}, f32[64,1280]{1,0:T(8,128)S(1)}) custom-call(f32[128,1280]{1,0:T(8,128)S(1)} %collective-permute-done.11.refs_0_, f32[128,1280]{1,0:T(8,128)S(1)} %collective-permute-done.14.refs_1_, bf16[1280,1280]{1,0:T(8,128)(2,1)S(1)} %get-tuple-element.68.refs_2_.refs_1_, ...), custom_call_target="tpu_custom_call" | custom-call | flops 2516582400 | bytes 9175040 | tf_op jit(solution)/shard_map/product_far/pallas_call | solution.py:198
  79.5 3.3 %collective-permute-start.18 = (f32[64,1280]{1,0:T(8,128)S(1)}, f32[64,1280]{1,0:T(8,128)S(1)}, u32[]{:S(2)}, u32[]{:S(2)}) collective-permute-start(f32[64,1280]{1,0:T(8,128)S(1)} %get-tuple-element.79), channel_id=1, source_target_pairs={{0,6},{1,25},{2,0},{3,27},{4,2},{5,29},{6,4},{7,31},{8,14},{9,1},{... | collective-permute-start | bytes 983048 | tf_op jit(solution)/shard_map/ppermute | solution.py:45
  82.8 3.9 %product_own.1 = (f32[64,1280]{1,0:T(8,128)S(1)}, f32[64,1280]{1,0:T(8,128)S(1)}, f32[64,1280]{1,0:T(8,128)S(1)}, f32[64,1280]{1,0:T(8,128)S(1)}) custom-call(f32[256,1280]{1,0:T(8,128)S(1)} %get-tuple-element.73.refs_0_, bf16[1280,1280]{1,0:T(8,128)(2,1)S(1)} %get-tuple-element.68.refs_2_.refs_1_, bf16[1280,1280]{1,0:T(8,128)(2,1)S(1)} %get-tuple-element.69.refs_3_.refs_2_), custom_call_target="tpu_custom_call" | custom-call | flops 2516582400 | bytes 9175040 | tf_op jit(solution)/shard_map/product_own/pallas_call | solution.py:198
  89.2 2.3 %collective-permute-done.16 = f32[128,1280]{1,0:T(8,128)S(1)} collective-permute-done((f32[128,1280]{1,0:T(8,128)S(1)}, f32[128,1280]{1,0:T(8,128)S(1)}, u32[]{:S(2)}, u32[]{:S(2)}) %collective-permute-start.16) | collective-permute-done | bytes 655392 | tf_op jit(solution)/shard_map/ppermute | solution.py:45
  91.8 2.7 %collective-permute-start.21 = (f32[64,1280]{1,0:T(8,128)S(1)}, f32[64,1280]{1,0:T(8,128)S(1)}, u32[]{:S(2)}, u32[]{:S(2)}) collective-permute-start(f32[64,1280]{1,0:T(8,128)S(1)} %get-tuple-element.91), channel_id=1, source_target_pairs={{0,96},{1,97},{2,98},{3,99},{4,100},{5,101},{6,102},{7,103},{8,104... | collective-permute-start | bytes 983048 | tf_op jit(solution)/shard_map/ppermute | solution.py:45
  95.0 3.5 %collective-permute-done.19 = f32[64,1280]{1,0:T(8,128)S(1)} collective-permute-done((f32[64,1280]{1,0:T(8,128)S(1)}, f32[64,1280]{1,0:T(8,128)S(1)}, u32[]{:S(2)}, u32[]{:S(2)}) %collective-permute-start.19) | collective-permute-done | bytes 327712 | tf_op jit(solution)/shard_map/ppermute | solution.py:45
  100.2 5.8 %collective-permute-start.23 = (f32[2,32,1280]{2,1,0:T(8,128)S(1)}, f32[2,32,1280]{2,1,0:T(8,128)S(1)}, u32[]{:S(2)}, u32[]{:S(2)}) collective-permute-start(f32[2,32,1280]{2,1,0:T(8,128)S(1)} %pad_maximum_fusion), channel_id=1, source_target_pairs={{0,1},{1,0},{2,3},{3,2},{4,5},{5,4},{6,7},{7,6},{8,9},{9,8},{10,11... | collective-permute-start | bytes 983048 | tf_op jit(solution)/shard_map/ppermute | solution.py:45
  107.3 2.1 %collective-permute-done.25 = f32[64,1280]{1,0:T(8,128)S(1)} collective-permute-done((f32[64,1280]{1,0:T(8,128)S(1)}, f32[64,1280]{1,0:T(8,128)S(1)}, u32[]{:S(2)}, u32[]{:S(2)}) %collective-permute-start.25) | collective-permute-done | bytes 327712 | tf_op jit(solution)/shard_map/ppermute | solution.py:45
  109.5 3.6 %collective-permute-start.28 = (f32[2,32,1280]{2,1,0:T(8,128)S(1)}, f32[2,32,1280]{2,1,0:T(8,128)S(1)}, u32[]{:S(2)}, u32[]{:S(2)}) collective-permute-start(f32[2,32,1280]{2,1,0:T(8,128)S(1)} %pad_maximum_fusion.1), channel_id=1, source_target_pairs={{0,1},{1,0},{2,3},{3,2},{4,5},{5,4},{6,7},{7,6},{8,9},{9,8},{10,11... | collective-permute-start | bytes 983048 | tf_op jit(solution)/shard_map/ppermute | solution.py:45
  113.2 1.5 %finish_near.1.refs_5_ = f32[2,32,5120]{2,1,0:T(8,128)} custom-call(s32[4]{0:T(128)S(1)} %pad_add_fusion.where_ref, f32[64,1280]{1,0:T(8,128)S(1)} %collective-permute-done.21.refs_0_, f32[64,1280]{1,0:T(8,128)S(1)} %collective-permute-done.22.refs_1_, f32[2,32,1280]{2,1,0:T(8,128)S(1)} %collective-permute-done.23.refs_2_, f32[2,32,1]{2,1,0:T(8,128)S(1)} %copy.11.refs_3_, ...), custom_call_target="tpu_custom_call" | custom-call | flops 491520 | bytes 1310720 | tf_op jit(solution)/shard_map/finish_near/pallas_call | solution.py:236
  114.7 1.5 %finish_last.1 = f32[2,32,5120]{2,1,0:T(8,128)} custom-call(s32[4]{0:T(128)S(1)} %pad_add_fusion.where_ref, f32[64,1280]{1,0:T(8,128)S(1)} %add_add_fusion.1.refs_0_, f32[64,1280]{1,0:T(8,128)S(1)} %collective-permute-done.27.refs_1_, f32[2,32,1280]{2,1,0:T(8,128)S(1)} %collective-permute-done.28.refs_2_, ...), custom_call_target="tpu_custom_call", output_to_operand_aliasing={{}: (6, {})} | custom-call | flops 491520 | bytes 1310720 | tf_op jit(solution)/shard_map/finish_last/pallas_call | solution.py:236
  (70 shorter events, 25.9 us)
Async XLA Ops:
  5.1 7.9 %collective-permute-start.4 = (f32[72,1280]{1,0:T(8,128)S(1)}, f32[72,1280]{1,0:T(8,128)S(1)}, u32[]{:S(2)}, u32[]{:S(2)}) collective-permute-start(f32[72,1280]{1,0:T(8,128)S(1)} %get-tuple-element.55), channel_id=1, source_target_pairs={{0,2},{1,9},{2,4},{3,11},{4,6},{5,13},{6,0},{7,15},{8,10},{9,17},{... | collective-permute-start | bytes 1105928 | tf_op jit(solution)/shard_map/ppermute | solution.py:45
  6.4 11.6 %collective-permute-start.5 = (f32[72,1280]{1,0:T(8,128)S(1)}, f32[72,1280]{1,0:T(8,128)S(1)}, u32[]{:S(2)}, u32[]{:S(2)}) collective-permute-start(f32[72,1280]{1,0:T(8,128)S(1)} %get-tuple-element.56), channel_id=1, source_target_pairs={{0,4},{1,17},{2,6},{3,19},{4,0},{5,21},{6,2},{7,23},{8,12},{9,25},... | collective-permute-start | bytes 1105928 | tf_op jit(solution)/shard_map/ppermute | solution.py:45
  8.8 9.2 %collective-permute-start.6 = (f32[72,1280]{1,0:T(8,128)S(1)}, f32[72,1280]{1,0:T(8,128)S(1)}, u32[]{:S(2)}, u32[]{:S(2)}) collective-permute-start(f32[72,1280]{1,0:T(8,128)S(1)} %get-tuple-element.57), channel_id=1, source_target_pairs={{0,6},{1,25},{2,0},{3,27},{4,2},{5,29},{6,4},{7,31},{8,14},{9,1},{... | collective-permute-start | bytes 1105928 | tf_op jit(solution)/shard_map/ppermute | solution.py:45
  10.6 11.3 %collective-permute-start.1 = (f32[72,1280]{1,0:T(8,128)S(1)}, f32[72,1280]{1,0:T(8,128)S(1)}, u32[]{:S(2)}, u32[]{:S(2)}) collective-permute-start(f32[72,1280]{1,0:T(8,128)S(1)} %get-tuple-element.51), channel_id=1, source_target_pairs={{0,2},{1,9},{2,4},{3,11},{4,6},{5,13},{6,0},{7,15},{8,10},{9,17},{... | collective-permute-start | bytes 1105928 | tf_op jit(solution)/shard_map/ppermute | solution.py:45
  11.0 14.9 %collective-permute-start.2 = (f32[72,1280]{1,0:T(8,128)S(1)}, f32[72,1280]{1,0:T(8,128)S(1)}, u32[]{:S(2)}, u32[]{:S(2)}) collective-permute-start(f32[72,1280]{1,0:T(8,128)S(1)} %get-tuple-element.52), channel_id=1, source_target_pairs={{0,4},{1,17},{2,6},{3,19},{4,0},{5,21},{6,2},{7,23},{8,12},{9,25},... | collective-permute-start | bytes 1105928 | tf_op jit(solution)/shard_map/ppermute | solution.py:45
  12.9 13.0 %collective-permute-start.3 = (f32[72,1280]{1,0:T(8,128)S(1)}, f32[72,1280]{1,0:T(8,128)S(1)}, u32[]{:S(2)}, u32[]{:S(2)}) collective-permute-start(f32[72,1280]{1,0:T(8,128)S(1)} %get-tuple-element.53), channel_id=1, source_target_pairs={{0,6},{1,25},{2,0},{3,27},{4,2},{5,29},{6,4},{7,31},{8,14},{9,1},{... | collective-permute-start | bytes 1105928 | tf_op jit(solution)/shard_map/ppermute | solution.py:45
  26.6 22.3 %collective-permute-start.9 = (f32[320,1280]{1,0:T(8,128)S(1)}, f32[320,1280]{1,0:T(8,128)S(1)}, u32[]{:S(2)}, u32[]{:S(2)}) collective-permute-start(f32[320,1280]{1,0:T(8,128)S(1)} %get-tuple-element.61.refs_0_), channel_id=1, source_target_pairs={{0,8},{1,3},{2,10},{3,5},{4,12},{5,7},{6,14},{7,1},{8,16},{9,11},{... | collective-permute-start | bytes 4915208 | tf_op jit(solution)/shard_map/ppermute | solution.py:45
  28.0 21.1 %collective-permute-start.10 = (f32[320,1280]{1,0:T(8,128)S(1)}, f32[320,1280]{1,0:T(8,128)S(1)}, u32[]{:S(2)}, u32[]{:S(2)}) collective-permute-start(f32[320,1280]{1,0:T(8,128)S(1)} %get-tuple-element.61.refs_0_), channel_id=1, source_target_pairs={{0,24},{1,7},{2,26},{3,1},{4,28},{5,3},{6,30},{7,5},{8,0},{9,15},{... | collective-permute-start | bytes 4915208 | tf_op jit(solution)/shard_map/ppermute | solution.py:45
  30.2 29.7 %collective-permute-start.7 = (f32[256,1280]{1,0:T(8,128)S(1)}, f32[256,1280]{1,0:T(8,128)S(1)}, u32[]{:S(2)}, u32[]{:S(2)}) collective-permute-start(f32[256,1280]{1,0:T(8,128)S(1)} %get-tuple-element.73.refs_0_), channel_id=1, source_target_pairs={{0,32},{1,33},{2,34},{3,35},{4,36},{5,37},{6,38},{7,39},{8,40},{9,... | collective-permute-start | bytes 3932168 | tf_op jit(solution)/shard_map/ppermute | solution.py:45
  31.5 28.4 %collective-permute-start.8 = (f32[256,1280]{1,0:T(8,128)S(1)}, f32[256,1280]{1,0:T(8,128)S(1)}, u32[]{:S(2)}, u32[]{:S(2)}) collective-permute-start(f32[256,1280]{1,0:T(8,128)S(1)} %get-tuple-element.73.refs_0_), channel_id=1, source_target_pairs={{0,96},{1,97},{2,98},{3,99},{4,100},{5,101},{6,102},{7,103},{8,104... | collective-permute-start | bytes 3932168 | tf_op jit(solution)/shard_map/ppermute | solution.py:45
  48.9 13.8 %collective-permute-start.12 = (f32[160,1280]{1,0:T(8,128)S(1)}, f32[160,1280]{1,0:T(8,128)S(1)}, u32[]{:S(2)}, u32[]{:S(2)}) collective-permute-start(f32[160,1280]{1,0:T(8,128)S(1)} %slice.40), channel_id=1, source_target_pairs={{0,8},{1,3},{2,10},{3,5},{4,12},{5,7},{6,14},{7,1},{8,16},{9,11},{... | collective-permute-start | bytes 2457608 | tf_op jit(solution)/shard_map/ppermute | solution.py:45
  49.1 13.7 %collective-permute-start.13 = (f32[160,1280]{1,0:T(8,128)S(1)}, f32[160,1280]{1,0:T(8,128)S(1)}, u32[]{:S(2)}, u32[]{:S(2)}) collective-permute-start(f32[160,1280]{1,0:T(8,128)S(1)} %slice.41), channel_id=1, source_target_pairs={{0,24},{1,7},{2,26},{3,1},{4,28},{5,3},{6,30},{7,5},{8,0},{9,15},{... | collective-permute-start | bytes 2457608 | tf_op jit(solution)/shard_map/ppermute | solution.py:45
  59.9 15.7 %collective-permute-start.11 = (f32[128,1280]{1,0:T(8,128)S(1)}, f32[128,1280]{1,0:T(8,128)S(1)}, u32[]{:S(2)}, u32[]{:S(2)}) collective-permute-start(f32[128,1280]{1,0:T(8,128)S(1)} %slice.30), channel_id=1, source_target_pairs={{0,32},{1,33},{2,34},{3,35},{4,36},{5,37},{6,38},{7,39},{8,40},{9,... | collective-permute-start | bytes 1966088 | tf_op jit(solution)/shard_map/ppermute | solution.py:45
  61.0 14.6 %collective-permute-start.14 = (f32[128,1280]{1,0:T(8,128)S(1)}, f32[128,1280]{1,0:T(8,128)S(1)}, u32[]{:S(2)}, u32[]{:S(2)}) collective-permute-start(f32[128,1280]{1,0:T(8,128)S(1)} %slice.33), channel_id=1, source_target_pairs={{0,96},{1,97},{2,98},{3,99},{4,100},{5,101},{6,102},{7,103},{8,104... | collective-permute-start | bytes 1966088 | tf_op jit(solution)/shard_map/ppermute | solution.py:45
  70.2 17.8 %collective-permute-start.15 = (f32[128,1280]{1,0:T(8,128)S(1)}, f32[128,1280]{1,0:T(8,128)S(1)}, u32[]{:S(2)}, u32[]{:S(2)}) collective-permute-start(f32[128,1280]{1,0:T(8,128)S(1)} %get-tuple-element.75), channel_id=1, source_target_pairs={{0,6},{1,25},{2,0},{3,27},{4,2},{5,29},{6,4},{7,31},{8,14},{9,1},{... | collective-permute-start | bytes 1966088 | tf_op jit(solution)/shard_map/ppermute | solution.py:45
  73.5 18.0 %collective-permute-start.16 = (f32[128,1280]{1,0:T(8,128)S(1)}, f32[128,1280]{1,0:T(8,128)S(1)}, u32[]{:S(2)}, u32[]{:S(2)}) collective-permute-start(f32[128,1280]{1,0:T(8,128)S(1)} %get-tuple-element.76), channel_id=1, source_target_pairs={{0,2},{1,9},{2,4},{3,11},{4,6},{5,13},{6,0},{7,15},{8,10},{9,17},{... | collective-permute-start | bytes 1966088 | tf_op jit(solution)/shard_map/ppermute | solution.py:45
  73.5 18.0 %collective-permute-start.17 = (f32[128,1280]{1,0:T(8,128)S(1)}, f32[128,1280]{1,0:T(8,128)S(1)}, u32[]{:S(2)}, u32[]{:S(2)}) collective-permute-start(f32[128,1280]{1,0:T(8,128)S(1)} %get-tuple-element.77), channel_id=1, source_target_pairs={{0,4},{1,17},{2,6},{3,19},{4,0},{5,21},{6,2},{7,23},{8,12},{9,25},... | collective-permute-start | bytes 1966088 | tf_op jit(solution)/shard_map/ppermute | solution.py:45
  79.5 14.9 %collective-permute-start.18 = (f32[64,1280]{1,0:T(8,128)S(1)}, f32[64,1280]{1,0:T(8,128)S(1)}, u32[]{:S(2)}, u32[]{:S(2)}) collective-permute-start(f32[64,1280]{1,0:T(8,128)S(1)} %get-tuple-element.79), channel_id=1, source_target_pairs={{0,6},{1,25},{2,0},{3,27},{4,2},{5,29},{6,4},{7,31},{8,14},{9,1},{... | collective-permute-start | bytes 983048 | tf_op jit(solution)/shard_map/ppermute | solution.py:45
  82.8 15.6 %collective-permute-start.19 = (f32[64,1280]{1,0:T(8,128)S(1)}, f32[64,1280]{1,0:T(8,128)S(1)}, u32[]{:S(2)}, u32[]{:S(2)}) collective-permute-start(f32[64,1280]{1,0:T(8,128)S(1)} %get-tuple-element.80), channel_id=1, source_target_pairs={{0,2},{1,9},{2,4},{3,11},{4,6},{5,13},{6,0},{7,15},{8,10},{9,17},{... | collective-permute-start | bytes 983048 | tf_op jit(solution)/shard_map/ppermute | solution.py:45
  88.0 10.4 %collective-permute-start.20 = (f32[64,1280]{1,0:T(8,128)S(1)}, f32[64,1280]{1,0:T(8,128)S(1)}, u32[]{:S(2)}, u32[]{:S(2)}) collective-permute-start(f32[64,1280]{1,0:T(8,128)S(1)} %get-tuple-element.81), channel_id=1, source_target_pairs={{0,4},{1,17},{2,6},{3,19},{4,0},{5,21},{6,2},{7,23},{8,12},{9,25},... | collective-permute-start | bytes 983048 | tf_op jit(solution)/shard_map/ppermute | solution.py:45
  91.8 8.4 %collective-permute-start.21 = (f32[64,1280]{1,0:T(8,128)S(1)}, f32[64,1280]{1,0:T(8,128)S(1)}, u32[]{:S(2)}, u32[]{:S(2)}) collective-permute-start(f32[64,1280]{1,0:T(8,128)S(1)} %get-tuple-element.91), channel_id=1, source_target_pairs={{0,96},{1,97},{2,98},{3,99},{4,100},{5,101},{6,102},{7,103},{8,104... | collective-permute-start | bytes 983048 | tf_op jit(solution)/shard_map/ppermute | solution.py:45
  94.4 12.9 %collective-permute-start.24 = (f32[64,1280]{1,0:T(8,128)S(1)}, f32[64,1280]{1,0:T(8,128)S(1)}, u32[]{:S(2)}, u32[]{:S(2)}) collective-permute-start(f32[64,1280]{1,0:T(8,128)S(1)} %get-tuple-element.84), channel_id=1, source_target_pairs={{0,6},{1,25},{2,0},{3,27},{4,2},{5,29},{6,4},{7,31},{8,14},{9,1},{... | collective-permute-start | bytes 983048 | tf_op jit(solution)/shard_map/ppermute | solution.py:45
  98.5 10.9 %collective-permute-start.25 = (f32[64,1280]{1,0:T(8,128)S(1)}, f32[64,1280]{1,0:T(8,128)S(1)}, u32[]{:S(2)}, u32[]{:S(2)}) collective-permute-start(f32[64,1280]{1,0:T(8,128)S(1)} %get-tuple-element.86), channel_id=1, source_target_pairs={{0,2},{1,9},{2,4},{3,11},{4,6},{5,13},{6,0},{7,15},{8,10},{9,17},{... | collective-permute-start | bytes 983048 | tf_op jit(solution)/shard_map/ppermute | solution.py:45
  98.5 10.9 %collective-permute-start.26 = (f32[64,1280]{1,0:T(8,128)S(1)}, f32[64,1280]{1,0:T(8,128)S(1)}, u32[]{:S(2)}, u32[]{:S(2)}) collective-permute-start(f32[64,1280]{1,0:T(8,128)S(1)} %get-tuple-element.88), channel_id=1, source_target_pairs={{0,4},{1,17},{2,6},{3,19},{4,0},{5,21},{6,2},{7,23},{8,12},{9,25},... | collective-permute-start | bytes 983048 | tf_op jit(solution)/shard_map/ppermute | solution.py:45
  (9 other events, 71.5 us)

commit v6 on v5

--- a/solution.py
+++ b/solution.py
@@ -189,7 +189,7 @@
             at += count
         return carry
 
-    lax.fori_loop(0, high_ref.shape[0] // tile, body, 0)
+    lax.fori_loop(0, high_ref.shape[0] // tile, body, 0, unroll=True)
 
 
 def product(sources, spans, out_rows, high, low, name):

time: 117 us -> 115 us (0.983)
  Pallas kernels: 22.4 us -> 18.8 us
  waiting for transfers between devices: 44.9 us -> 47.3 us
    pallas_call x3, Pallas kernels: 14.4 us -> 10.8 us  [product(): pl.pallas_call(functools.partial(product_kernel, spans, len(sources)), ou...]
    ppermute x29, waiting for transfers between devices: 44.9 us -> 47.3 us  [send(): return lax.ppermute(value, AXES, route)]
  transfers between devices with their start and end apart: 29 -> 29, of which waited for: 12 -> 13; matrix products, arithmetic and copies ran while one was open for 1% -> 1% of each run, Pallas kernels for 17% -> 14%
where the time goes in v6:
time: 115 us
  waiting for transfers between devices  47.3 us (41%)
  starting transfers between devices  45 us (39%)
  Pallas kernels  18.8 us (16%)
  local copies, waits for them, and re-layouts  3.17 us (3%)
    ppermute x29, waiting for transfers between devices, send(): return lax.ppermute(value, AXES, route)  47.3 us
    ppermute x29, starting transfers between devices, send(): return lax.ppermute(value, AXES, route)  45 us
    pallas_call x3, Pallas kernels, product(): pl.pallas_call(functools.partial(product_kernel, spans, len(sources)), ou...  10.8 us
    pallas_call x2, Pallas kernels, finish(): pl.pallas_call(functools.partial(finish_kernel, turns), out_shape=jax.Sha...  3.01 us
    unnamed x8, local copies, waits for them, and re-layouts  2.76 us
    pallas_call x2, Pallas kernels, place(): pl.pallas_call(functools.partial(place_kernel, sources), out_shape=[jax.S...  2.31 us
  transfers between devices with their start and end apart: 29, of which 13 were waited for; matrix products, arithmetic and copies ran while one was open for 1% of the time, Pallas kernels for 14%

profile of v6, /device:TPU:1, one launch (start us, length us, event | category | flops | bytes accessed | tf_op | source)
XLA Modules:
  0.0 115.2 jit_solution(11154453535322585738)
XLA Ops:
  6.4 2.5 %collective-permute-start.5 = (f32[72,1280]{1,0:T(8,128)S(1)}, f32[72,1280]{1,0:T(8,128)S(1)}, u32[]{:S(2)}, u32[]{:S(2)}) collective-permute-start(f32[72,1280]{1,0:T(8,128)S(1)} %get-tuple-element.56), channel_id=1, source_target_pairs={{0,4},{1,17},{2,6},{3,19},{4,0},{5,21},{6,2},{7,23},{8,12},{9,25},... | collective-permute-start | bytes 1105928 | tf_op jit(solution)/shard_map/ppermute | solution.py:45
  14.3 3.7 %collective-permute-done.5.refs_2_ = f32[72,1280]{1,0:T(8,128)S(1)} collective-permute-done((f32[72,1280]{1,0:T(8,128)S(1)}, f32[72,1280]{1,0:T(8,128)S(1)}, u32[]{:S(2)}, u32[]{:S(2)}) %collective-permute-start.5) | collective-permute-done | bytes 368672 | tf_op jit(solution)/shard_map/ppermute | solution.py:45
  18.7 3.3 %collective-permute-done.1.refs_1_ = f32[72,1280]{1,0:T(8,128)S(1)} collective-permute-done((f32[72,1280]{1,0:T(8,128)S(1)}, f32[72,1280]{1,0:T(8,128)S(1)}, u32[]{:S(2)}, u32[]{:S(2)}) %collective-permute-start.1) | collective-permute-done | bytes 368672 | tf_op jit(solution)/shard_map/ppermute | solution.py:45
  21.9 4.0 %collective-permute-done.2.refs_2_ = f32[72,1280]{1,0:T(8,128)S(1)} collective-permute-done((f32[72,1280]{1,0:T(8,128)S(1)}, f32[72,1280]{1,0:T(8,128)S(1)}, u32[]{:S(2)}, u32[]{:S(2)}) %collective-permute-start.2) | collective-permute-done | bytes 368672 | tf_op jit(solution)/shard_map/ppermute | solution.py:45
  28.0 2.2 %collective-permute-start.10 = (f32[320,1280]{1,0:T(8,128)S(1)}, f32[320,1280]{1,0:T(8,128)S(1)}, u32[]{:S(2)}, u32[]{:S(2)}) collective-permute-start(f32[320,1280]{1,0:T(8,128)S(1)} %get-tuple-element.61.refs_0_), channel_id=1, source_target_pairs={{0,24},{1,7},{2,26},{3,1},{4,28},{5,3},{6,30},{7,5},{8,0},{9,15},{... | collective-permute-start | bytes 4915208 | tf_op jit(solution)/shard_map/ppermute | solution.py:45
  32.9 16.0 %collective-permute-done.9.refs_1_ = f32[320,1280]{1,0:T(8,128)S(1)} collective-permute-done((f32[320,1280]{1,0:T(8,128)S(1)}, f32[320,1280]{1,0:T(8,128)S(1)}, u32[]{:S(2)}, u32[]{:S(2)}) %collective-permute-start.9) | collective-permute-done | bytes 1638432 | tf_op jit(solution)/shard_map/ppermute | solution.py:45
  49.1 2.7 %collective-permute-start.13 = (f32[160,1280]{1,0:T(8,128)S(1)}, f32[160,1280]{1,0:T(8,128)S(1)}, u32[]{:S(2)}, u32[]{:S(2)}) collective-permute-start(f32[160,1280]{1,0:T(8,128)S(1)} %slice.41), channel_id=1, source_target_pairs={{0,24},{1,7},{2,26},{3,1},{4,28},{5,3},{6,30},{7,5},{8,0},{9,15},{... | collective-permute-start | bytes 2457608 | tf_op jit(solution)/shard_map/ppermute | solution.py:45
  53.3 6.5 %collective-permute-done.7.refs_0_ = f32[256,1280]{1,0:T(8,128)S(1)} collective-permute-done((f32[256,1280]{1,0:T(8,128)S(1)}, f32[256,1280]{1,0:T(8,128)S(1)}, u32[]{:S(2)}, u32[]{:S(2)}) %collective-permute-start.7) | collective-permute-done | bytes 1310752 | tf_op jit(solution)/shard_map/ppermute | solution.py:45
  61.0 1.8 %collective-permute-start.14 = (f32[128,1280]{1,0:T(8,128)S(1)}, f32[128,1280]{1,0:T(8,128)S(1)}, u32[]{:S(2)}, u32[]{:S(2)}) collective-permute-start(f32[128,1280]{1,0:T(8,128)S(1)} %slice.33), channel_id=1, source_target_pairs={{0,96},{1,97},{2,98},{3,99},{4,100},{5,101},{6,102},{7,103},{8,104... | collective-permute-start | bytes 1966088 | tf_op jit(solution)/shard_map/ppermute | solution.py:45
  63.6 5.3 %product_near.1 = (f32[128,1280]{1,0:T(8,128)S(1)}, f32[128,1280]{1,0:T(8,128)S(1)}, f32[128,1280]{1,0:T(8,128)S(1)}, f32[128,1280]{1,0:T(8,128)S(1)}) custom-call(f32[256,1280]{1,0:T(8,128)S(1)} %collective-permute-done.7.refs_0_, f32[256,1280]{1,0:T(8,128)S(1)} %collective-permute-done.8.refs_1_, bf16[1280,1280]{1,0:T(8,128)(2,1)S(1)} %get-tuple-element.68.refs_2_.refs_1_, ...), custom_call_target="tpu_custom_call" | custom-call | flops 5033164800 | bytes 11796480 | tf_op jit(solution)/shard_map/product_near/pallas_call | solution.py:198
  68.9 3.3 %collective-permute-start.15 = (f32[128,1280]{1,0:T(8,128)S(1)}, f32[128,1280]{1,0:T(8,128)S(1)}, u32[]{:S(2)}, u32[]{:S(2)}) collective-permute-start(f32[128,1280]{1,0:T(8,128)S(1)} %get-tuple-element.75), channel_id=1, source_target_pairs={{0,6},{1,25},{2,0},{3,27},{4,2},{5,29},{6,4},{7,31},{8,14},{9,1},{... | collective-permute-start | bytes 1966088 | tf_op jit(solution)/shard_map/ppermute | solution.py:45
  72.2 2.1 %collective-permute-start.17 = (f32[128,1280]{1,0:T(8,128)S(1)}, f32[128,1280]{1,0:T(8,128)S(1)}, u32[]{:S(2)}, u32[]{:S(2)}) collective-permute-start(f32[128,1280]{1,0:T(8,128)S(1)} %get-tuple-element.77), channel_id=1, source_target_pairs={{0,4},{1,17},{2,6},{3,19},{4,0},{5,21},{6,2},{7,23},{8,12},{9,25},... | collective-permute-start | bytes 1966088 | tf_op jit(solution)/shard_map/ppermute | solution.py:45
  74.6 2.8 %product_far.1 = (f32[64,1280]{1,0:T(8,128)S(1)}, f32[64,1280]{1,0:T(8,128)S(1)}, f32[64,1280]{1,0:T(8,128)S(1)}, f32[64,1280]{1,0:T(8,128)S(1)}) custom-call(f32[128,1280]{1,0:T(8,128)S(1)} %collective-permute-done.11.refs_0_, f32[128,1280]{1,0:T(8,128)S(1)} %collective-permute-done.14.refs_1_, bf16[1280,1280]{1,0:T(8,128)(2,1)S(1)} %get-tuple-element.68.refs_2_.refs_1_, ...), custom_call_target="tpu_custom_call" | custom-call | flops 2516582400 | bytes 9175040 | tf_op jit(solution)/shard_map/product_far/pallas_call | solution.py:198
  77.4 4.3 %collective-permute-start.18 = (f32[64,1280]{1,0:T(8,128)S(1)}, f32[64,1280]{1,0:T(8,128)S(1)}, u32[]{:S(2)}, u32[]{:S(2)}) collective-permute-start(f32[64,1280]{1,0:T(8,128)S(1)} %get-tuple-element.79), channel_id=1, source_target_pairs={{0,6},{1,25},{2,0},{3,27},{4,2},{5,29},{6,4},{7,31},{8,14},{9,1},{... | collective-permute-start | bytes 983048 | tf_op jit(solution)/shard_map/ppermute | solution.py:45
  81.7 2.8 %product_own.1 = (f32[64,1280]{1,0:T(8,128)S(1)}, f32[64,1280]{1,0:T(8,128)S(1)}, f32[64,1280]{1,0:T(8,128)S(1)}, f32[64,1280]{1,0:T(8,128)S(1)}) custom-call(f32[256,1280]{1,0:T(8,128)S(1)} %get-tuple-element.73.refs_0_, bf16[1280,1280]{1,0:T(8,128)(2,1)S(1)} %get-tuple-element.68.refs_2_.refs_1_, bf16[1280,1280]{1,0:T(8,128)(2,1)S(1)} %get-tuple-element.69.refs_3_.refs_2_), custom_call_target="tpu_custom_call" | custom-call | flops 2516582400 | bytes 9175040 | tf_op jit(solution)/shard_map/product_own/pallas_call | solution.py:198
  84.5 2.3 %collective-permute-done.15 = f32[128,1280]{1,0:T(8,128)S(1)} collective-permute-done((f32[128,1280]{1,0:T(8,128)S(1)}, f32[128,1280]{1,0:T(8,128)S(1)}, u32[]{:S(2)}, u32[]{:S(2)}) %collective-permute-start.15) | collective-permute-done | bytes 655392 | tf_op jit(solution)/shard_map/ppermute | solution.py:45
  86.9 3.3 %collective-permute-done.16 = f32[128,1280]{1,0:T(8,128)S(1)} collective-permute-done((f32[128,1280]{1,0:T(8,128)S(1)}, f32[128,1280]{1,0:T(8,128)S(1)}, u32[]{:S(2)}, u32[]{:S(2)}) %collective-permute-start.16) | collective-permute-done | bytes 655392 | tf_op jit(solution)/shard_map/ppermute | solution.py:45
  90.5 2.7 %collective-permute-start.21 = (f32[64,1280]{1,0:T(8,128)S(1)}, f32[64,1280]{1,0:T(8,128)S(1)}, u32[]{:S(2)}, u32[]{:S(2)}) collective-permute-start(f32[64,1280]{1,0:T(8,128)S(1)} %get-tuple-element.91), channel_id=1, source_target_pairs={{0,96},{1,97},{2,98},{3,99},{4,100},{5,101},{6,102},{7,103},{8,104... | collective-permute-start | bytes 983048 | tf_op jit(solution)/shard_map/ppermute | solution.py:45
  93.7 3.5 %collective-permute-done.19 = f32[64,1280]{1,0:T(8,128)S(1)} collective-permute-done((f32[64,1280]{1,0:T(8,128)S(1)}, f32[64,1280]{1,0:T(8,128)S(1)}, u32[]{:S(2)}, u32[]{:S(2)}) %collective-permute-start.19) | collective-permute-done | bytes 327712 | tf_op jit(solution)/shard_map/ppermute | solution.py:45
  99.0 5.8 %collective-permute-start.23 = (f32[2,32,1280]{2,1,0:T(8,128)S(1)}, f32[2,32,1280]{2,1,0:T(8,128)S(1)}, u32[]{:S(2)}, u32[]{:S(2)}) collective-permute-start(f32[2,32,1280]{2,1,0:T(8,128)S(1)} %pad_maximum_fusion), channel_id=1, source_target_pairs={{0,1},{1,0},{2,3},{3,2},{4,5},{5,4},{6,7},{7,6},{8,9},{9,8},{10,11... | collective-permute-start | bytes 983048 | tf_op jit(solution)/shard_map/ppermute | solution.py:45
  106.0 2.1 %collective-permute-done.25 = f32[64,1280]{1,0:T(8,128)S(1)} collective-permute-done((f32[64,1280]{1,0:T(8,128)S(1)}, f32[64,1280]{1,0:T(8,128)S(1)}, u32[]{:S(2)}, u32[]{:S(2)}) %collective-permute-start.25) | collective-permute-done | bytes 327712 | tf_op jit(solution)/shard_map/ppermute | solution.py:45
  108.3 3.6 %collective-permute-start.28 = (f32[2,32,1280]{2,1,0:T(8,128)S(1)}, f32[2,32,1280]{2,1,0:T(8,128)S(1)}, u32[]{:S(2)}, u32[]{:S(2)}) collective-permute-start(f32[2,32,1280]{2,1,0:T(8,128)S(1)} %pad_maximum_fusion.1), channel_id=1, source_target_pairs={{0,1},{1,0},{2,3},{3,2},{4,5},{5,4},{6,7},{7,6},{8,9},{9,8},{10,11... | collective-permute-start | bytes 983048 | tf_op jit(solution)/shard_map/ppermute | solution.py:45
  112.0 1.5 %finish_near.1.refs_5_ = f32[2,32,5120]{2,1,0:T(8,128)} custom-call(s32[4]{0:T(128)S(1)} %pad_add_fusion.where_ref, f32[64,1280]{1,0:T(8,128)S(1)} %collective-permute-done.21.refs_0_, f32[64,1280]{1,0:T(8,128)S(1)} %collective-permute-done.22.refs_1_, f32[2,32,1280]{2,1,0:T(8,128)S(1)} %collective-permute-done.23.refs_2_, f32[2,32,1]{2,1,0:T(8,128)S(1)} %copy.11.refs_3_, ...), custom_call_target="tpu_custom_call" | custom-call | flops 491520 | bytes 1310720 | tf_op jit(solution)/shard_map/finish_near/pallas_call | solution.py:236
  113.5 1.5 %finish_last.1 = f32[2,32,5120]{2,1,0:T(8,128)} custom-call(s32[4]{0:T(128)S(1)} %pad_add_fusion.where_ref, f32[64,1280]{1,0:T(8,128)S(1)} %add_add_fusion.1.refs_0_, f32[64,1280]{1,0:T(8,128)S(1)} %collective-permute-done.27.refs_1_, f32[2,32,1280]{2,1,0:T(8,128)S(1)} %collective-permute-done.28.refs_2_, ...), custom_call_target="tpu_custom_call", output_to_operand_aliasing={{}: (6, {})} | custom-call | flops 491520 | bytes 1310720 | tf_op jit(solution)/shard_map/finish_last/pallas_call | solution.py:236
  (70 shorter events, 25.4 us)
Async XLA Ops:
  5.1 7.9 %collective-permute-start.4 = (f32[72,1280]{1,0:T(8,128)S(1)}, f32[72,1280]{1,0:T(8,128)S(1)}, u32[]{:S(2)}, u32[]{:S(2)}) collective-permute-start(f32[72,1280]{1,0:T(8,128)S(1)} %get-tuple-element.55), channel_id=1, source_target_pairs={{0,2},{1,9},{2,4},{3,11},{4,6},{5,13},{6,0},{7,15},{8,10},{9,17},{... | collective-permute-start | bytes 1105928 | tf_op jit(solution)/shard_map/ppermute | solution.py:45
  6.4 11.6 %collective-permute-start.5 = (f32[72,1280]{1,0:T(8,128)S(1)}, f32[72,1280]{1,0:T(8,128)S(1)}, u32[]{:S(2)}, u32[]{:S(2)}) collective-permute-start(f32[72,1280]{1,0:T(8,128)S(1)} %get-tuple-element.56), channel_id=1, source_target_pairs={{0,4},{1,17},{2,6},{3,19},{4,0},{5,21},{6,2},{7,23},{8,12},{9,25},... | collective-permute-start | bytes 1105928 | tf_op jit(solution)/shard_map/ppermute | solution.py:45
  8.8 9.2 %collective-permute-start.6 = (f32[72,1280]{1,0:T(8,128)S(1)}, f32[72,1280]{1,0:T(8,128)S(1)}, u32[]{:S(2)}, u32[]{:S(2)}) collective-permute-start(f32[72,1280]{1,0:T(8,128)S(1)} %get-tuple-element.57), channel_id=1, source_target_pairs={{0,6},{1,25},{2,0},{3,27},{4,2},{5,29},{6,4},{7,31},{8,14},{9,1},{... | collective-permute-start | bytes 1105928 | tf_op jit(solution)/shard_map/ppermute | solution.py:45
  10.6 11.3 %collective-permute-start.1 = (f32[72,1280]{1,0:T(8,128)S(1)}, f32[72,1280]{1,0:T(8,128)S(1)}, u32[]{:S(2)}, u32[]{:S(2)}) collective-permute-start(f32[72,1280]{1,0:T(8,128)S(1)} %get-tuple-element.51), channel_id=1, source_target_pairs={{0,2},{1,9},{2,4},{3,11},{4,6},{5,13},{6,0},{7,15},{8,10},{9,17},{... | collective-permute-start | bytes 1105928 | tf_op jit(solution)/shard_map/ppermute | solution.py:45
  11.0 14.9 %collective-permute-start.2 = (f32[72,1280]{1,0:T(8,128)S(1)}, f32[72,1280]{1,0:T(8,128)S(1)}, u32[]{:S(2)}, u32[]{:S(2)}) collective-permute-start(f32[72,1280]{1,0:T(8,128)S(1)} %get-tuple-element.52), channel_id=1, source_target_pairs={{0,4},{1,17},{2,6},{3,19},{4,0},{5,21},{6,2},{7,23},{8,12},{9,25},... | collective-permute-start | bytes 1105928 | tf_op jit(solution)/shard_map/ppermute | solution.py:45
  12.9 13.0 %collective-permute-start.3 = (f32[72,1280]{1,0:T(8,128)S(1)}, f32[72,1280]{1,0:T(8,128)S(1)}, u32[]{:S(2)}, u32[]{:S(2)}) collective-permute-start(f32[72,1280]{1,0:T(8,128)S(1)} %get-tuple-element.53), channel_id=1, source_target_pairs={{0,6},{1,25},{2,0},{3,27},{4,2},{5,29},{6,4},{7,31},{8,14},{9,1},{... | collective-permute-start | bytes 1105928 | tf_op jit(solution)/shard_map/ppermute | solution.py:45
  26.6 22.3 %collective-permute-start.9 = (f32[320,1280]{1,0:T(8,128)S(1)}, f32[320,1280]{1,0:T(8,128)S(1)}, u32[]{:S(2)}, u32[]{:S(2)}) collective-permute-start(f32[320,1280]{1,0:T(8,128)S(1)} %get-tuple-element.61.refs_0_), channel_id=1, source_target_pairs={{0,8},{1,3},{2,10},{3,5},{4,12},{5,7},{6,14},{7,1},{8,16},{9,11},{... | collective-permute-start | bytes 4915208 | tf_op jit(solution)/shard_map/ppermute | solution.py:45
  28.0 21.1 %collective-permute-start.10 = (f32[320,1280]{1,0:T(8,128)S(1)}, f32[320,1280]{1,0:T(8,128)S(1)}, u32[]{:S(2)}, u32[]{:S(2)}) collective-permute-start(f32[320,1280]{1,0:T(8,128)S(1)} %get-tuple-element.61.refs_0_), channel_id=1, source_target_pairs={{0,24},{1,7},{2,26},{3,1},{4,28},{5,3},{6,30},{7,5},{8,0},{9,15},{... | collective-permute-start | bytes 4915208 | tf_op jit(solution)/shard_map/ppermute | solution.py:45
  30.2 29.7 %collective-permute-start.7 = (f32[256,1280]{1,0:T(8,128)S(1)}, f32[256,1280]{1,0:T(8,128)S(1)}, u32[]{:S(2)}, u32[]{:S(2)}) collective-permute-start(f32[256,1280]{1,0:T(8,128)S(1)} %get-tuple-element.73.refs_0_), channel_id=1, source_target_pairs={{0,32},{1,33},{2,34},{3,35},{4,36},{5,37},{6,38},{7,39},{8,40},{9,... | collective-permute-start | bytes 3932168 | tf_op jit(solution)/shard_map/ppermute | solution.py:45
  31.5 28.4 %collective-permute-start.8 = (f32[256,1280]{1,0:T(8,128)S(1)}, f32[256,1280]{1,0:T(8,128)S(1)}, u32[]{:S(2)}, u32[]{:S(2)}) collective-permute-start(f32[256,1280]{1,0:T(8,128)S(1)} %get-tuple-element.73.refs_0_), channel_id=1, source_target_pairs={{0,96},{1,97},{2,98},{3,99},{4,100},{5,101},{6,102},{7,103},{8,104... | collective-permute-start | bytes 3932168 | tf_op jit(solution)/shard_map/ppermute | solution.py:45
  48.9 13.8 %collective-permute-start.12 = (f32[160,1280]{1,0:T(8,128)S(1)}, f32[160,1280]{1,0:T(8,128)S(1)}, u32[]{:S(2)}, u32[]{:S(2)}) collective-permute-start(f32[160,1280]{1,0:T(8,128)S(1)} %slice.40), channel_id=1, source_target_pairs={{0,8},{1,3},{2,10},{3,5},{4,12},{5,7},{6,14},{7,1},{8,16},{9,11},{... | collective-permute-start | bytes 2457608 | tf_op jit(solution)/shard_map/ppermute | solution.py:45
  49.1 13.7 %collective-permute-start.13 = (f32[160,1280]{1,0:T(8,128)S(1)}, f32[160,1280]{1,0:T(8,128)S(1)}, u32[]{:S(2)}, u32[]{:S(2)}) collective-permute-start(f32[160,1280]{1,0:T(8,128)S(1)} %slice.41), channel_id=1, source_target_pairs={{0,24},{1,7},{2,26},{3,1},{4,28},{5,3},{6,30},{7,5},{8,0},{9,15},{... | collective-permute-start | bytes 2457608 | tf_op jit(solution)/shard_map/ppermute | solution.py:45
  59.9 14.7 %collective-permute-start.11 = (f32[128,1280]{1,0:T(8,128)S(1)}, f32[128,1280]{1,0:T(8,128)S(1)}, u32[]{:S(2)}, u32[]{:S(2)}) collective-permute-start(f32[128,1280]{1,0:T(8,128)S(1)} %slice.30), channel_id=1, source_target_pairs={{0,32},{1,33},{2,34},{3,35},{4,36},{5,37},{6,38},{7,39},{8,40},{9,... | collective-permute-start | bytes 1966088 | tf_op jit(solution)/shard_map/ppermute | solution.py:45
  61.0 13.6 %collective-permute-start.14 = (f32[128,1280]{1,0:T(8,128)S(1)}, f32[128,1280]{1,0:T(8,128)S(1)}, u32[]{:S(2)}, u32[]{:S(2)}) collective-permute-start(f32[128,1280]{1,0:T(8,128)S(1)} %slice.33), channel_id=1, source_target_pairs={{0,96},{1,97},{2,98},{3,99},{4,100},{5,101},{6,102},{7,103},{8,104... | collective-permute-start | bytes 1966088 | tf_op jit(solution)/shard_map/ppermute | solution.py:45
  68.9 17.8 %collective-permute-start.15 = (f32[128,1280]{1,0:T(8,128)S(1)}, f32[128,1280]{1,0:T(8,128)S(1)}, u32[]{:S(2)}, u32[]{:S(2)}) collective-permute-start(f32[128,1280]{1,0:T(8,128)S(1)} %get-tuple-element.75), channel_id=1, source_target_pairs={{0,6},{1,25},{2,0},{3,27},{4,2},{5,29},{6,4},{7,31},{8,14},{9,1},{... | collective-permute-start | bytes 1966088 | tf_op jit(solution)/shard_map/ppermute | solution.py:45
  72.2 18.0 %collective-permute-start.16 = (f32[128,1280]{1,0:T(8,128)S(1)}, f32[128,1280]{1,0:T(8,128)S(1)}, u32[]{:S(2)}, u32[]{:S(2)}) collective-permute-start(f32[128,1280]{1,0:T(8,128)S(1)} %get-tuple-element.76), channel_id=1, source_target_pairs={{0,2},{1,9},{2,4},{3,11},{4,6},{5,13},{6,0},{7,15},{8,10},{9,17},{... | collective-permute-start | bytes 1966088 | tf_op jit(solution)/shard_map/ppermute | solution.py:45
  72.2 18.0 %collective-permute-start.17 = (f32[128,1280]{1,0:T(8,128)S(1)}, f32[128,1280]{1,0:T(8,128)S(1)}, u32[]{:S(2)}, u32[]{:S(2)}) collective-permute-start(f32[128,1280]{1,0:T(8,128)S(1)} %get-tuple-element.77), channel_id=1, source_target_pairs={{0,4},{1,17},{2,6},{3,19},{4,0},{5,21},{6,2},{7,23},{8,12},{9,25},... | collective-permute-start | bytes 1966088 | tf_op jit(solution)/shard_map/ppermute | solution.py:45
  77.4 15.7 %collective-permute-start.18 = (f32[64,1280]{1,0:T(8,128)S(1)}, f32[64,1280]{1,0:T(8,128)S(1)}, u32[]{:S(2)}, u32[]{:S(2)}) collective-permute-start(f32[64,1280]{1,0:T(8,128)S(1)} %get-tuple-element.79), channel_id=1, source_target_pairs={{0,6},{1,25},{2,0},{3,27},{4,2},{5,29},{6,4},{7,31},{8,14},{9,1},{... | collective-permute-start | bytes 983048 | tf_op jit(solution)/shard_map/ppermute | solution.py:45
  81.7 15.5 %collective-permute-start.19 = (f32[64,1280]{1,0:T(8,128)S(1)}, f32[64,1280]{1,0:T(8,128)S(1)}, u32[]{:S(2)}, u32[]{:S(2)}) collective-permute-start(f32[64,1280]{1,0:T(8,128)S(1)} %get-tuple-element.80), channel_id=1, source_target_pairs={{0,2},{1,9},{2,4},{3,11},{4,6},{5,13},{6,0},{7,15},{8,10},{9,17},{... | collective-permute-start | bytes 983048 | tf_op jit(solution)/shard_map/ppermute | solution.py:45
  86.8 10.4 %collective-permute-start.20 = (f32[64,1280]{1,0:T(8,128)S(1)}, f32[64,1280]{1,0:T(8,128)S(1)}, u32[]{:S(2)}, u32[]{:S(2)}) collective-permute-start(f32[64,1280]{1,0:T(8,128)S(1)} %get-tuple-element.81), channel_id=1, source_target_pairs={{0,4},{1,17},{2,6},{3,19},{4,0},{5,21},{6,2},{7,23},{8,12},{9,25},... | collective-permute-start | bytes 983048 | tf_op jit(solution)/shard_map/ppermute | solution.py:45
  90.5 8.4 %collective-permute-start.21 = (f32[64,1280]{1,0:T(8,128)S(1)}, f32[64,1280]{1,0:T(8,128)S(1)}, u32[]{:S(2)}, u32[]{:S(2)}) collective-permute-start(f32[64,1280]{1,0:T(8,128)S(1)} %get-tuple-element.91), channel_id=1, source_target_pairs={{0,96},{1,97},{2,98},{3,99},{4,100},{5,101},{6,102},{7,103},{8,104... | collective-permute-start | bytes 983048 | tf_op jit(solution)/shard_map/ppermute | solution.py:45
  93.2 12.9 %collective-permute-start.24 = (f32[64,1280]{1,0:T(8,128)S(1)}, f32[64,1280]{1,0:T(8,128)S(1)}, u32[]{:S(2)}, u32[]{:S(2)}) collective-permute-start(f32[64,1280]{1,0:T(8,128)S(1)} %get-tuple-element.84), channel_id=1, source_target_pairs={{0,6},{1,25},{2,0},{3,27},{4,2},{5,29},{6,4},{7,31},{8,14},{9,1},{... | collective-permute-start | bytes 983048 | tf_op jit(solution)/shard_map/ppermute | solution.py:45
  97.2 10.9 %collective-permute-start.25 = (f32[64,1280]{1,0:T(8,128)S(1)}, f32[64,1280]{1,0:T(8,128)S(1)}, u32[]{:S(2)}, u32[]{:S(2)}) collective-permute-start(f32[64,1280]{1,0:T(8,128)S(1)} %get-tuple-element.86), channel_id=1, source_target_pairs={{0,2},{1,9},{2,4},{3,11},{4,6},{5,13},{6,0},{7,15},{8,10},{9,17},{... | collective-permute-start | bytes 983048 | tf_op jit(solution)/shard_map/ppermute | solution.py:45
  97.2 10.9 %collective-permute-start.26 = (f32[64,1280]{1,0:T(8,128)S(1)}, f32[64,1280]{1,0:T(8,128)S(1)}, u32[]{:S(2)}, u32[]{:S(2)}) collective-permute-start(f32[64,1280]{1,0:T(8,128)S(1)} %get-tuple-element.88), channel_id=1, source_target_pairs={{0,4},{1,17},{2,6},{3,19},{4,0},{5,21},{6,2},{7,23},{8,12},{9,25},... | collective-permute-start | bytes 983048 | tf_op jit(solution)/shard_map/ppermute | solution.py:45
  (9 other events, 71.5 us)

commit v7 on v6

--- a/solution.py
+++ b/solution.py
@@ -145,7 +145,7 @@
             low_ref[pl.ds(pl.multiple_of(row, 16), wide), :] = low
             return carry
 
-        lax.fori_loop(0, count, body, 0)
+        lax.fori_loop(0, count, body, 0, unroll=True)
 
 
 def place(where, blocks, sources, total, into=()):

time: 115 us -> 115 us (level)
  no operation moved by 1% of the time
where the time goes in v7:
time: 115 us
  waiting for transfers between devices  47.3 us (41%)
  starting transfers between devices  45 us (39%)
  Pallas kernels  18.8 us (16%)
  local copies, waits for them, and re-layouts  3.17 us (3%)
    ppermute x29, waiting for transfers between devices, send(): return lax.ppermute(value, AXES, route)  47.3 us
    ppermute x29, starting transfers between devices, send(): return lax.ppermute(value, AXES, route)  45 us
    pallas_call x3, Pallas kernels, product(): pl.pallas_call(functools.partial(product_kernel, spans, len(sources)), ou...  10.8 us
    pallas_call x2, Pallas kernels, finish(): pl.pallas_call(functools.partial(finish_kernel, turns), out_shape=jax.Sha...  3.01 us
    unnamed x8, local copies, waits for them, and re-layouts  2.76 us
  transfers between devices with their start and end apart: 29, of which 13 were waited for; matrix products, arithmetic and copies ran while one was open for 1% of the time, Pallas kernels for 14%

profile of v7, /device:TPU:1, one launch (start us, length us, event | category | flops | bytes accessed | tf_op | source)
XLA Modules:
  0.0 115.2 jit_solution(752005660657949406)
XLA Ops:
  6.4 2.5 %collective-permute-start.5 = (f32[72,1280]{1,0:T(8,128)S(1)}, f32[72,1280]{1,0:T(8,128)S(1)}, u32[]{:S(2)}, u32[]{:S(2)}) collective-permute-start(f32[72,1280]{1,0:T(8,128)S(1)} %get-tuple-element.56), channel_id=1, source_target_pairs={{0,4},{1,17},{2,6},{3,19},{4,0},{5,21},{6,2},{7,23},{8,12},{9,25},... | collective-permute-start | bytes 1105928 | tf_op jit(solution)/shard_map/ppermute | solution.py:45
  14.3 3.7 %collective-permute-done.5.refs_2_ = f32[72,1280]{1,0:T(8,128)S(1)} collective-permute-done((f32[72,1280]{1,0:T(8,128)S(1)}, f32[72,1280]{1,0:T(8,128)S(1)}, u32[]{:S(2)}, u32[]{:S(2)}) %collective-permute-start.5) | collective-permute-done | bytes 368672 | tf_op jit(solution)/shard_map/ppermute | solution.py:45
  18.7 3.3 %collective-permute-done.1.refs_1_ = f32[72,1280]{1,0:T(8,128)S(1)} collective-permute-done((f32[72,1280]{1,0:T(8,128)S(1)}, f32[72,1280]{1,0:T(8,128)S(1)}, u32[]{:S(2)}, u32[]{:S(2)}) %collective-permute-start.1) | collective-permute-done | bytes 368672 | tf_op jit(solution)/shard_map/ppermute | solution.py:45
  21.9 4.0 %collective-permute-done.2.refs_2_ = f32[72,1280]{1,0:T(8,128)S(1)} collective-permute-done((f32[72,1280]{1,0:T(8,128)S(1)}, f32[72,1280]{1,0:T(8,128)S(1)}, u32[]{:S(2)}, u32[]{:S(2)}) %collective-permute-start.2) | collective-permute-done | bytes 368672 | tf_op jit(solution)/shard_map/ppermute | solution.py:45
  28.0 2.2 %collective-permute-start.10 = (f32[320,1280]{1,0:T(8,128)S(1)}, f32[320,1280]{1,0:T(8,128)S(1)}, u32[]{:S(2)}, u32[]{:S(2)}) collective-permute-start(f32[320,1280]{1,0:T(8,128)S(1)} %get-tuple-element.61.refs_0_), channel_id=1, source_target_pairs={{0,24},{1,7},{2,26},{3,1},{4,28},{5,3},{6,30},{7,5},{8,0},{9,15},{... | collective-permute-start | bytes 4915208 | tf_op jit(solution)/shard_map/ppermute | solution.py:45
  32.9 16.0 %collective-permute-done.9.refs_1_ = f32[320,1280]{1,0:T(8,128)S(1)} collective-permute-done((f32[320,1280]{1,0:T(8,128)S(1)}, f32[320,1280]{1,0:T(8,128)S(1)}, u32[]{:S(2)}, u32[]{:S(2)}) %collective-permute-start.9) | collective-permute-done | bytes 1638432 | tf_op jit(solution)/shard_map/ppermute | solution.py:45
  49.1 2.7 %collective-permute-start.13 = (f32[160,1280]{1,0:T(8,128)S(1)}, f32[160,1280]{1,0:T(8,128)S(1)}, u32[]{:S(2)}, u32[]{:S(2)}) collective-permute-start(f32[160,1280]{1,0:T(8,128)S(1)} %slice.41), channel_id=1, source_target_pairs={{0,24},{1,7},{2,26},{3,1},{4,28},{5,3},{6,30},{7,5},{8,0},{9,15},{... | collective-permute-start | bytes 2457608 | tf_op jit(solution)/shard_map/ppermute | solution.py:45
  53.3 6.6 %collective-permute-done.7.refs_0_ = f32[256,1280]{1,0:T(8,128)S(1)} collective-permute-done((f32[256,1280]{1,0:T(8,128)S(1)}, f32[256,1280]{1,0:T(8,128)S(1)}, u32[]{:S(2)}, u32[]{:S(2)}) %collective-permute-start.7) | collective-permute-done | bytes 1310752 | tf_op jit(solution)/shard_map/ppermute | solution.py:45
  61.0 1.8 %collective-permute-start.14 = (f32[128,1280]{1,0:T(8,128)S(1)}, f32[128,1280]{1,0:T(8,128)S(1)}, u32[]{:S(2)}, u32[]{:S(2)}) collective-permute-start(f32[128,1280]{1,0:T(8,128)S(1)} %slice.33), channel_id=1, source_target_pairs={{0,96},{1,97},{2,98},{3,99},{4,100},{5,101},{6,102},{7,103},{8,104... | collective-permute-start | bytes 1966088 | tf_op jit(solution)/shard_map/ppermute | solution.py:45
  63.6 5.3 %product_near.1 = (f32[128,1280]{1,0:T(8,128)S(1)}, f32[128,1280]{1,0:T(8,128)S(1)}, f32[128,1280]{1,0:T(8,128)S(1)}, f32[128,1280]{1,0:T(8,128)S(1)}) custom-call(f32[256,1280]{1,0:T(8,128)S(1)} %collective-permute-done.7.refs_0_, f32[256,1280]{1,0:T(8,128)S(1)} %collective-permute-done.8.refs_1_, bf16[1280,1280]{1,0:T(8,128)(2,1)S(1)} %get-tuple-element.68.refs_2_.refs_1_, ...), custom_call_target="tpu_custom_call" | custom-call | flops 5033164800 | bytes 11796480 | tf_op jit(solution)/shard_map/product_near/pallas_call | solution.py:198
  68.9 3.3 %collective-permute-start.15 = (f32[128,1280]{1,0:T(8,128)S(1)}, f32[128,1280]{1,0:T(8,128)S(1)}, u32[]{:S(2)}, u32[]{:S(2)}) collective-permute-start(f32[128,1280]{1,0:T(8,128)S(1)} %get-tuple-element.75), channel_id=1, source_target_pairs={{0,6},{1,25},{2,0},{3,27},{4,2},{5,29},{6,4},{7,31},{8,14},{9,1},{... | collective-permute-start | bytes 1966088 | tf_op jit(solution)/shard_map/ppermute | solution.py:45
  72.2 2.1 %collective-permute-start.17 = (f32[128,1280]{1,0:T(8,128)S(1)}, f32[128,1280]{1,0:T(8,128)S(1)}, u32[]{:S(2)}, u32[]{:S(2)}) collective-permute-start(f32[128,1280]{1,0:T(8,128)S(1)} %get-tuple-element.77), channel_id=1, source_target_pairs={{0,4},{1,17},{2,6},{3,19},{4,0},{5,21},{6,2},{7,23},{8,12},{9,25},... | collective-permute-start | bytes 1966088 | tf_op jit(solution)/shard_map/ppermute | solution.py:45
  74.6 2.8 %product_far.1 = (f32[64,1280]{1,0:T(8,128)S(1)}, f32[64,1280]{1,0:T(8,128)S(1)}, f32[64,1280]{1,0:T(8,128)S(1)}, f32[64,1280]{1,0:T(8,128)S(1)}) custom-call(f32[128,1280]{1,0:T(8,128)S(1)} %collective-permute-done.11.refs_0_, f32[128,1280]{1,0:T(8,128)S(1)} %collective-permute-done.14.refs_1_, bf16[1280,1280]{1,0:T(8,128)(2,1)S(1)} %get-tuple-element.68.refs_2_.refs_1_, ...), custom_call_target="tpu_custom_call" | custom-call | flops 2516582400 | bytes 9175040 | tf_op jit(solution)/shard_map/product_far/pallas_call | solution.py:198
  77.4 4.3 %collective-permute-start.18 = (f32[64,1280]{1,0:T(8,128)S(1)}, f32[64,1280]{1,0:T(8,128)S(1)}, u32[]{:S(2)}, u32[]{:S(2)}) collective-permute-start(f32[64,1280]{1,0:T(8,128)S(1)} %get-tuple-element.79), channel_id=1, source_target_pairs={{0,6},{1,25},{2,0},{3,27},{4,2},{5,29},{6,4},{7,31},{8,14},{9,1},{... | collective-permute-start | bytes 983048 | tf_op jit(solution)/shard_map/ppermute | solution.py:45
  81.7 2.8 %product_own.1 = (f32[64,1280]{1,0:T(8,128)S(1)}, f32[64,1280]{1,0:T(8,128)S(1)}, f32[64,1280]{1,0:T(8,128)S(1)}, f32[64,1280]{1,0:T(8,128)S(1)}) custom-call(f32[256,1280]{1,0:T(8,128)S(1)} %get-tuple-element.73.refs_0_, bf16[1280,1280]{1,0:T(8,128)(2,1)S(1)} %get-tuple-element.68.refs_2_.refs_1_, bf16[1280,1280]{1,0:T(8,128)(2,1)S(1)} %get-tuple-element.69.refs_3_.refs_2_), custom_call_target="tpu_custom_call" | custom-call | flops 2516582400 | bytes 9175040 | tf_op jit(solution)/shard_map/product_own/pallas_call | solution.py:198
  84.5 2.3 %collective-permute-done.15 = f32[128,1280]{1,0:T(8,128)S(1)} collective-permute-done((f32[128,1280]{1,0:T(8,128)S(1)}, f32[128,1280]{1,0:T(8,128)S(1)}, u32[]{:S(2)}, u32[]{:S(2)}) %collective-permute-start.15) | collective-permute-done | bytes 655392 | tf_op jit(solution)/shard_map/ppermute | solution.py:45
  86.9 3.3 %collective-permute-done.16 = f32[128,1280]{1,0:T(8,128)S(1)} collective-permute-done((f32[128,1280]{1,0:T(8,128)S(1)}, f32[128,1280]{1,0:T(8,128)S(1)}, u32[]{:S(2)}, u32[]{:S(2)}) %collective-permute-start.16) | collective-permute-done | bytes 655392 | tf_op jit(solution)/shard_map/ppermute | solution.py:45
  90.5 2.7 %collective-permute-start.21 = (f32[64,1280]{1,0:T(8,128)S(1)}, f32[64,1280]{1,0:T(8,128)S(1)}, u32[]{:S(2)}, u32[]{:S(2)}) collective-permute-start(f32[64,1280]{1,0:T(8,128)S(1)} %get-tuple-element.91), channel_id=1, source_target_pairs={{0,96},{1,97},{2,98},{3,99},{4,100},{5,101},{6,102},{7,103},{8,104... | collective-permute-start | bytes 983048 | tf_op jit(solution)/shard_map/ppermute | solution.py:45
  93.7 3.5 %collective-permute-done.19 = f32[64,1280]{1,0:T(8,128)S(1)} collective-permute-done((f32[64,1280]{1,0:T(8,128)S(1)}, f32[64,1280]{1,0:T(8,128)S(1)}, u32[]{:S(2)}, u32[]{:S(2)}) %collective-permute-start.19) | collective-permute-done | bytes 327712 | tf_op jit(solution)/shard_map/ppermute | solution.py:45
  99.0 5.8 %collective-permute-start.23 = (f32[2,32,1280]{2,1,0:T(8,128)S(1)}, f32[2,32,1280]{2,1,0:T(8,128)S(1)}, u32[]{:S(2)}, u32[]{:S(2)}) collective-permute-start(f32[2,32,1280]{2,1,0:T(8,128)S(1)} %pad_maximum_fusion), channel_id=1, source_target_pairs={{0,1},{1,0},{2,3},{3,2},{4,5},{5,4},{6,7},{7,6},{8,9},{9,8},{10,11... | collective-permute-start | bytes 983048 | tf_op jit(solution)/shard_map/ppermute | solution.py:45
  106.0 2.1 %collective-permute-done.25 = f32[64,1280]{1,0:T(8,128)S(1)} collective-permute-done((f32[64,1280]{1,0:T(8,128)S(1)}, f32[64,1280]{1,0:T(8,128)S(1)}, u32[]{:S(2)}, u32[]{:S(2)}) %collective-permute-start.25) | collective-permute-done | bytes 327712 | tf_op jit(solution)/shard_map/ppermute | solution.py:45
  108.3 3.6 %collective-permute-start.28 = (f32[2,32,1280]{2,1,0:T(8,128)S(1)}, f32[2,32,1280]{2,1,0:T(8,128)S(1)}, u32[]{:S(2)}, u32[]{:S(2)}) collective-permute-start(f32[2,32,1280]{2,1,0:T(8,128)S(1)} %pad_maximum_fusion.1), channel_id=1, source_target_pairs={{0,1},{1,0},{2,3},{3,2},{4,5},{5,4},{6,7},{7,6},{8,9},{9,8},{10,11... | collective-permute-start | bytes 983048 | tf_op jit(solution)/shard_map/ppermute | solution.py:45
  112.0 1.5 %finish_near.1.refs_5_ = f32[2,32,5120]{2,1,0:T(8,128)} custom-call(s32[4]{0:T(128)S(1)} %pad_add_fusion.where_ref, f32[64,1280]{1,0:T(8,128)S(1)} %collective-permute-done.21.refs_0_, f32[64,1280]{1,0:T(8,128)S(1)} %collective-permute-done.22.refs_1_, f32[2,32,1280]{2,1,0:T(8,128)S(1)} %collective-permute-done.23.refs_2_, f32[2,32,1]{2,1,0:T(8,128)S(1)} %copy.11.refs_3_, ...), custom_call_target="tpu_custom_call" | custom-call | flops 491520 | bytes 1310720 | tf_op jit(solution)/shard_map/finish_near/pallas_call | solution.py:236
  113.5 1.5 %finish_last.1 = f32[2,32,5120]{2,1,0:T(8,128)} custom-call(s32[4]{0:T(128)S(1)} %pad_add_fusion.where_ref, f32[64,1280]{1,0:T(8,128)S(1)} %add_add_fusion.1.refs_0_, f32[64,1280]{1,0:T(8,128)S(1)} %collective-permute-done.27.refs_1_, f32[2,32,1280]{2,1,0:T(8,128)S(1)} %collective-permute-done.28.refs_2_, ...), custom_call_target="tpu_custom_call", output_to_operand_aliasing={{}: (6, {})} | custom-call | flops 491520 | bytes 1310720 | tf_op jit(solution)/shard_map/finish_last/pallas_call | solution.py:236
  (70 shorter events, 25.4 us)
Async XLA Ops:
  5.1 7.9 %collective-permute-start.4 = (f32[72,1280]{1,0:T(8,128)S(1)}, f32[72,1280]{1,0:T(8,128)S(1)}, u32[]{:S(2)}, u32[]{:S(2)}) collective-permute-start(f32[72,1280]{1,0:T(8,128)S(1)} %get-tuple-element.55), channel_id=1, source_target_pairs={{0,2},{1,9},{2,4},{3,11},{4,6},{5,13},{6,0},{7,15},{8,10},{9,17},{... | collective-permute-start | bytes 1105928 | tf_op jit(solution)/shard_map/ppermute | solution.py:45
  6.4 11.6 %collective-permute-start.5 = (f32[72,1280]{1,0:T(8,128)S(1)}, f32[72,1280]{1,0:T(8,128)S(1)}, u32[]{:S(2)}, u32[]{:S(2)}) collective-permute-start(f32[72,1280]{1,0:T(8,128)S(1)} %get-tuple-element.56), channel_id=1, source_target_pairs={{0,4},{1,17},{2,6},{3,19},{4,0},{5,21},{6,2},{7,23},{8,12},{9,25},... | collective-permute-start | bytes 1105928 | tf_op jit(solution)/shard_map/ppermute | solution.py:45
  8.8 9.2 %collective-permute-start.6 = (f32[72,1280]{1,0:T(8,128)S(1)}, f32[72,1280]{1,0:T(8,128)S(1)}, u32[]{:S(2)}, u32[]{:S(2)}) collective-permute-start(f32[72,1280]{1,0:T(8,128)S(1)} %get-tuple-element.57), channel_id=1, source_target_pairs={{0,6},{1,25},{2,0},{3,27},{4,2},{5,29},{6,4},{7,31},{8,14},{9,1},{... | collective-permute-start | bytes 1105928 | tf_op jit(solution)/shard_map/ppermute | solution.py:45
  10.6 11.3 %collective-permute-start.1 = (f32[72,1280]{1,0:T(8,128)S(1)}, f32[72,1280]{1,0:T(8,128)S(1)}, u32[]{:S(2)}, u32[]{:S(2)}) collective-permute-start(f32[72,1280]{1,0:T(8,128)S(1)} %get-tuple-element.51), channel_id=1, source_target_pairs={{0,2},{1,9},{2,4},{3,11},{4,6},{5,13},{6,0},{7,15},{8,10},{9,17},{... | collective-permute-start | bytes 1105928 | tf_op jit(solution)/shard_map/ppermute | solution.py:45
  11.0 14.9 %collective-permute-start.2 = (f32[72,1280]{1,0:T(8,128)S(1)}, f32[72,1280]{1,0:T(8,128)S(1)}, u32[]{:S(2)}, u32[]{:S(2)}) collective-permute-start(f32[72,1280]{1,0:T(8,128)S(1)} %get-tuple-element.52), channel_id=1, source_target_pairs={{0,4},{1,17},{2,6},{3,19},{4,0},{5,21},{6,2},{7,23},{8,12},{9,25},... | collective-permute-start | bytes 1105928 | tf_op jit(solution)/shard_map/ppermute | solution.py:45
  12.9 13.0 %collective-permute-start.3 = (f32[72,1280]{1,0:T(8,128)S(1)}, f32[72,1280]{1,0:T(8,128)S(1)}, u32[]{:S(2)}, u32[]{:S(2)}) collective-permute-start(f32[72,1280]{1,0:T(8,128)S(1)} %get-tuple-element.53), channel_id=1, source_target_pairs={{0,6},{1,25},{2,0},{3,27},{4,2},{5,29},{6,4},{7,31},{8,14},{9,1},{... | collective-permute-start | bytes 1105928 | tf_op jit(solution)/shard_map/ppermute | solution.py:45
  26.6 22.3 %collective-permute-start.9 = (f32[320,1280]{1,0:T(8,128)S(1)}, f32[320,1280]{1,0:T(8,128)S(1)}, u32[]{:S(2)}, u32[]{:S(2)}) collective-permute-start(f32[320,1280]{1,0:T(8,128)S(1)} %get-tuple-element.61.refs_0_), channel_id=1, source_target_pairs={{0,8},{1,3},{2,10},{3,5},{4,12},{5,7},{6,14},{7,1},{8,16},{9,11},{... | collective-permute-start | bytes 4915208 | tf_op jit(solution)/shard_map/ppermute | solution.py:45
  28.0 21.1 %collective-permute-start.10 = (f32[320,1280]{1,0:T(8,128)S(1)}, f32[320,1280]{1,0:T(8,128)S(1)}, u32[]{:S(2)}, u32[]{:S(2)}) collective-permute-start(f32[320,1280]{1,0:T(8,128)S(1)} %get-tuple-element.61.refs_0_), channel_id=1, source_target_pairs={{0,24},{1,7},{2,26},{3,1},{4,28},{5,3},{6,30},{7,5},{8,0},{9,15},{... | collective-permute-start | bytes 4915208 | tf_op jit(solution)/shard_map/ppermute | solution.py:45
  30.2 29.7 %collective-permute-start.7 = (f32[256,1280]{1,0:T(8,128)S(1)}, f32[256,1280]{1,0:T(8,128)S(1)}, u32[]{:S(2)}, u32[]{:S(2)}) collective-permute-start(f32[256,1280]{1,0:T(8,128)S(1)} %get-tuple-element.73.refs_0_), channel_id=1, source_target_pairs={{0,32},{1,33},{2,34},{3,35},{4,36},{5,37},{6,38},{7,39},{8,40},{9,... | collective-permute-start | bytes 3932168 | tf_op jit(solution)/shard_map/ppermute | solution.py:45
  31.5 28.4 %collective-permute-start.8 = (f32[256,1280]{1,0:T(8,128)S(1)}, f32[256,1280]{1,0:T(8,128)S(1)}, u32[]{:S(2)}, u32[]{:S(2)}) collective-permute-start(f32[256,1280]{1,0:T(8,128)S(1)} %get-tuple-element.73.refs_0_), channel_id=1, source_target_pairs={{0,96},{1,97},{2,98},{3,99},{4,100},{5,101},{6,102},{7,103},{8,104... | collective-permute-start | bytes 3932168 | tf_op jit(solution)/shard_map/ppermute | solution.py:45
  48.9 13.8 %collective-permute-start.12 = (f32[160,1280]{1,0:T(8,128)S(1)}, f32[160,1280]{1,0:T(8,128)S(1)}, u32[]{:S(2)}, u32[]{:S(2)}) collective-permute-start(f32[160,1280]{1,0:T(8,128)S(1)} %slice.40), channel_id=1, source_target_pairs={{0,8},{1,3},{2,10},{3,5},{4,12},{5,7},{6,14},{7,1},{8,16},{9,11},{... | collective-permute-start | bytes 2457608 | tf_op jit(solution)/shard_map/ppermute | solution.py:45
  49.1 13.7 %collective-permute-start.13 = (f32[160,1280]{1,0:T(8,128)S(1)}, f32[160,1280]{1,0:T(8,128)S(1)}, u32[]{:S(2)}, u32[]{:S(2)}) collective-permute-start(f32[160,1280]{1,0:T(8,128)S(1)} %slice.41), channel_id=1, source_target_pairs={{0,24},{1,7},{2,26},{3,1},{4,28},{5,3},{6,30},{7,5},{8,0},{9,15},{... | collective-permute-start | bytes 2457608 | tf_op jit(solution)/shard_map/ppermute | solution.py:45
  59.9 14.7 %collective-permute-start.11 = (f32[128,1280]{1,0:T(8,128)S(1)}, f32[128,1280]{1,0:T(8,128)S(1)}, u32[]{:S(2)}, u32[]{:S(2)}) collective-permute-start(f32[128,1280]{1,0:T(8,128)S(1)} %slice.30), channel_id=1, source_target_pairs={{0,32},{1,33},{2,34},{3,35},{4,36},{5,37},{6,38},{7,39},{8,40},{9,... | collective-permute-start | bytes 1966088 | tf_op jit(solution)/shard_map/ppermute | solution.py:45
  61.0 13.6 %collective-permute-start.14 = (f32[128,1280]{1,0:T(8,128)S(1)}, f32[128,1280]{1,0:T(8,128)S(1)}, u32[]{:S(2)}, u32[]{:S(2)}) collective-permute-start(f32[128,1280]{1,0:T(8,128)S(1)} %slice.33), channel_id=1, source_target_pairs={{0,96},{1,97},{2,98},{3,99},{4,100},{5,101},{6,102},{7,103},{8,104... | collective-permute-start | bytes 1966088 | tf_op jit(solution)/shard_map/ppermute | solution.py:45
  68.9 17.8 %collective-permute-start.15 = (f32[128,1280]{1,0:T(8,128)S(1)}, f32[128,1280]{1,0:T(8,128)S(1)}, u32[]{:S(2)}, u32[]{:S(2)}) collective-permute-start(f32[128,1280]{1,0:T(8,128)S(1)} %get-tuple-element.75), channel_id=1, source_target_pairs={{0,6},{1,25},{2,0},{3,27},{4,2},{5,29},{6,4},{7,31},{8,14},{9,1},{... | collective-permute-start | bytes 1966088 | tf_op jit(solution)/shard_map/ppermute | solution.py:45
  72.2 18.0 %collective-permute-start.16 = (f32[128,1280]{1,0:T(8,128)S(1)}, f32[128,1280]{1,0:T(8,128)S(1)}, u32[]{:S(2)}, u32[]{:S(2)}) collective-permute-start(f32[128,1280]{1,0:T(8,128)S(1)} %get-tuple-element.76), channel_id=1, source_target_pairs={{0,2},{1,9},{2,4},{3,11},{4,6},{5,13},{6,0},{7,15},{8,10},{9,17},{... | collective-permute-start | bytes 1966088 | tf_op jit(solution)/shard_map/ppermute | solution.py:45
  72.2 18.0 %collective-permute-start.17 = (f32[128,1280]{1,0:T(8,128)S(1)}, f32[128,1280]{1,0:T(8,128)S(1)}, u32[]{:S(2)}, u32[]{:S(2)}) collective-permute-start(f32[128,1280]{1,0:T(8,128)S(1)} %get-tuple-element.77), channel_id=1, source_target_pairs={{0,4},{1,17},{2,6},{3,19},{4,0},{5,21},{6,2},{7,23},{8,12},{9,25},... | collective-permute-start | bytes 1966088 | tf_op jit(solution)/shard_map/ppermute | solution.py:45
  77.4 15.7 %collective-permute-start.18 = (f32[64,1280]{1,0:T(8,128)S(1)}, f32[64,1280]{1,0:T(8,128)S(1)}, u32[]{:S(2)}, u32[]{:S(2)}) collective-permute-start(f32[64,1280]{1,0:T(8,128)S(1)} %get-tuple-element.79), channel_id=1, source_target_pairs={{0,6},{1,25},{2,0},{3,27},{4,2},{5,29},{6,4},{7,31},{8,14},{9,1},{... | collective-permute-start | bytes 983048 | tf_op jit(solution)/shard_map/ppermute | solution.py:45
  81.7 15.5 %collective-permute-start.19 = (f32[64,1280]{1,0:T(8,128)S(1)}, f32[64,1280]{1,0:T(8,128)S(1)}, u32[]{:S(2)}, u32[]{:S(2)}) collective-permute-start(f32[64,1280]{1,0:T(8,128)S(1)} %get-tuple-element.80), channel_id=1, source_target_pairs={{0,2},{1,9},{2,4},{3,11},{4,6},{5,13},{6,0},{7,15},{8,10},{9,17},{... | collective-permute-start | bytes 983048 | tf_op jit(solution)/shard_map/ppermute | solution.py:45
  86.8 10.4 %collective-permute-start.20 = (f32[64,1280]{1,0:T(8,128)S(1)}, f32[64,1280]{1,0:T(8,128)S(1)}, u32[]{:S(2)}, u32[]{:S(2)}) collective-permute-start(f32[64,1280]{1,0:T(8,128)S(1)} %get-tuple-element.81), channel_id=1, source_target_pairs={{0,4},{1,17},{2,6},{3,19},{4,0},{5,21},{6,2},{7,23},{8,12},{9,25},... | collective-permute-start | bytes 983048 | tf_op jit(solution)/shard_map/ppermute | solution.py:45
  90.5 8.4 %collective-permute-start.21 = (f32[64,1280]{1,0:T(8,128)S(1)}, f32[64,1280]{1,0:T(8,128)S(1)}, u32[]{:S(2)}, u32[]{:S(2)}) collective-permute-start(f32[64,1280]{1,0:T(8,128)S(1)} %get-tuple-element.91), channel_id=1, source_target_pairs={{0,96},{1,97},{2,98},{3,99},{4,100},{5,101},{6,102},{7,103},{8,104... | collective-permute-start | bytes 983048 | tf_op jit(solution)/shard_map/ppermute | solution.py:45
  93.2 12.9 %collective-permute-start.24 = (f32[64,1280]{1,0:T(8,128)S(1)}, f32[64,1280]{1,0:T(8,128)S(1)}, u32[]{:S(2)}, u32[]{:S(2)}) collective-permute-start(f32[64,1280]{1,0:T(8,128)S(1)} %get-tuple-element.84), channel_id=1, source_target_pairs={{0,6},{1,25},{2,0},{3,27},{4,2},{5,29},{6,4},{7,31},{8,14},{9,1},{... | collective-permute-start | bytes 983048 | tf_op jit(solution)/shard_map/ppermute | solution.py:45
  97.2 10.9 %collective-permute-start.25 = (f32[64,1280]{1,0:T(8,128)S(1)}, f32[64,1280]{1,0:T(8,128)S(1)}, u32[]{:S(2)}, u32[]{:S(2)}) collective-permute-start(f32[64,1280]{1,0:T(8,128)S(1)} %get-tuple-element.86), channel_id=1, source_target_pairs={{0,2},{1,9},{2,4},{3,11},{4,6},{5,13},{6,0},{7,15},{8,10},{9,17},{... | collective-permute-start | bytes 983048 | tf_op jit(solution)/shard_map/ppermute | solution.py:45
  97.2 10.9 %collective-permute-start.26 = (f32[64,1280]{1,0:T(8,128)S(1)}, f32[64,1280]{1,0:T(8,128)S(1)}, u32[]{:S(2)}, u32[]{:S(2)}) collective-permute-start(f32[64,1280]{1,0:T(8,128)S(1)} %get-tuple-element.88), channel_id=1, source_target_pairs={{0,4},{1,17},{2,6},{3,19},{4,0},{5,21},{6,2},{7,23},{8,12},{9,25},... | collective-permute-start | bytes 983048 | tf_op jit(solution)/shard_map/ppermute | solution.py:45
  (9 other events, 71.5 us)

commit v8 on v7

--- a/solution.py
+++ b/solution.py
@@ -38,7 +38,7 @@
 OTHER_CORE = routes(lambda y, x, z, c: (y, x, z, c + 1))
 VMEM_SPEC = pl.BlockSpec(memory_space=pltpu.VMEM)
 SMEM_SPEC = pl.BlockSpec(memory_space=pltpu.SMEM)
-GRANT = pltpu.CompilerParams(vmem_limit_bytes=20 * 2**20)
+GRANT = pltpu.CompilerParams(vmem_limit_bytes=14 * 2**20)
 
 
 def send(value, route):

time: 115 us -> 115 us (level)
  no operation moved by 1% of the time
where the time goes in v8:
time: 115 us
  waiting for transfers between devices  47.3 us (41%)
  starting transfers between devices  45 us (39%)
  Pallas kernels  18.8 us (16%)
  local copies, waits for them, and re-layouts  3.17 us (3%)
    ppermute x29, waiting for transfers between devices, send(): return lax.ppermute(value, AXES, route)  47.3 us
    ppermute x29, starting transfers between devices, send(): return lax.ppermute(value, AXES, route)  45 us
    pallas_call x3, Pallas kernels, product(): pl.pallas_call(functools.partial(product_kernel, spans, len(sources)), ou...  10.8 us
    pallas_call x2, Pallas kernels, finish(): pl.pallas_call(functools.partial(finish_kernel, turns), out_shape=jax.Sha...  3.01 us
    unnamed x8, local copies, waits for them, and re-layouts  2.76 us
  transfers between devices with their start and end apart: 29, of which 13 were waited for; matrix products, arithmetic and copies ran while one was open for 1% of the time, Pallas kernels for 14%

profile of v8, /device:TPU:1, one launch (start us, length us, event | category | flops | bytes accessed | tf_op | source)
XLA Modules:
  0.0 115.2 jit_solution(6574147664824998130)
XLA Ops:
  6.4 2.5 %collective-permute-start.5 = (f32[72,1280]{1,0:T(8,128)S(1)}, f32[72,1280]{1,0:T(8,128)S(1)}, u32[]{:S(2)}, u32[]{:S(2)}) collective-permute-start(f32[72,1280]{1,0:T(8,128)S(1)} %get-tuple-element.56), channel_id=1, source_target_pairs={{0,4},{1,17},{2,6},{3,19},{4,0},{5,21},{6,2},{7,23},{8,12},{9,25},... | collective-permute-start | bytes 1105928 | tf_op jit(solution)/shard_map/ppermute | solution.py:45
  14.3 3.7 %collective-permute-done.5.refs_2_ = f32[72,1280]{1,0:T(8,128)S(1)} collective-permute-done((f32[72,1280]{1,0:T(8,128)S(1)}, f32[72,1280]{1,0:T(8,128)S(1)}, u32[]{:S(2)}, u32[]{:S(2)}) %collective-permute-start.5) | collective-permute-done | bytes 368672 | tf_op jit(solution)/shard_map/ppermute | solution.py:45
  18.7 3.3 %collective-permute-done.1.refs_1_ = f32[72,1280]{1,0:T(8,128)S(1)} collective-permute-done((f32[72,1280]{1,0:T(8,128)S(1)}, f32[72,1280]{1,0:T(8,128)S(1)}, u32[]{:S(2)}, u32[]{:S(2)}) %collective-permute-start.1) | collective-permute-done | bytes 368672 | tf_op jit(solution)/shard_map/ppermute | solution.py:45
  21.9 4.0 %collective-permute-done.2.refs_2_ = f32[72,1280]{1,0:T(8,128)S(1)} collective-permute-done((f32[72,1280]{1,0:T(8,128)S(1)}, f32[72,1280]{1,0:T(8,128)S(1)}, u32[]{:S(2)}, u32[]{:S(2)}) %collective-permute-start.2) | collective-permute-done | bytes 368672 | tf_op jit(solution)/shard_map/ppermute | solution.py:45
  28.0 2.2 %collective-permute-start.10 = (f32[320,1280]{1,0:T(8,128)S(1)}, f32[320,1280]{1,0:T(8,128)S(1)}, u32[]{:S(2)}, u32[]{:S(2)}) collective-permute-start(f32[320,1280]{1,0:T(8,128)S(1)} %get-tuple-element.61.refs_0_), channel_id=1, source_target_pairs={{0,24},{1,7},{2,26},{3,1},{4,28},{5,3},{6,30},{7,5},{8,0},{9,15},{... | collective-permute-start | bytes 4915208 | tf_op jit(solution)/shard_map/ppermute | solution.py:45
  32.9 16.0 %collective-permute-done.9.refs_1_ = f32[320,1280]{1,0:T(8,128)S(1)} collective-permute-done((f32[320,1280]{1,0:T(8,128)S(1)}, f32[320,1280]{1,0:T(8,128)S(1)}, u32[]{:S(2)}, u32[]{:S(2)}) %collective-permute-start.9) | collective-permute-done | bytes 1638432 | tf_op jit(solution)/shard_map/ppermute | solution.py:45
  49.1 2.7 %collective-permute-start.13 = (f32[160,1280]{1,0:T(8,128)S(1)}, f32[160,1280]{1,0:T(8,128)S(1)}, u32[]{:S(2)}, u32[]{:S(2)}) collective-permute-start(f32[160,1280]{1,0:T(8,128)S(1)} %slice.41), channel_id=1, source_target_pairs={{0,24},{1,7},{2,26},{3,1},{4,28},{5,3},{6,30},{7,5},{8,0},{9,15},{... | collective-permute-start | bytes 2457608 | tf_op jit(solution)/shard_map/ppermute | solution.py:45
  53.3 6.6 %collective-permute-done.7.refs_0_ = f32[256,1280]{1,0:T(8,128)S(1)} collective-permute-done((f32[256,1280]{1,0:T(8,128)S(1)}, f32[256,1280]{1,0:T(8,128)S(1)}, u32[]{:S(2)}, u32[]{:S(2)}) %collective-permute-start.7) | collective-permute-done | bytes 1310752 | tf_op jit(solution)/shard_map/ppermute | solution.py:45
  61.0 1.8 %collective-permute-start.14 = (f32[128,1280]{1,0:T(8,128)S(1)}, f32[128,1280]{1,0:T(8,128)S(1)}, u32[]{:S(2)}, u32[]{:S(2)}) collective-permute-start(f32[128,1280]{1,0:T(8,128)S(1)} %slice.33), channel_id=1, source_target_pairs={{0,96},{1,97},{2,98},{3,99},{4,100},{5,101},{6,102},{7,103},{8,104... | collective-permute-start | bytes 1966088 | tf_op jit(solution)/shard_map/ppermute | solution.py:45
  63.6 5.3 %product_near.1 = (f32[128,1280]{1,0:T(8,128)S(1)}, f32[128,1280]{1,0:T(8,128)S(1)}, f32[128,1280]{1,0:T(8,128)S(1)}, f32[128,1280]{1,0:T(8,128)S(1)}) custom-call(f32[256,1280]{1,0:T(8,128)S(1)} %collective-permute-done.7.refs_0_, f32[256,1280]{1,0:T(8,128)S(1)} %collective-permute-done.8.refs_1_, bf16[1280,1280]{1,0:T(8,128)(2,1)S(1)} %get-tuple-element.68.refs_2_.refs_1_, ...), custom_call_target="tpu_custom_call" | custom-call | flops 5033164800 | bytes 11796480 | tf_op jit(solution)/shard_map/product_near/pallas_call | solution.py:198
  68.9 3.3 %collective-permute-start.15 = (f32[128,1280]{1,0:T(8,128)S(1)}, f32[128,1280]{1,0:T(8,128)S(1)}, u32[]{:S(2)}, u32[]{:S(2)}) collective-permute-start(f32[128,1280]{1,0:T(8,128)S(1)} %get-tuple-element.75), channel_id=1, source_target_pairs={{0,6},{1,25},{2,0},{3,27},{4,2},{5,29},{6,4},{7,31},{8,14},{9,1},{... | collective-permute-start | bytes 1966088 | tf_op jit(solution)/shard_map/ppermute | solution.py:45
  72.2 2.1 %collective-permute-start.17 = (f32[128,1280]{1,0:T(8,128)S(1)}, f32[128,1280]{1,0:T(8,128)S(1)}, u32[]{:S(2)}, u32[]{:S(2)}) collective-permute-start(f32[128,1280]{1,0:T(8,128)S(1)} %get-tuple-element.77), channel_id=1, source_target_pairs={{0,4},{1,17},{2,6},{3,19},{4,0},{5,21},{6,2},{7,23},{8,12},{9,25},... | collective-permute-start | bytes 1966088 | tf_op jit(solution)/shard_map/ppermute | solution.py:45
  74.6 2.8 %product_far.1 = (f32[64,1280]{1,0:T(8,128)S(1)}, f32[64,1280]{1,0:T(8,128)S(1)}, f32[64,1280]{1,0:T(8,128)S(1)}, f32[64,1280]{1,0:T(8,128)S(1)}) custom-call(f32[128,1280]{1,0:T(8,128)S(1)} %collective-permute-done.11.refs_0_, f32[128,1280]{1,0:T(8,128)S(1)} %collective-permute-done.14.refs_1_, bf16[1280,1280]{1,0:T(8,128)(2,1)S(1)} %get-tuple-element.68.refs_2_.refs_1_, ...), custom_call_target="tpu_custom_call" | custom-call | flops 2516582400 | bytes 9175040 | tf_op jit(solution)/shard_map/product_far/pallas_call | solution.py:198
  77.4 4.3 %collective-permute-start.18 = (f32[64,1280]{1,0:T(8,128)S(1)}, f32[64,1280]{1,0:T(8,128)S(1)}, u32[]{:S(2)}, u32[]{:S(2)}) collective-permute-start(f32[64,1280]{1,0:T(8,128)S(1)} %get-tuple-element.79), channel_id=1, source_target_pairs={{0,6},{1,25},{2,0},{3,27},{4,2},{5,29},{6,4},{7,31},{8,14},{9,1},{... | collective-permute-start | bytes 983048 | tf_op jit(solution)/shard_map/ppermute | solution.py:45
  81.7 2.8 %product_own.1 = (f32[64,1280]{1,0:T(8,128)S(1)}, f32[64,1280]{1,0:T(8,128)S(1)}, f32[64,1280]{1,0:T(8,128)S(1)}, f32[64,1280]{1,0:T(8,128)S(1)}) custom-call(f32[256,1280]{1,0:T(8,128)S(1)} %get-tuple-element.73.refs_0_, bf16[1280,1280]{1,0:T(8,128)(2,1)S(1)} %get-tuple-element.68.refs_2_.refs_1_, bf16[1280,1280]{1,0:T(8,128)(2,1)S(1)} %get-tuple-element.69.refs_3_.refs_2_), custom_call_target="tpu_custom_call" | custom-call | flops 2516582400 | bytes 9175040 | tf_op jit(solution)/shard_map/product_own/pallas_call | solution.py:198
  84.5 2.3 %collective-permute-done.15 = f32[128,1280]{1,0:T(8,128)S(1)} collective-permute-done((f32[128,1280]{1,0:T(8,128)S(1)}, f32[128,1280]{1,0:T(8,128)S(1)}, u32[]{:S(2)}, u32[]{:S(2)}) %collective-permute-start.15) | collective-permute-done | bytes 655392 | tf_op jit(solution)/shard_map/ppermute | solution.py:45
  86.9 3.3 %collective-permute-done.16 = f32[128,1280]{1,0:T(8,128)S(1)} collective-permute-done((f32[128,1280]{1,0:T(8,128)S(1)}, f32[128,1280]{1,0:T(8,128)S(1)}, u32[]{:S(2)}, u32[]{:S(2)}) %collective-permute-start.16) | collective-permute-done | bytes 655392 | tf_op jit(solution)/shard_map/ppermute | solution.py:45
  90.5 2.7 %collective-permute-start.21 = (f32[64,1280]{1,0:T(8,128)S(1)}, f32[64,1280]{1,0:T(8,128)S(1)}, u32[]{:S(2)}, u32[]{:S(2)}) collective-permute-start(f32[64,1280]{1,0:T(8,128)S(1)} %get-tuple-element.91), channel_id=1, source_target_pairs={{0,96},{1,97},{2,98},{3,99},{4,100},{5,101},{6,102},{7,103},{8,104... | collective-permute-start | bytes 983048 | tf_op jit(solution)/shard_map/ppermute | solution.py:45
  93.7 3.5 %collective-permute-done.19 = f32[64,1280]{1,0:T(8,128)S(1)} collective-permute-done((f32[64,1280]{1,0:T(8,128)S(1)}, f32[64,1280]{1,0:T(8,128)S(1)}, u32[]{:S(2)}, u32[]{:S(2)}) %collective-permute-start.19) | collective-permute-done | bytes 327712 | tf_op jit(solution)/shard_map/ppermute | solution.py:45
  99.0 5.8 %collective-permute-start.23 = (f32[2,32,1280]{2,1,0:T(8,128)S(1)}, f32[2,32,1280]{2,1,0:T(8,128)S(1)}, u32[]{:S(2)}, u32[]{:S(2)}) collective-permute-start(f32[2,32,1280]{2,1,0:T(8,128)S(1)} %pad_maximum_fusion), channel_id=1, source_target_pairs={{0,1},{1,0},{2,3},{3,2},{4,5},{5,4},{6,7},{7,6},{8,9},{9,8},{10,11... | collective-permute-start | bytes 983048 | tf_op jit(solution)/shard_map/ppermute | solution.py:45
  106.0 2.1 %collective-permute-done.25 = f32[64,1280]{1,0:T(8,128)S(1)} collective-permute-done((f32[64,1280]{1,0:T(8,128)S(1)}, f32[64,1280]{1,0:T(8,128)S(1)}, u32[]{:S(2)}, u32[]{:S(2)}) %collective-permute-start.25) | collective-permute-done | bytes 327712 | tf_op jit(solution)/shard_map/ppermute | solution.py:45
  108.3 3.6 %collective-permute-start.28 = (f32[2,32,1280]{2,1,0:T(8,128)S(1)}, f32[2,32,1280]{2,1,0:T(8,128)S(1)}, u32[]{:S(2)}, u32[]{:S(2)}) collective-permute-start(f32[2,32,1280]{2,1,0:T(8,128)S(1)} %pad_maximum_fusion.1), channel_id=1, source_target_pairs={{0,1},{1,0},{2,3},{3,2},{4,5},{5,4},{6,7},{7,6},{8,9},{9,8},{10,11... | collective-permute-start | bytes 983048 | tf_op jit(solution)/shard_map/ppermute | solution.py:45
  112.0 1.5 %finish_near.1.refs_5_ = f32[2,32,5120]{2,1,0:T(8,128)} custom-call(s32[4]{0:T(128)S(1)} %pad_add_fusion.where_ref, f32[64,1280]{1,0:T(8,128)S(1)} %collective-permute-done.21.refs_0_, f32[64,1280]{1,0:T(8,128)S(1)} %collective-permute-done.22.refs_1_, f32[2,32,1280]{2,1,0:T(8,128)S(1)} %collective-permute-done.23.refs_2_, f32[2,32,1]{2,1,0:T(8,128)S(1)} %copy.11.refs_3_, ...), custom_call_target="tpu_custom_call" | custom-call | flops 491520 | bytes 1310720 | tf_op jit(solution)/shard_map/finish_near/pallas_call | solution.py:236
  113.5 1.5 %finish_last.1 = f32[2,32,5120]{2,1,0:T(8,128)} custom-call(s32[4]{0:T(128)S(1)} %pad_add_fusion.where_ref, f32[64,1280]{1,0:T(8,128)S(1)} %add_add_fusion.1.refs_0_, f32[64,1280]{1,0:T(8,128)S(1)} %collective-permute-done.27.refs_1_, f32[2,32,1280]{2,1,0:T(8,128)S(1)} %collective-permute-done.28.refs_2_, ...), custom_call_target="tpu_custom_call", output_to_operand_aliasing={{}: (6, {})} | custom-call | flops 491520 | bytes 1310720 | tf_op jit(solution)/shard_map/finish_last/pallas_call | solution.py:236
  (70 shorter events, 25.3 us)
Async XLA Ops:
  5.1 7.9 %collective-permute-start.4 = (f32[72,1280]{1,0:T(8,128)S(1)}, f32[72,1280]{1,0:T(8,128)S(1)}, u32[]{:S(2)}, u32[]{:S(2)}) collective-permute-start(f32[72,1280]{1,0:T(8,128)S(1)} %get-tuple-element.55), channel_id=1, source_target_pairs={{0,2},{1,9},{2,4},{3,11},{4,6},{5,13},{6,0},{7,15},{8,10},{9,17},{... | collective-permute-start | bytes 1105928 | tf_op jit(solution)/shard_map/ppermute | solution.py:45
  6.4 11.6 %collective-permute-start.5 = (f32[72,1280]{1,0:T(8,128)S(1)}, f32[72,1280]{1,0:T(8,128)S(1)}, u32[]{:S(2)}, u32[]{:S(2)}) collective-permute-start(f32[72,1280]{1,0:T(8,128)S(1)} %get-tuple-element.56), channel_id=1, source_target_pairs={{0,4},{1,17},{2,6},{3,19},{4,0},{5,21},{6,2},{7,23},{8,12},{9,25},... | collective-permute-start | bytes 1105928 | tf_op jit(solution)/shard_map/ppermute | solution.py:45
  8.8 9.2 %collective-permute-start.6 = (f32[72,1280]{1,0:T(8,128)S(1)}, f32[72,1280]{1,0:T(8,128)S(1)}, u32[]{:S(2)}, u32[]{:S(2)}) collective-permute-start(f32[72,1280]{1,0:T(8,128)S(1)} %get-tuple-element.57), channel_id=1, source_target_pairs={{0,6},{1,25},{2,0},{3,27},{4,2},{5,29},{6,4},{7,31},{8,14},{9,1},{... | collective-permute-start | bytes 1105928 | tf_op jit(solution)/shard_map/ppermute | solution.py:45
  10.6 11.3 %collective-permute-start.1 = (f32[72,1280]{1,0:T(8,128)S(1)}, f32[72,1280]{1,0:T(8,128)S(1)}, u32[]{:S(2)}, u32[]{:S(2)}) collective-permute-start(f32[72,1280]{1,0:T(8,128)S(1)} %get-tuple-element.51), channel_id=1, source_target_pairs={{0,2},{1,9},{2,4},{3,11},{4,6},{5,13},{6,0},{7,15},{8,10},{9,17},{... | collective-permute-start | bytes 1105928 | tf_op jit(solution)/shard_map/ppermute | solution.py:45
  11.0 14.9 %collective-permute-start.2 = (f32[72,1280]{1,0:T(8,128)S(1)}, f32[72,1280]{1,0:T(8,128)S(1)}, u32[]{:S(2)}, u32[]{:S(2)}) collective-permute-start(f32[72,1280]{1,0:T(8,128)S(1)} %get-tuple-element.52), channel_id=1, source_target_pairs={{0,4},{1,17},{2,6},{3,19},{4,0},{5,21},{6,2},{7,23},{8,12},{9,25},... | collective-permute-start | bytes 1105928 | tf_op jit(solution)/shard_map/ppermute | solution.py:45
  12.9 13.0 %collective-permute-start.3 = (f32[72,1280]{1,0:T(8,128)S(1)}, f32[72,1280]{1,0:T(8,128)S(1)}, u32[]{:S(2)}, u32[]{:S(2)}) collective-permute-start(f32[72,1280]{1,0:T(8,128)S(1)} %get-tuple-element.53), channel_id=1, source_target_pairs={{0,6},{1,25},{2,0},{3,27},{4,2},{5,29},{6,4},{7,31},{8,14},{9,1},{... | collective-permute-start | bytes 1105928 | tf_op jit(solution)/shard_map/ppermute | solution.py:45
  26.6 22.3 %collective-permute-start.9 = (f32[320,1280]{1,0:T(8,128)S(1)}, f32[320,1280]{1,0:T(8,128)S(1)}, u32[]{:S(2)}, u32[]{:S(2)}) collective-permute-start(f32[320,1280]{1,0:T(8,128)S(1)} %get-tuple-element.61.refs_0_), channel_id=1, source_target_pairs={{0,8},{1,3},{2,10},{3,5},{4,12},{5,7},{6,14},{7,1},{8,16},{9,11},{... | collective-permute-start | bytes 4915208 | tf_op jit(solution)/shard_map/ppermute | solution.py:45
  28.0 21.1 %collective-permute-start.10 = (f32[320,1280]{1,0:T(8,128)S(1)}, f32[320,1280]{1,0:T(8,128)S(1)}, u32[]{:S(2)}, u32[]{:S(2)}) collective-permute-start(f32[320,1280]{1,0:T(8,128)S(1)} %get-tuple-element.61.refs_0_), channel_id=1, source_target_pairs={{0,24},{1,7},{2,26},{3,1},{4,28},{5,3},{6,30},{7,5},{8,0},{9,15},{... | collective-permute-start | bytes 4915208 | tf_op jit(solution)/shard_map/ppermute | solution.py:45
  30.2 29.7 %collective-permute-start.7 = (f32[256,1280]{1,0:T(8,128)S(1)}, f32[256,1280]{1,0:T(8,128)S(1)}, u32[]{:S(2)}, u32[]{:S(2)}) collective-permute-start(f32[256,1280]{1,0:T(8,128)S(1)} %get-tuple-element.73.refs_0_), channel_id=1, source_target_pairs={{0,32},{1,33},{2,34},{3,35},{4,36},{5,37},{6,38},{7,39},{8,40},{9,... | collective-permute-start | bytes 3932168 | tf_op jit(solution)/shard_map/ppermute | solution.py:45
  31.5 28.4 %collective-permute-start.8 = (f32[256,1280]{1,0:T(8,128)S(1)}, f32[256,1280]{1,0:T(8,128)S(1)}, u32[]{:S(2)}, u32[]{:S(2)}) collective-permute-start(f32[256,1280]{1,0:T(8,128)S(1)} %get-tuple-element.73.refs_0_), channel_id=1, source_target_pairs={{0,96},{1,97},{2,98},{3,99},{4,100},{5,101},{6,102},{7,103},{8,104... | collective-permute-start | bytes 3932168 | tf_op jit(solution)/shard_map/ppermute | solution.py:45
  48.9 13.8 %collective-permute-start.12 = (f32[160,1280]{1,0:T(8,128)S(1)}, f32[160,1280]{1,0:T(8,128)S(1)}, u32[]{:S(2)}, u32[]{:S(2)}) collective-permute-start(f32[160,1280]{1,0:T(8,128)S(1)} %slice.40), channel_id=1, source_target_pairs={{0,8},{1,3},{2,10},{3,5},{4,12},{5,7},{6,14},{7,1},{8,16},{9,11},{... | collective-permute-start | bytes 2457608 | tf_op jit(solution)/shard_map/ppermute | solution.py:45
  49.1 13.7 %collective-permute-start.13 = (f32[160,1280]{1,0:T(8,128)S(1)}, f32[160,1280]{1,0:T(8,128)S(1)}, u32[]{:S(2)}, u32[]{:S(2)}) collective-permute-start(f32[160,1280]{1,0:T(8,128)S(1)} %slice.41), channel_id=1, source_target_pairs={{0,24},{1,7},{2,26},{3,1},{4,28},{5,3},{6,30},{7,5},{8,0},{9,15},{... | collective-permute-start | bytes 2457608 | tf_op jit(solution)/shard_map/ppermute | solution.py:45
  59.9 14.7 %collective-permute-start.11 = (f32[128,1280]{1,0:T(8,128)S(1)}, f32[128,1280]{1,0:T(8,128)S(1)}, u32[]{:S(2)}, u32[]{:S(2)}) collective-permute-start(f32[128,1280]{1,0:T(8,128)S(1)} %slice.30), channel_id=1, source_target_pairs={{0,32},{1,33},{2,34},{3,35},{4,36},{5,37},{6,38},{7,39},{8,40},{9,... | collective-permute-start | bytes 1966088 | tf_op jit(solution)/shard_map/ppermute | solution.py:45
  61.0 13.6 %collective-permute-start.14 = (f32[128,1280]{1,0:T(8,128)S(1)}, f32[128,1280]{1,0:T(8,128)S(1)}, u32[]{:S(2)}, u32[]{:S(2)}) collective-permute-start(f32[128,1280]{1,0:T(8,128)S(1)} %slice.33), channel_id=1, source_target_pairs={{0,96},{1,97},{2,98},{3,99},{4,100},{5,101},{6,102},{7,103},{8,104... | collective-permute-start | bytes 1966088 | tf_op jit(solution)/shard_map/ppermute | solution.py:45
  68.9 17.8 %collective-permute-start.15 = (f32[128,1280]{1,0:T(8,128)S(1)}, f32[128,1280]{1,0:T(8,128)S(1)}, u32[]{:S(2)}, u32[]{:S(2)}) collective-permute-start(f32[128,1280]{1,0:T(8,128)S(1)} %get-tuple-element.75), channel_id=1, source_target_pairs={{0,6},{1,25},{2,0},{3,27},{4,2},{5,29},{6,4},{7,31},{8,14},{9,1},{... | collective-permute-start | bytes 1966088 | tf_op jit(solution)/shard_map/ppermute | solution.py:45
  72.2 18.0 %collective-permute-start.16 = (f32[128,1280]{1,0:T(8,128)S(1)}, f32[128,1280]{1,0:T(8,128)S(1)}, u32[]{:S(2)}, u32[]{:S(2)}) collective-permute-start(f32[128,1280]{1,0:T(8,128)S(1)} %get-tuple-element.76), channel_id=1, source_target_pairs={{0,2},{1,9},{2,4},{3,11},{4,6},{5,13},{6,0},{7,15},{8,10},{9,17},{... | collective-permute-start | bytes 1966088 | tf_op jit(solution)/shard_map/ppermute | solution.py:45
  72.2 18.0 %collective-permute-start.17 = (f32[128,1280]{1,0:T(8,128)S(1)}, f32[128,1280]{1,0:T(8,128)S(1)}, u32[]{:S(2)}, u32[]{:S(2)}) collective-permute-start(f32[128,1280]{1,0:T(8,128)S(1)} %get-tuple-element.77), channel_id=1, source_target_pairs={{0,4},{1,17},{2,6},{3,19},{4,0},{5,21},{6,2},{7,23},{8,12},{9,25},... | collective-permute-start | bytes 1966088 | tf_op jit(solution)/shard_map/ppermute | solution.py:45
  77.4 15.7 %collective-permute-start.18 = (f32[64,1280]{1,0:T(8,128)S(1)}, f32[64,1280]{1,0:T(8,128)S(1)}, u32[]{:S(2)}, u32[]{:S(2)}) collective-permute-start(f32[64,1280]{1,0:T(8,128)S(1)} %get-tuple-element.79), channel_id=1, source_target_pairs={{0,6},{1,25},{2,0},{3,27},{4,2},{5,29},{6,4},{7,31},{8,14},{9,1},{... | collective-permute-start | bytes 983048 | tf_op jit(solution)/shard_map/ppermute | solution.py:45
  81.7 15.5 %collective-permute-start.19 = (f32[64,1280]{1,0:T(8,128)S(1)}, f32[64,1280]{1,0:T(8,128)S(1)}, u32[]{:S(2)}, u32[]{:S(2)}) collective-permute-start(f32[64,1280]{1,0:T(8,128)S(1)} %get-tuple-element.80), channel_id=1, source_target_pairs={{0,2},{1,9},{2,4},{3,11},{4,6},{5,13},{6,0},{7,15},{8,10},{9,17},{... | collective-permute-start | bytes 983048 | tf_op jit(solution)/shard_map/ppermute | solution.py:45
  86.8 10.4 %collective-permute-start.20 = (f32[64,1280]{1,0:T(8,128)S(1)}, f32[64,1280]{1,0:T(8,128)S(1)}, u32[]{:S(2)}, u32[]{:S(2)}) collective-permute-start(f32[64,1280]{1,0:T(8,128)S(1)} %get-tuple-element.81), channel_id=1, source_target_pairs={{0,4},{1,17},{2,6},{3,19},{4,0},{5,21},{6,2},{7,23},{8,12},{9,25},... | collective-permute-start | bytes 983048 | tf_op jit(solution)/shard_map/ppermute | solution.py:45
  90.5 8.4 %collective-permute-start.21 = (f32[64,1280]{1,0:T(8,128)S(1)}, f32[64,1280]{1,0:T(8,128)S(1)}, u32[]{:S(2)}, u32[]{:S(2)}) collective-permute-start(f32[64,1280]{1,0:T(8,128)S(1)} %get-tuple-element.91), channel_id=1, source_target_pairs={{0,96},{1,97},{2,98},{3,99},{4,100},{5,101},{6,102},{7,103},{8,104... | collective-permute-start | bytes 983048 | tf_op jit(solution)/shard_map/ppermute | solution.py:45
  93.2 12.9 %collective-permute-start.24 = (f32[64,1280]{1,0:T(8,128)S(1)}, f32[64,1280]{1,0:T(8,128)S(1)}, u32[]{:S(2)}, u32[]{:S(2)}) collective-permute-start(f32[64,1280]{1,0:T(8,128)S(1)} %get-tuple-element.84), channel_id=1, source_target_pairs={{0,6},{1,25},{2,0},{3,27},{4,2},{5,29},{6,4},{7,31},{8,14},{9,1},{... | collective-permute-start | bytes 983048 | tf_op jit(solution)/shard_map/ppermute | solution.py:45
  97.2 10.9 %collective-permute-start.25 = (f32[64,1280]{1,0:T(8,128)S(1)}, f32[64,1280]{1,0:T(8,128)S(1)}, u32[]{:S(2)}, u32[]{:S(2)}) collective-permute-start(f32[64,1280]{1,0:T(8,128)S(1)} %get-tuple-element.86), channel_id=1, source_target_pairs={{0,2},{1,9},{2,4},{3,11},{4,6},{5,13},{6,0},{7,15},{8,10},{9,17},{... | collective-permute-start | bytes 983048 | tf_op jit(solution)/shard_map/ppermute | solution.py:45
  97.2 10.9 %collective-permute-start.26 = (f32[64,1280]{1,0:T(8,128)S(1)}, f32[64,1280]{1,0:T(8,128)S(1)}, u32[]{:S(2)}, u32[]{:S(2)}) collective-permute-start(f32[64,1280]{1,0:T(8,128)S(1)} %get-tuple-element.88), channel_id=1, source_target_pairs={{0,4},{1,17},{2,6},{3,19},{4,0},{5,21},{6,2},{7,23},{8,12},{9,25},... | collective-permute-start | bytes 983048 | tf_op jit(solution)/shard_map/ppermute | solution.py:45
  (9 other events, 71.5 us)
